TPU v7x, 256 devices: a whole 4x4x8 slice. The times are simulated.
256 devices in a mesh: ment: 64 (over z, x, core), ent: 4 (over y).
Axes of the slice: x: 4, y: 4, z: 8, core: 2. Of those that a mesh axis runs over, the one named last changes fastest.
Arguments:
- hidden_in: bfloat16 [4096, 32, 1024], P('ment'), may hold values from -16 to 16
- w_qkv: bfloat16 [1024, 3, 1024], P(None, None, 'ent'), may hold values from -0.1875 to 0.1875
- w_out: bfloat16 [1024, 1024], P('ent'), may hold values from -0.1875 to 0.1875
- ln_gain: float32 [1024], replicated, may hold values from 0.5 to 1.5
- ln_bias: float32 [1024], replicated, may hold values from -3 to 3
- table: bfloat16 [32, 256, 1024], P('ent'), may hold values from -0.5 to 0.5
- key_len: int32 [4096], P('ment'), may hold values from 4 to 32
- gold_block: int32 [4096], P('ment'), may hold values from 0 to 31
- gold_row: int32 [4096], P('ment'), may hold values from 0 to 255
- neg_blocks: int32 [64, 4], P('ment'), may hold values from 0 to 31, as said below
Outputs:
- grad_hidden: bfloat16 [4096, 32, 1024], P(('ment', 'ent'))
- grad_qkv: float32 [1024, 3, 1024], P('ment', None, 'ent')
- grad_wo: float32 [1024, 1024], P('ent', 'ment')
- grad_ln: float32 [2, 1024], P(None, 'ment')
- grad_table: float32 [32, 256, 1024], P('ent', 'ment')
Inputs may be any that keep to these rules, and one draw needn't show every extreme that they name: `neg_blocks`: each row lists 4 different blocks.
All inputs are finite; a program needn't handle non-finite values.
Results may differ from a plain program's by a relative error of at most 0.028.
Values may be sent and summed in bfloat16 or wider, within the bound.
A program may use at most 128 MiB of HBM per device.

v0:
```python
import jax
import jax.numpy as jnp
from jax import lax
from jax.sharding import PartitionSpec as P

HD = 64


ln_eps = 1e-06


def contract(left, right, left_dim, right_dim):
    return lax.dot_general(
        left, right, (((left_dim,), (right_dim,)), ((), ())), preferred_element_type=jnp.float32
    )


def on_device(
    hidden_in, w_qkv, w_out, ln_gain, ln_bias, table, key_len, gold_block, gold_row, neg_blocks
):
    ment_rows, seq_len, width = hidden_in.shape
    local_cols = w_qkv.shape[2]
    local_heads = local_cols // HD
    own_blocks, block_rows = (table.shape[0], table.shape[1])
    score_scale = HD ** (-0.5)
    owner = lax.axis_index("ent")
    first_block = owner * own_blocks
    cls_rows = hidden_in[:, 0, :]
    w_query = w_qkv[:, 0, :]
    w_keyval = w_qkv[:, 1:, :].reshape(width, 2 * local_cols)
    query = jnp.dot(cls_rows, w_query, preferred_element_type=jnp.float32).astype(jnp.bfloat16)
    keyval = jnp.dot(
        hidden_in.reshape(ment_rows * seq_len, width), w_keyval, preferred_element_type=jnp.float32
    )
    keyval = keyval.astype(jnp.bfloat16).reshape(ment_rows, seq_len, 2, local_heads, HD)
    key_heads = keyval[:, :, 0]
    value_heads = keyval[:, :, 1]
    query_heads = query.reshape(ment_rows, local_heads, HD)
    attention_scores = (
        jnp.einsum("ybn,yqbn->ybq", query_heads, key_heads, preferred_element_type=jnp.float32)
        * score_scale
    )
    valid = (jnp.arange(seq_len, dtype=jnp.int32)[None, :] < key_len[:, None]).astype(jnp.float32)
    expo = jnp.exp(attention_scores) * valid[:, None, :]
    probs = expo / jnp.sum(expo, axis=-1, keepdims=True)
    probability_half = probs.astype(jnp.bfloat16)
    context_rows = jnp.einsum(
        "qjp,qpjb->qjb", probability_half, value_heads, preferred_element_type=jnp.float32
    )
    context_rows = context_rows.reshape(ment_rows, local_cols).astype(jnp.bfloat16)
    attn_part = jnp.dot(context_rows, w_out, preferred_element_type=jnp.float32)
    local_block = gold_block - first_block
    owned = (local_block >= 0) & (local_block < own_blocks)
    safe_block = jnp.clip(local_block, 0, own_blocks - 1)
    flat_table = table.reshape(own_blocks * block_rows, width)
    picked = flat_table[safe_block * block_rows + gold_row]
    picked = jnp.where(owned[:, None], picked.astype(jnp.float32), 0.0)
    attn_out, gold_sum = (
        lax.psum(attn_part.astype(jnp.bfloat16), "ent").astype(jnp.float32),
        lax.psum(picked.astype(jnp.bfloat16), "ent").astype(jnp.float32),
    )
    golds = gold_sum.astype(jnp.bfloat16)
    resid = cls_rows.astype(jnp.float32) + attn_out
    centre = resid - jnp.mean(resid, axis=-1, keepdims=True)
    rstd = lax.rsqrt(jnp.mean(centre * centre, axis=-1, keepdims=True) + ln_eps)
    normed = centre * rstd
    embed = (normed * ln_gain + ln_bias).astype(jnp.bfloat16)
    inbatch = contract(embed, golds, 1, 1)
    negscore = contract(embed, flat_table, 1, 1)
    block_ids = first_block + jnp.arange(own_blocks, dtype=jnp.int32)
    listed = jnp.any(neg_blocks[0][:, None] == block_ids[None, :], axis=0).astype(jnp.float32)
    row_mask = jnp.repeat(listed, block_rows)
    neg_part = jnp.sum(jnp.exp(negscore) * row_mask[None, :], axis=1)
    neg_total = lax.psum(neg_part, "ent")
    lse = jnp.log(jnp.sum(jnp.exp(inbatch), axis=1) + neg_total)
    eye = jnp.eye(ment_rows, dtype=jnp.float32)
    w_inb = (jnp.exp(inbatch - lse[:, None]) - eye).astype(jnp.bfloat16)
    w_neg = (jnp.exp(negscore - lse[:, None]) * row_mask[None, :]).astype(jnp.bfloat16)
    embed_part = jnp.dot(w_neg, flat_table, preferred_element_type=jnp.float32)
    d_embed = jnp.dot(w_inb, golds, preferred_element_type=jnp.float32) + lax.psum(
        embed_part.astype(jnp.bfloat16), "ent"
    ).astype(jnp.float32)
    ln_terms = jnp.stack([jnp.sum(d_embed * normed, axis=0), jnp.sum(d_embed, axis=0)])
    upper = d_embed * ln_gain
    d_resid = rstd * (
        upper
        - jnp.mean(upper, axis=-1, keepdims=True)
        - normed * jnp.mean(upper * normed, axis=-1, keepdims=True)
    )
    d_resid_bf = d_resid.astype(jnp.bfloat16)
    wo_term = contract(context_rows, d_resid_bf, 0, 0)
    grad_wo, grad_ln = (
        lax.psum_scatter(wo_term, "ment", scatter_dimension=1, tiled=True),
        lax.psum_scatter(ln_terms, "ment", scatter_dimension=1, tiled=True),
    )
    d_context = contract(d_resid_bf, w_out, 1, 1).astype(jnp.bfloat16)
    context_head_gradient = d_context.reshape(ment_rows, local_heads, HD)
    probability_gradient = jnp.einsum(
        "ybn,yqbn->ybq", context_head_gradient, value_heads, preferred_element_type=jnp.float32
    )
    score_gradient = probs * (
        probability_gradient - jnp.sum(probs * probability_gradient, axis=-1, keepdims=True)
    )
    query_gradient = (
        jnp.einsum("qjp,qpjb->qjb", score_gradient, key_heads, preferred_element_type=jnp.float32)
        * score_scale
    )
    query_gradient = query_gradient.reshape(ment_rows, local_cols).astype(jnp.bfloat16)
    key_gradient = (
        jnp.einsum("ryk,ryo->rkyo", score_gradient, query_heads, preferred_element_type=jnp.float32)
        * score_scale
    )
    value_gradient = jnp.einsum(
        "ryk,ryo->rkyo", probability_half, context_head_gradient, preferred_element_type=jnp.float32
    )
    d_keyval = (
        jnp.stack([key_gradient, value_gradient], axis=2)
        .reshape(ment_rows, seq_len, 2 * local_cols)
        .astype(jnp.bfloat16)
    )
    flat_grad = d_keyval.reshape(ment_rows * seq_len, 2 * local_cols)
    count = lax.axis_size("ment") * (width // lax.axis_size("ment"))
    kv_term = contract(hidden_in.reshape(ment_rows * seq_len, count), flat_grad, 0, 0)
    query_term = contract(hidden_in[:, 0, :], query_gradient, 0, 0)
    grad_qkv = lax.psum_scatter(
        jnp.concatenate([query_term[:, None, :], kv_term.reshape(count, 2, local_cols)], axis=1),
        "ment",
        scatter_dimension=0,
        tiled=True,
    )
    share = ment_rows // lax.axis_size("ent")
    grad_part = d_keyval.reshape(share * lax.axis_size("ent") * seq_len, 2 * local_cols)
    token_term = contract(grad_part, w_keyval, 1, 1).reshape(
        share * lax.axis_size("ent"), seq_len, width
    )
    summed = lax.psum_scatter(
        token_term.at[:, 0, :].add(contract(query_gradient, w_query, 1, 1)).astype(jnp.bfloat16),
        "ent",
        scatter_dimension=0,
        tiled=True,
    ).astype(jnp.float32)
    resid_mine = lax.dynamic_slice_in_dim(d_resid, owner * share, share, 0)
    grad_hidden = summed.at[:, 0, :].add(resid_mine).astype(jnp.bfloat16)
    gold_terms = contract(w_inb, embed, 0, 0)
    weight_blocks = w_neg.reshape(ment_rows, own_blocks, block_rows)
    count = lax.axis_size("ment") * (block_rows // lax.axis_size("ment"))
    neg_term = jnp.einsum("mbr,md->rbd", weight_blocks, embed, preferred_element_type=jnp.float32)
    inside = owned & (gold_row >= 0) & (gold_row < count)
    row_slot = jnp.where(inside, gold_row, count)
    reduced = lax.psum_scatter(
        neg_term.at[row_slot, safe_block].add(gold_terms, mode="drop"),
        "ment",
        scatter_dimension=0,
        tiled=True,
    )
    grad_table = jnp.transpose(reduced, (1, 0, 2))
    return (grad_hidden, grad_qkv, grad_wo, grad_ln, grad_table)


def solution(mesh):
    placed = (
        P("ment", None, None),
        P(None, None, "ent"),
        P("ent", None),
        P(),
        P(),
        P("ent", None, None),
        P("ment"),
        P("ment"),
        P("ment"),
        P("ment", None),
    )
    return jax.shard_map(
        on_device,
        mesh=mesh,
        in_specs=placed,
        out_specs=(
            P(("ment", "ent"), None, None),
            P("ment", None, "ent"),
            P("ent", "ment"),
            P(None, "ment"),
            P("ent", "ment", None),
        ),
        check_vma=False,
    )
```

profile of v0, /device:TPU:1, one launch (start us, length us, event | category | flops | bytes accessed | tf_op | source)
XLA Modules:
  0.0 709.1 jit_solution(6832385997085273812)
XLA Ops:
  7.2 0.7 compare_and_fusion
  7.9 0.7 compare_select_fusion.2
  8.6 0.7 fusion.34
  9.4 1.4 slice.60
  10.8 2.3 fusion.60
  13.2 1.2 convolution_convert_fusion.4
  14.6 4.5 convolution_convert_fusion
  19.1 3.7 reshape.170
  22.8 4.8 slice_bitcast_fusion
  27.6 1.3 copy-done.7
  29.0 1.2 fusion.6
  30.6 6.0 fusion.13
  36.6 1.0 copy-done.3
  37.8 0.8 copy.43
  38.6 2.3 fusion.2
  41.1 3.5 gather_fusion
  44.6 0.7 select_convert_fusion
  45.4 0.9 convolution_convert_fusion.2
  46.5 48.5 %all-reduce.7.cloned.1.call-done = (bf16[64,1024]{1,0:T(8,128)(2,1)}, bf16[64,1024]{1,0:T(8,128)(2,1)}) async-done(((bf16[64,1024]{1,0:T(8,128)(2,1)}, bf16[64,1024]{1,0:T(8,128)(2,1)}), (bf16[64,1024]{1,0:T(8,128)(2,1)}, bf16[64,1024]{1,0:T(8,128)(2,1)})) %all-reduce.7.cloned.1.call-update) | async-done | bytes 262160 | tf_op jit(solution)/shard_map/psum | solution.py:60
  95.0 1.1 fusion.28
  96.0 1.1 multiply_reduce_fusion.3
  97.2 1.0 add_convert_fusion
  98.2 1.1 exponential_reduce_fusion
  99.3 3.7 multiply_reduce_fusion
  103.0 7.6 %psum.30 = f32[64]{0:T(128)S(1)} all-reduce(f32[64]{0:T(128)S(1)} %get-tuple-element.58), channel_id=1, replica_groups=mesh['ment'=64,'ent'=4] {'ent'}, use_global_device_ids=true, to_apply=%region_8.9 | all-reduce | flops 64 | bytes 512 | tf_op jit(solution)/shard_map/psum | solution.py:74
  110.8 3.7 convolution_convert_fusion.1
  114.9 3.3 copy.34
  118.2 2.5 reshape.198
  120.8 41.2 %all-reduce.5.cloned.1.call-done = bf16[64,1024]{1,0:T(8,128)(2,1)} async-done(((bf16[64,1024]{1,0:T(8,128)(2,1)}), bf16[64,1024]{1,0:T(8,128)(2,1)}) %all-reduce.5.cloned.1.call-update) | async-done | bytes 131088 | tf_op jit(solution)/shard_map/psum | solution.py:80
  162.0 1.3 multiply_reduce_fusion.1
  164.0 2.8 fusion
  166.8 1.4 copy.47
  168.2 2.4 fusion.9
  170.6 0.8 copy.48
  171.4 2.3 fusion.4
  173.8 1.3 fusion.15
  175.2 2.5 multiply_bitcast_fusion.1
  177.7 2.5 multiply_bitcast_fusion
  180.2 5.4 maximum_convert_fusion
  185.6 6.8 convert_element_type.118
  192.4 4.5 fusion.61
  196.9 3.2 copy-done.2
  200.5 6.1 scatter-add.14
  206.6 6.0 convert_element_type.121
  212.6 0.6 copy-done.17
  213.2 4.5 convolution_bitcast_fusion
  217.7 9.0 %copy.38 = f32[256,8,1024]{2,1,0:T(8,128)} copy(f32[256,8,1024]{0,2,1:T(8,128)} %convolution_bitcast_fusion) | data formatting | bytes 16777216 | tf_op jit(solution)/shard_map/mbr,md->rbd/transpose | solution.py:147
  226.9 10.4 %scatter_fusion = f32[256,8,1024]{2,1,0:T(8,128)} fusion(f32[256,8,1024]{2,1,0:T(8,128)} %copy.38, s32[64]{0:T(128)S(1)} %fusion.38, f32[64,1024]{1,0:T(8,128)S(1)} %fusion.39), kind=kCustom, calls=%fused_computation.1 | custom fusion | flops 65536 | bytes 786944 | tf_op jit(solution)/shard_map/scatter-add | solution.py:151
  237.3 0.7 copy-done.9
  238.3 1.3 copy.35
  239.6 1.3 fusion.31
  241.6 6.0 fusion.62
  247.6 1.9 copy.36
  249.5 3.3 pad_maximum_fusion
  252.8 0.6 copy-done.20
  253.5 0.6 dynamic-slice.16
  254.7 129.4 %all-reduce = f32[2,1024]{1,0:T(2,128)S(1)} all-reduce(f32[2,1024]{1,0:T(2,128)S(1)} %pad_maximum_fusion.1), channel_id=5, replica_groups=mesh['ment'=64,'ent'=4] {'ment'}, use_global_device_ids=true, to_apply=%region_18.19.clone | all-reduce | flops 2048 | bytes 16384
  384.1 0.6 constant_dynamic-slice_fusion
  384.8 1.5 convert_element_type.122
  386.9 1.1 convert_element_type.123
  388.0 27.7 %reduce-scatter.12.cloned.1.call-done = f32[4,8,1024]{2,1,0:T(8,128)} async-done(((f32[256,8,1024]{2,1,0:T(8,128)}), f32[4,8,1024]{2,1,0:T(8,128)}) %reduce-scatter.12.cloned.1.call-update) | async-done | bytes 131088 | tf_op jit(solution)/shard_map/reduce_scatter | solution.py:150
  415.7 1.6 copy.39
  417.3 140.1 %reduce-scatter.10.cloned.1.call-done = f32[256,16]{0,1:T(8,128)} async-done(((f32[256,1024]{0,1:T(8,128)}), f32[256,16]{0,1:T(8,128)}) %reduce-scatter.10.cloned.1.call-update) | async-done | bytes 16400 | tf_op jit(solution)/shard_map/reduce_scatter | solution.py:93
  557.4 144.9 %reduce-scatter.8.cloned.1.call-done = f32[16,3,256]{2,0,1:T(8,128)} async-done(((f32[1024,3,256]{2,0,1:T(8,128)}), f32[16,3,256]{2,0,1:T(8,128)}) %reduce-scatter.8.cloned.1.call-update) | async-done | bytes 49168 | tf_op jit(solution)/shard_map/reduce_scatter | solution.py:125
  (84 shorter events, 4.9 us)
Async XLA Ops:
  7.2 38.2 %copy-start = (bf16[256,1024]{1,0:T(8,128)(2,1)S(1)}, bf16[256,1024]{1,0:T(8,128)(2,1)}, u32[]{:S(2)}) copy-start(bf16[256,1024]{1,0:T(8,128)(2,1)} %param.16) | copy-start | bytes 1572868
  7.2 87.8 %all-reduce.7.cloned.1.call-start = ((), (), s32[]{:S(2)}) async-start(), calls=%async_computation.9 | async-start | bytes 524288 | tf_op jit(solution)/shard_map/psum | solution.py:60
  27.6 1.4 copy-start.7
  36.6 1.0 copy-start.3
  38.6 7.7 %copy-start.19 = (s32[1,4]{1,0:T(1,128)S(1)}, s32[1,4]{1,0:T(1,128)}, u32[]{:S(2)}) copy-start(s32[1,4]{1,0:T(1,128)} %param.23) | copy-start | bytes 52
  40.9 56.3 %copy-start.15 = (f32[1024]{0:T(1024)S(1)}, f32[1024]{0:T(1024)}, u32[]{:S(2)}) copy-start(f32[1024]{0:T(1024)} %param.17) | copy-start | bytes 12292
  40.9 56.3 %copy-start.16 = (f32[1024]{0:T(1024)S(1)}, f32[1024]{0:T(1024)}, u32[]{:S(2)}) copy-start(f32[1024]{0:T(1024)} %param.18) | copy-start | bytes 12292
  41.1 62.0 %copy-start.10 = (bf16[64,256]{1,0:T(8,128)(2,1)}, bf16[64,256]{1,0:T(8,128)(2,1)S(1)}, u32[]{:S(2)}) copy-start(bf16[64,256]{1,0:T(8,128)(2,1)S(1)} %convert_element_type.103) | copy-start | bytes 98308
  46.2 115.7 %all-reduce.5.cloned.1.call-start = ((), (), s32[]{:S(2)}) async-start(), calls=%async_computation.4 | async-start | bytes 262144 | tf_op jit(solution)/shard_map/psum | solution.py:80
  99.3 62.7 %copy-start.13 = (f32[64,64]{0,1:T(8,128)}, f32[64,64]{0,1:T(8,128)S(1)}, u32[]{:S(2)}) copy-start(f32[64,64]{0,1:T(8,128)S(1)} %get-tuple-element.57) | copy-start | bytes 49156
  114.5 270.3 %reduce-scatter.6.cloned.1.call-start = ((), (), s32[]{:S(2)}) async-start(), calls=%async_computation.5 | async-start | bytes 5242880 | tf_op jit(solution)/shard_map/reduce_scatter | solution.py:136
  114.9 47.1 %copy-start.6 = (bf16[64,1024]{1,0:T(8,128)(2,1)S(1)}, bf16[64,1024]{1,0:T(8,128)(2,1)}, u32[]{:S(2)}) copy-start(bf16[64,1024]{1,0:T(8,128)(2,1)} %get-tuple-element.49) | copy-start | bytes 393220
  114.9 47.1 %copy-start.12 = (bf16[64,1024]{1,0:T(8,128)(2,1)S(1)}, bf16[64,1024]{1,0:T(8,128)(2,1)}, u32[]{:S(2)}) copy-start(bf16[64,1024]{1,0:T(8,128)(2,1)} %get-tuple-element.48) | copy-start | bytes 393220
  173.8 6.3 copy-start.8
  192.4 4.5 copy-start.4
  196.9 3.2 copy-start.2
  212.5 0.7 copy-start.17
  212.5 0.7 copy-start.18
  212.6 203.1 %reduce-scatter.12.cloned.1.call-start = ((), (), s32[]{:S(2)}) async-start(), calls=%async_computation.8 | async-start | bytes 8519680 | tf_op jit(solution)/shard_map/reduce_scatter | solution.py:150
  217.7 9.0 %copy-start.14 = (f32[64,64]{0,1:T(8,128)S(1)}, f32[64,64]{0,1:T(8,128)}, u32[]{:S(2)}) copy-start(f32[64,64]{0,1:T(8,128)} %copy-done.13) | copy-start | bytes 49156
  237.2 0.8 copy-start.9
  237.3 2.4 copy-start.11
  237.3 320.1 %reduce-scatter.10.cloned.1.call-start = ((), (), s32[]{:S(2)}) async-start(), calls=%async_computation.7 | async-start | bytes 1064960 | tf_op jit(solution)/shard_map/reduce_scatter | solution.py:93
  239.6 2.0 copy-start.5
  241.0 461.3 %reduce-scatter.8.cloned.1.call-start = ((), (), s32[]{:S(2)}) async-start(), calls=%async_computation.6 | async-start | bytes 3194880 | tf_op jit(solution)/shard_map/reduce_scatter | solution.py:125
  252.8 0.7 copy-start.20
  384.8 317.5 %copy-start.1 = (bf16[256,1024]{1,0:T(8,128)(2,1)S(1)}, bf16[256,1024]{1,0:T(8,128)(2,1)}, u32[]{:S(2)}) copy-start(bf16[256,1024]{1,0:T(8,128)(2,1)} %param.16) | copy-start | bytes 1572868
Sparse Core Ops, SparseCore 0:
  46.4 48.5 all-reduce.6
  114.6 47.2 all-reduce.4
  212.7 51.9 reduce-scatter.5
  269.3 146.3 reduce-scatter.11
  420.1 137.2 reduce-scatter.9
  562.0 140.2 reduce-scatter.7
where the time goes:
time: 716 us; the launch traced here: 709 us
  waiting for transfers between devices  402 us (56%)
  blocking collectives  137 us (19%)
  local copies, waits for them, and re-layouts  62.5 us (9%)
  other arithmetic  48.3 us (7%)
  matrix products  43.3 us (6%)
  between operations  15.2 us (2%)
    reduce_scatter x1, waiting for transfers between devices, on_device(): lax.psum_scatter(jnp.concatenate([query_term[:, None, :], kv_term.reshape...  145 us
    reduce_scatter x1, waiting for transfers between devices, on_device(): lax.psum_scatter(wo_term, 'ment', scatter_dimension=1, tiled=True)  140 us
    unnamed x1, blocking collectives  129 us
    psum x1, waiting for transfers between devices, on_device(): lax.psum(picked.astype(jnp.bfloat16), 'ent').astype(jnp.float32)  48.5 us
    psum x1, waiting for transfers between devices, on_device(): lax.psum(embed_part.astype(jnp.bfloat16), 'ent').astype(jnp.float32)  41.2 us
    reduce_scatter x1, waiting for transfers between devices, on_device(): lax.psum_scatter(neg_term.at[row_slot, safe_block].add(gold_terms, mode='...  27.7 us
    dot_general x9, matrix products, contract(): lax.dot_general(left, right, (((left_dim,), (right_dim,)), ((), ())), pre...  18.7 us
  transfers between devices with their start and end apart: 6, of which 5 were waited for; matrix products, arithmetic and copies ran while one was open for 7% of the time, Pallas kernels for 0%

commit v1 on v0

--- a/solution.py
+++ b/solution.py
@@ -89,10 +89,6 @@
     )
     d_resid_bf = d_resid.astype(jnp.bfloat16)
     wo_term = contract(context_rows, d_resid_bf, 0, 0)
-    grad_wo, grad_ln = (
-        lax.psum_scatter(wo_term, "ment", scatter_dimension=1, tiled=True),
-        lax.psum_scatter(ln_terms, "ment", scatter_dimension=1, tiled=True),
-    )
     d_context = contract(d_resid_bf, w_out, 1, 1).astype(jnp.bfloat16)
     context_head_gradient = d_context.reshape(ment_rows, local_heads, HD)
     probability_gradient = jnp.einsum(
@@ -122,11 +118,8 @@
     count = lax.axis_size("ment") * (width // lax.axis_size("ment"))
     kv_term = contract(hidden_in.reshape(ment_rows * seq_len, count), flat_grad, 0, 0)
     query_term = contract(hidden_in[:, 0, :], query_gradient, 0, 0)
-    grad_qkv = lax.psum_scatter(
-        jnp.concatenate([query_term[:, None, :], kv_term.reshape(count, 2, local_cols)], axis=1),
-        "ment",
-        scatter_dimension=0,
-        tiled=True,
+    qkv_term = jnp.concatenate(
+        [query_term[:, None, :], kv_term.reshape(count, 2, local_cols)], axis=1
     )
     share = ment_rows // lax.axis_size("ent")
     grad_part = d_keyval.reshape(share * lax.axis_size("ent") * seq_len, 2 * local_cols)
@@ -147,13 +140,29 @@
     neg_term = jnp.einsum("mbr,md->rbd", weight_blocks, embed, preferred_element_type=jnp.float32)
     inside = owned & (gold_row >= 0) & (gold_row < count)
     row_slot = jnp.where(inside, gold_row, count)
-    reduced = lax.psum_scatter(
-        neg_term.at[row_slot, safe_block].add(gold_terms, mode="drop"),
-        "ment",
-        scatter_dimension=0,
-        tiled=True,
-    )
-    grad_table = jnp.transpose(reduced, (1, 0, 2))
+    table_term = neg_term.at[row_slot, safe_block].add(gold_terms, mode="drop")
+    parts = lax.axis_size("ment")
+    qkv_rows = width // parts
+    wo_cols = width // parts
+    tab_rows = block_rows // parts
+    pieces = [
+        qkv_term.reshape(parts, qkv_rows * 3 * local_cols),
+        wo_term.reshape(local_cols, parts, wo_cols).transpose(1, 0, 2).reshape(parts, -1),
+        table_term.reshape(parts, tab_rows, own_blocks, width)
+        .transpose(0, 2, 1, 3)
+        .reshape(parts, -1),
+        ln_terms.reshape(2, parts, wo_cols).transpose(1, 0, 2).reshape(parts, -1),
+    ]
+    sizes = [piece.shape[1] for piece in pieces]
+    padded = -sum(sizes) % 1024
+    pieces.append(jnp.zeros((parts, padded), jnp.float32))
+    stacked = jnp.concatenate(pieces, axis=1).reshape(parts * 8, -1)
+    merged = lax.psum_scatter(stacked, "ment", scatter_dimension=0, tiled=True).reshape(-1)
+    offsets = [sum(sizes[:k]) for k in range(len(sizes))]
+    grad_qkv = merged[offsets[0] : offsets[0] + sizes[0]].reshape(qkv_rows, 3, local_cols)
+    grad_wo = merged[offsets[1] : offsets[1] + sizes[1]].reshape(local_cols, wo_cols)
+    grad_table = merged[offsets[2] : offsets[2] + sizes[2]].reshape(own_blocks, tab_rows, width)
+    grad_ln = merged[offsets[3] : offsets[3] + sizes[3]].reshape(2, wo_cols)
     return (grad_hidden, grad_qkv, grad_wo, grad_ln, grad_table)
 
 

time: 716 us -> 540 us (0.75)
  blocking collectives: 137 us -> 7.58 us
  waiting for transfers between devices: 402 us -> 288 us
  local copies, waits for them, and re-layouts: 62.5 us -> 128 us
    reduce_scatter x3 -> x0, waiting for transfers between devices: 313 us -> none  [the longest x1 145 us: on_device(): lax.psum_scatter(jnp.concatenate([query_term[:, None, :], kv_term.reshape...]
    unnamed x6 -> x5, waiting for transfers between devices: 0.1 us -> 192 us
    unnamed x1 -> x0, blocking collectives: 129 us -> none
    reduce_scatter x1, waiting for transfers between devices: 0.01 us -> 47.7 us  [on_device(): lax.psum_scatter(token_term.at[:, 0, :].add(contract(query_gradient, w_qu...]
    reshape x0 -> x9, local copies, waits for them, and re-layouts: none -> 45.5 us  [the longest x1 14.6 us: on_device(): table_term.reshape(parts, tab_rows, own_blocks, width).transpose(0, 2, 1, 3)]
    psum x1, waiting for transfers between devices: 41.2 us -> 0.02 us  [on_device(): lax.psum(embed_part.astype(jnp.bfloat16), 'ent').astype(jnp.float32)]
    unnamed x48 -> x39, local copies, waits for them, and re-layouts: 11.1 us -> 24.2 us
  transfers between devices with their start and end apart: 6 -> 4, of which waited for: 5 -> 3; matrix products, arithmetic and copies ran while one was open for 7% -> 14% of each run, Pallas kernels for 0% -> 0%
where the time goes in v1:
time: 540 us; the launch traced here: 530 us
  waiting for transfers between devices  288 us (53%)
  local copies, waits for them, and re-layouts  128 us (24%)
  other arithmetic  46.5 us (9%)
  matrix products  43.6 us (8%)
  between operations  15.1 us (3%)
  blocking collectives  7.58 us (1%)
    unnamed x5, waiting for transfers between devices  192 us
    psum x1, waiting for transfers between devices, on_device(): lax.psum(picked.astype(jnp.bfloat16), 'ent').astype(jnp.float32)  48.3 us
    reduce_scatter x1, waiting for transfers between devices, on_device(): lax.psum_scatter(token_term.at[:, 0, :].add(contract(query_gradient, w_qu...  47.7 us
    unnamed x39, local copies, waits for them, and re-layouts  24.2 us
    dot_general x9, matrix products, contract(): lax.dot_general(left, right, (((left_dim,), (right_dim,)), ((), ())), pre...  19 us
    reshape x1, local copies, waits for them, and re-layouts, on_device(): table_term.reshape(parts, tab_rows, own_blocks, width).transpose(0, 2, 1, 3)  14.6 us
    reshape x1, local copies, waits for them, and re-layouts, on_device(): stacked = jnp.concatenate(pieces, axis=1).reshape(parts * 8, -1)  11.9 us
    reshape x1, local copies, waits for them, and re-layouts, on_device(): pieces = [qkv_term.reshape(parts, qkv_rows * 3 * local_cols), wo_term.res...  11.1 us
  transfers between devices with their start and end apart: 4, of which 3 were waited for; matrix products, arithmetic and copies ran while one was open for 14% of the time, Pallas kernels for 0%

profile of v1, /device:TPU:1, one launch (start us, length us, event | category | flops | bytes accessed | tf_op | source)
XLA Modules:
  0.0 529.7 jit_solution(5040138010901825369)
XLA Ops:
  7.2 1.4 slice.76
  8.7 2.3 fusion.59
  11.1 1.2 convolution_convert_fusion.4
  12.5 4.5 convolution_convert_fusion
  17.1 3.7 reshape.211
  20.7 4.8 slice_bitcast_fusion
  25.5 1.3 copy-done.4
  26.9 1.2 fusion.6
  28.1 1.5 copy.74
  29.6 2.2 fusion.13
  31.8 1.2 convert_bitcast_fusion
  33.0 0.8 copy.75
  33.8 2.3 fusion.2
  36.3 3.5 gather_fusion
  40.5 0.9 convolution_convert_fusion.2
  41.9 48.3 %all-reduce.10.cloned.1.call-done = (bf16[64,1024]{1,0:T(8,128)(2,1)}, bf16[64,1024]{1,0:T(8,128)(2,1)}) async-done(((bf16[64,1024]{1,0:T(8,128)(2,1)}, bf16[64,1024]{1,0:T(8,128)(2,1)}), (bf16[64,1024]{1,0:T(8,128)(2,1)}, bf16[64,1024]{1,0:T(8,128)(2,1)})) %all-reduce.10.cloned.1.call-update) | async-done | bytes 262160 | tf_op jit(solution)/shard_map/psum | solution.py:60
  90.2 1.1 fusion.29
  91.3 1.1 multiply_reduce_fusion.3
  92.5 1.0 add_convert_fusion
  93.5 3.7 multiply_reduce_fusion
  97.4 7.6 %psum.30 = f32[64]{0:T(128)S(1)} all-reduce(f32[64]{0:T(128)S(1)} %get-tuple-element.65), channel_id=1, replica_groups=mesh['ment'=64,'ent'=4] {'ent'}, use_global_device_ids=true, to_apply=%region_8.9 | all-reduce | flops 64 | bytes 512 | tf_op jit(solution)/shard_map/psum | solution.py:74
  105.2 3.7 convolution_convert_fusion.1
  109.4 4.5 convolution_bitcast_fusion
  113.9 9.0 %copy.64 = f32[256,8,1024]{2,1,0:T(8,128)} copy(f32[256,8,1024]{0,2,1:T(8,128)} %convolution_bitcast_fusion) | data formatting | bytes 16777216 | tf_op jit(solution)/shard_map/mbr,md->rbd/transpose | solution.py:140
  123.0 10.4 %scatter_fusion = f32[256,8,1024]{2,1,0:T(8,128)} fusion(f32[256,8,1024]{2,1,0:T(8,128)} %copy.64, s32[64]{0:T(128)S(1)} %fusion.37, f32[64,1024]{1,0:T(8,128)S(1)} %fusion.38), kind=kCustom, calls=%fused_computation.1 | custom fusion | flops 65536 | bytes 786944 | tf_op jit(solution)/shard_map/scatter-add | solution.py:143
  133.5 14.6 %copy.110 = f32[64,4,8,1024]{3,1,2,0:T(4,128)} copy(f32[64,4,8,1024]{3,2,1,0:T(8,128)} %bitcast.153) | data formatting | bytes 16777216 | tf_op jit(solution)/shard_map/reshape | solution.py:151
  148.0 11.1 %reshape.221 = f32[64,32768]{1,0:T(8,128)} reshape(f32[64,8,4,1024]{3,2,1,0:T(4,128)} %bitcast.154) | data formatting | bytes 16777216 | tf_op jit(solution)/shard_map/reshape | solution.py:153
  159.2 1.3 multiply_reduce_fusion.1
  161.2 2.8 fusion
  163.9 1.5 copy.79
  165.4 1.8 fusion.9
  167.2 3.8 multiply_bitcast_fusion
  171.0 2.5 multiply_bitcast_fusion.1
  173.4 5.5 %maximum_convert_fusion = bf16[64,32,2,4,64]{4,3,2,1,0:T(4,128)(2,1)} fusion(bf16[64,32,1,4,64]{4,3,2,1,0:T(4,128)(2,1)S(1)} %multiply_bitcast_fusion, bf16[64,32,1,4,64]{4,3,2,1,0:T(4,128)(2,1)S(1)} %multiply_bitcast_fusion.1), kind=kLoop, calls=%fused_computation.2 | loop fusion | flops 1048576 | bytes 4194304 | tf_op jit(solution)/shard_map/convert_element_type | solution.py:115
  178.9 7.6 %convert_element_type.119 = bf16[64,32,512]{2,1,0:T(8,128)(2,1)} reshape(bf16[64,32,2,4,64]{4,3,2,1,0:T(4,128)(2,1)} %maximum_convert_fusion) | data formatting | bytes 4194304 | tf_op jit(solution)/shard_map/convert_element_type | solution.py:115
  186.5 0.8 copy.80
  187.3 2.3 fusion.4
  189.8 6.6 %fusion.61 = f32[512,1024,1]{1,0,2:T(8,128)} fusion(bf16[64,32,512]{2,1,0:T(8,128)(2,1)} %convert_element_type.119, bf16[64,32,1024]{2,1,0:T(8,128)(2,1)} %param.14), kind=kOutput, calls=%fused_computation.115 | convolution fusion | flops 2147483648 | bytes 8388608 | tf_op jit(solution)/shard_map/dot_general | solution.py:13
  196.3 2.8 copy.59
  199.2 1.4 convolution_bitcast_fusion.2
  200.6 3.8 copy.58
  204.4 5.1 pad_maximum_fusion
  209.5 5.4 %reshape.217 = f32[64,12288]{1,0:T(8,128)} reshape(f32[1024,3,256]{2,1,0:T(4,128)} %pad_maximum_fusion) | data formatting | bytes 6291456 | tf_op jit(solution)/shard_map/reshape | solution.py:149
  214.9 3.9 constant_dynamic-update-slice_fusion.2
  218.9 1.3 convolution_bitcast_fusion.1
  220.2 2.5 copy.62
  222.8 1.6 copy.68
  224.8 2.3 constant_dynamic-update-slice_fusion.1
  227.1 7.3 %constant_dynamic-update-slice_fusion = f32[64,50176]{1,0:T(8,128)} fusion(f32[64,50176]{1,0:T(8,128)} %constant_dynamic-update-slice_fusion.1, f32[64,32768]{1,0:T(8,128)} %reshape.221), kind=kLoop, calls=%fused_computation.75 | loop fusion | bytes 16777216
  234.4 1.4 dynamic-update-slice.9
  235.8 1.8 dynamic-update-slice.10
  237.6 11.9 %reshape.223 = f32[512,6272]{1,0:T(8,128)} reshape(f32[64,50176]{1,0:T(8,128)} %dynamic-update-slice.10) | data formatting | bytes 25690112 | tf_op jit(solution)/shard_map/reshape | solution.py:159
  249.7 1.1 copy-done.3
  250.8 1.1 copy.57
  252.6 1.3 fusion.15
  253.9 4.1 fusion.60
  258.0 3.2 copy-done.2
  261.6 6.1 %scatter-add.14 = f32[64,32,1024]{2,1,0:T(8,128)} dynamic-update-slice(f32[64,32,1024]{2,1,0:T(8,128)} %copy-done.2, f32[64,1,1024]{2,1,0:T(1,128)S(1)} %slice_add_fusion, s32[]{:T(128)} %constant.77.clone.1, s32[]{:T(128)} %constant.77.clone.1, s32[]{:T(128)} %constant.77.clone.1) | dynamic-update-slice | bytes 524292 | tf_op jit(solution)/shard_map/scatter-add | solution.py:130
  267.7 6.4 %convert_element_type.122 = bf16[64,32,1024]{2,1,0:T(8,128)(2,1)} convert(f32[64,32,1024]{2,1,0:T(8,128)} %scatter-add.14) | non-fusion elementwise | flops 2097152 | bytes 12582912 | tf_op jit(solution)/shard_map/convert_element_type | solution.py:130
  276.1 191.8 %all-reduce.8.cloned.1.call-done = f32[512,6272]{1,0:T(8,128)} async-done(((f32[512,6272]{1,0:T(8,128)}), f32[512,6272]{1,0:T(8,128)}) %all-reduce.8.cloned.1.call-update) | async-done | bytes 12845072
  467.9 0.9 constant_dynamic-slice_fusion
  472.1 47.7 %reduce-scatter.2.cloned.1.call-done = bf16[16,32,1024]{2,1,0:T(8,128)(2,1)} async-done(((bf16[64,32,1024]{2,1,0:T(8,128)(2,1)}), bf16[16,32,1024]{2,1,0:T(8,128)(2,1)}) %reduce-scatter.2.cloned.1.call-update) | async-done | bytes 1048592 | tf_op jit(solution)/shard_map/reduce_scatter | solution.py:129
  519.8 1.5 convert_element_type.123
  521.8 1.1 convert_element_type.124
  (91 shorter events, 10.3 us)
Async XLA Ops:
  7.2 33.4 %copy-start = (bf16[256,1024]{1,0:T(8,128)(2,1)S(1)}, bf16[256,1024]{1,0:T(8,128)(2,1)}, u32[]{:S(2)}) copy-start(bf16[256,1024]{1,0:T(8,128)(2,1)} %param.16) | copy-start | bytes 1572868
  7.2 83.0 %all-reduce.10.cloned.1.call-start = ((), (), s32[]{:S(2)}) async-start(), calls=%async_computation.4 | async-start | bytes 524288 | tf_op jit(solution)/shard_map/psum | solution.py:60
  20.7 8.8 %copy-start.11 = (s32[64]{0:T(128)S(1)}, s32[64]{0:T(128)}, u32[]{:S(2)}) copy-start(s32[64]{0:T(128)} %param.20) | copy-start | bytes 772
  25.5 1.4 copy-start.4
  29.5 3.5 copy-start.10
  29.5 3.5 copy-start.9
  31.8 9.7 %copy-start.12 = (s32[1,4]{1,0:T(1,128)S(1)}, s32[1,4]{1,0:T(1,128)}, u32[]{:S(2)}) copy-start(s32[1,4]{1,0:T(1,128)} %param.23) | copy-start | bytes 52
  31.8 60.7 %copy-start.7 = (f32[1024]{0:T(1024)S(1)}, f32[1024]{0:T(1024)}, u32[]{:S(2)}) copy-start(f32[1024]{0:T(1024)} %param.17) | copy-start | bytes 12292
  31.8 60.7 %copy-start.8 = (f32[1024]{0:T(1024)S(1)}, f32[1024]{0:T(1024)}, u32[]{:S(2)}) copy-start(f32[1024]{0:T(1024)} %param.18) | copy-start | bytes 12292
  41.4 117.7 %all-reduce.6.cloned.1.call-start = ((), (), s32[]{:S(2)}) async-start(), calls=%async_computation.1 | async-start | bytes 262144 | tf_op jit(solution)/shard_map/psum | solution.py:80
  90.2 7.0 %copy-start.6 = (bf16[64,1024]{1,0:T(8,128)(2,1)S(1)}, bf16[64,1024]{1,0:T(8,128)(2,1)}, u32[]{:S(2)}) copy-start(bf16[64,1024]{1,0:T(8,128)(2,1)} %get-tuple-element.53) | copy-start | bytes 393220
  108.9 359.1 %all-reduce.8.cloned.1.call-start = ((), (), s32[]{:S(2)}) async-start(), calls=%async_computation.3 | async-start | bytes 25690112
  148.0 11.1 %copy-start.5 = (bf16[64,1024]{1,0:T(8,128)(2,1)S(1)}, bf16[64,1024]{1,0:T(8,128)(2,1)}, u32[]{:S(2)}) copy-start(bf16[64,1024]{1,0:T(8,128)(2,1)} %get-tuple-element.54) | copy-start | bytes 393220
  249.6 1.2 copy-start.3
  249.6 270.2 %reduce-scatter.2.cloned.1.call-start = ((), (), s32[]{:S(2)}) async-start(), calls=%async_computation.2 | async-start | bytes 5242880 | tf_op jit(solution)/shard_map/reduce_scatter | solution.py:129
  258.0 3.2 copy-start.2
  274.2 0.7 copy-start.13
  468.9 54.0 %copy-start.1 = (bf16[256,1024]{1,0:T(8,128)(2,1)S(1)}, bf16[256,1024]{1,0:T(8,128)(2,1)}, u32[]{:S(2)}) copy-start(bf16[256,1024]{1,0:T(8,128)(2,1)} %param.16) | copy-start | bytes 1572868
Sparse Core Ops, SparseCore 0:
  41.5 48.6 all-reduce.9
  109.0 47.2 all-reduce.5
  249.7 218.1 all-reduce.7
  470.5 49.1 reduce-scatter.1

commit v2 on v1

--- a/solution.py
+++ b/solution.py
@@ -1,9 +1,141 @@
+import functools
+
 import jax
 import jax.numpy as jnp
 from jax import lax
+from jax.experimental import pallas as pl
+from jax.experimental.pallas import tpu as pltpu
 from jax.sharding import PartitionSpec as P
 
 HD = 64
+MESH = pl.DeviceIdType.MESH
+
+
+def _greet_peers(row, me, n):
+    barrier = pltpu.get_barrier_semaphore()
+    for k in range(1, n):
+        pl.semaphore_signal(
+            barrier, inc=1, device_id=(row, lax.rem(me + k, n)), device_id_type=MESH
+        )
+    pl.semaphore_wait(barrier, n - 1)
+
+
+def _peer_sum_kernel(n, x_ref, out_ref, recv, send_sem, recv_sem, own_sem):
+    row = lax.axis_index("ment")
+    me = lax.axis_index("ent")
+    _greet_peers(row, me, n)
+    sends = []
+    for k in range(1, n):
+        copy = pltpu.make_async_remote_copy(
+            src_ref=x_ref,
+            dst_ref=recv.at[me],
+            send_sem=send_sem.at[k - 1],
+            recv_sem=recv_sem.at[me],
+            device_id=(row, lax.rem(me + k, n)),
+            device_id_type=MESH,
+        )
+        copy.start()
+        sends.append(copy)
+    own = pltpu.make_async_copy(x_ref, recv.at[me], own_sem)
+    own.start()
+    for k in range(1, n):
+        source = lax.rem(me + n - k, n)
+        pltpu.make_async_remote_copy(
+            src_ref=x_ref,
+            dst_ref=recv.at[source],
+            send_sem=send_sem.at[k - 1],
+            recv_sem=recv_sem.at[source],
+            device_id=(row, source),
+            device_id_type=MESH,
+        ).wait_recv()
+    own.wait()
+    for copy in sends:
+        copy.wait_send()
+    total = recv[0].astype(jnp.float32)
+    for s in range(1, n):
+        total = total + recv[s].astype(jnp.float32)
+    out_ref[...] = total
+
+
+def peer_sum(x, collective):
+    n = lax.axis_size("ent")
+    return pl.pallas_call(
+        functools.partial(_peer_sum_kernel, n),
+        out_shape=jax.ShapeDtypeStruct(x.shape, jnp.float32),
+        in_specs=[pl.BlockSpec(memory_space=pltpu.VMEM)],
+        out_specs=pl.BlockSpec(memory_space=pltpu.VMEM),
+        scratch_shapes=[
+            pltpu.VMEM((n,) + x.shape, x.dtype),
+            pltpu.SemaphoreType.DMA((n - 1,)),
+            pltpu.SemaphoreType.DMA((n,)),
+            pltpu.SemaphoreType.DMA(()),
+        ],
+        compiler_params=pltpu.CompilerParams(collective_id=collective, has_side_effects=True),
+    )(x)
+
+
+def _peer_scatter_kernel(n, y_ref, resid_ref, out_ref, recv, send_sem, recv_sem, own_sem):
+    row = lax.axis_index("ment")
+    me = lax.axis_index("ent")
+    share = out_ref.shape[0]
+    _greet_peers(row, me, n)
+    sends = []
+    for k in range(1, n):
+        target = lax.rem(me + k, n)
+        copy = pltpu.make_async_remote_copy(
+            src_ref=y_ref.at[pl.ds(target * share, share)],
+            dst_ref=recv.at[me],
+            send_sem=send_sem.at[k - 1],
+            recv_sem=recv_sem.at[me],
+            device_id=(row, target),
+            device_id_type=MESH,
+        )
+        copy.start()
+        sends.append(copy)
+    own = pltpu.make_async_copy(y_ref.at[pl.ds(me * share, share)], recv.at[me], own_sem)
+    own.start()
+    for k in range(1, n):
+        source = lax.rem(me + n - k, n)
+        pltpu.make_async_remote_copy(
+            src_ref=y_ref.at[pl.ds(0, share)],
+            dst_ref=recv.at[source],
+            send_sem=send_sem.at[k - 1],
+            recv_sem=recv_sem.at[source],
+            device_id=(row, source),
+            device_id_type=MESH,
+        ).wait_recv()
+    own.wait()
+    for copy in sends:
+        copy.wait_send()
+    first = lax.broadcasted_iota(jnp.int32, out_ref.shape[1:], 0) == 0
+
+    def one_mention(i, carry):
+        total = recv[0, i].astype(jnp.float32)
+        for s in range(1, n):
+            total = total + recv[s, i].astype(jnp.float32)
+        total = total + jnp.where(first, resid_ref[pl.ds(i, 1), :], 0.0)
+        out_ref[i] = total.astype(out_ref.dtype)
+        return carry
+
+    lax.fori_loop(0, share, one_mention, 0)
+
+
+def peer_scatter(y, resid, collective):
+    n = lax.axis_size("ent")
+    share = y.shape[0] // n
+    return pl.pallas_call(
+        functools.partial(_peer_scatter_kernel, n),
+        out_shape=jax.ShapeDtypeStruct((share,) + y.shape[1:], jnp.bfloat16),
+        in_specs=[pl.BlockSpec(memory_space=pltpu.VMEM)] * 2,
+        out_specs=pl.BlockSpec(memory_space=pltpu.VMEM),
+        scratch_shapes=[
+            pltpu.VMEM((n, share) + y.shape[1:], y.dtype),
+            pltpu.SemaphoreType.DMA((n - 1,)),
+            pltpu.SemaphoreType.DMA((n,)),
+            pltpu.SemaphoreType.DMA(()),
+        ],
+        compiler_params=pltpu.CompilerParams(collective_id=collective, has_side_effects=True),
+    )(y, resid)
 
 
 ln_eps = 1e-06
@@ -55,10 +187,10 @@
     flat_table = table.reshape(own_blocks * block_rows, width)
     picked = flat_table[safe_block * block_rows + gold_row]
     picked = jnp.where(owned[:, None], picked.astype(jnp.float32), 0.0)
-    attn_out, gold_sum = (
-        lax.psum(attn_part.astype(jnp.bfloat16), "ent").astype(jnp.float32),
-        lax.psum(picked.astype(jnp.bfloat16), "ent").astype(jnp.float32),
-    )
+    both = peer_sum(
+        jnp.concatenate([attn_part.astype(jnp.bfloat16), picked.astype(jnp.bfloat16)], axis=0), 0
+    )
+    attn_out, gold_sum = both[:ment_rows], both[ment_rows:]
     golds = gold_sum.astype(jnp.bfloat16)
     resid = cls_rows.astype(jnp.float32) + attn_out
     centre = resid - jnp.mean(resid, axis=-1, keepdims=True)
@@ -71,15 +203,15 @@
     listed = jnp.any(neg_blocks[0][:, None] == block_ids[None, :], axis=0).astype(jnp.float32)
     row_mask = jnp.repeat(listed, block_rows)
     neg_part = jnp.sum(jnp.exp(negscore) * row_mask[None, :], axis=1)
-    neg_total = lax.psum(neg_part, "ent")
+    neg_total = peer_sum(jnp.pad(neg_part.reshape(1, ment_rows), ((0, 7), (0, 0))), 1)[0]
     lse = jnp.log(jnp.sum(jnp.exp(inbatch), axis=1) + neg_total)
     eye = jnp.eye(ment_rows, dtype=jnp.float32)
     w_inb = (jnp.exp(inbatch - lse[:, None]) - eye).astype(jnp.bfloat16)
     w_neg = (jnp.exp(negscore - lse[:, None]) * row_mask[None, :]).astype(jnp.bfloat16)
     embed_part = jnp.dot(w_neg, flat_table, preferred_element_type=jnp.float32)
-    d_embed = jnp.dot(w_inb, golds, preferred_element_type=jnp.float32) + lax.psum(
-        embed_part.astype(jnp.bfloat16), "ent"
-    ).astype(jnp.float32)
+    d_embed = jnp.dot(w_inb, golds, preferred_element_type=jnp.float32) + peer_sum(
+        embed_part.astype(jnp.bfloat16), 2
+    )
     ln_terms = jnp.stack([jnp.sum(d_embed * normed, axis=0), jnp.sum(d_embed, axis=0)])
     upper = d_embed * ln_gain
     d_resid = rstd * (
@@ -126,14 +258,12 @@
     token_term = contract(grad_part, w_keyval, 1, 1).reshape(
         share * lax.axis_size("ent"), seq_len, width
     )
-    summed = lax.psum_scatter(
+    resid_mine = lax.dynamic_slice_in_dim(d_resid, owner * share, share, 0)
+    grad_hidden = peer_scatter(
         token_term.at[:, 0, :].add(contract(query_gradient, w_query, 1, 1)).astype(jnp.bfloat16),
-        "ent",
-        scatter_dimension=0,
-        tiled=True,
-    ).astype(jnp.float32)
-    resid_mine = lax.dynamic_slice_in_dim(d_resid, owner * share, share, 0)
-    grad_hidden = summed.at[:, 0, :].add(resid_mine).astype(jnp.bfloat16)
+        resid_mine,
+        3,
+    )
     gold_terms = contract(w_inb, embed, 0, 0)
     weight_blocks = w_neg.reshape(ment_rows, own_blocks, block_rows)
     count = lax.axis_size("ment") * (block_rows // lax.axis_size("ment"))

time: 540 us -> 472 us (0.87)
  waiting for transfers between devices: 288 us -> 142 us
  Pallas kernels: 0 us -> 83.9 us
  blocking collectives: 7.58 us -> 0 us
    pallas_call x0 -> x4, Pallas kernels: none -> 83.9 us  [the longest x1 50.9 us: peer_scatter(): pl.pallas_call(functools.partial(_peer_scatter_kernel, n), out_shape=jax....]
    unnamed x5 -> x2, waiting for transfers between devices: 192 us -> 142 us
    psum x2 -> x0, waiting for transfers between devices: 48.3 us -> none  [the longest x1 48.3 us: on_device(): lax.psum(picked.astype(jnp.bfloat16), 'ent').astype(jnp.float32)]
    reduce_scatter x1 -> x0, waiting for transfers between devices: 47.7 us -> none  [on_device(): lax.psum_scatter(token_term.at[:, 0, :].add(contract(query_gradient, w_qu...]
    psum x1 -> x0, blocking collectives: 7.58 us -> none  [on_device(): neg_total = lax.psum(neg_part, 'ent')]
    unnamed x39 -> x67, local copies, waits for them, and re-layouts: 24.2 us -> 24.6 us
  transfers between devices with their start and end apart: 4 -> 1, of which waited for: 3 -> 1; matrix products, arithmetic and copies ran while one was open for 14% -> 5% of each run, Pallas kernels for 0% -> 11%
where the time goes in v2:
time: 472 us; the launch traced here: 466 us
  waiting for transfers between devices  142 us (30%)
  local copies, waits for them, and re-layouts  132 us (28%)
  Pallas kernels  83.9 us (18%)
  other arithmetic  46.5 us (10%)
  matrix products  45.4 us (10%)
  between operations  15.6 us (3%)
    unnamed x2, waiting for transfers between devices  142 us
    pallas_call x1, Pallas kernels, peer_scatter(): pl.pallas_call(functools.partial(_peer_scatter_kernel, n), out_shape=jax....  50.9 us
    pallas_call x3, Pallas kernels, peer_sum(): pl.pallas_call(functools.partial(_peer_sum_kernel, n), out_shape=jax.Shap...  33.1 us
    unnamed x67, local copies, waits for them, and re-layouts  24.6 us
    dot_general x9, matrix products, contract(): lax.dot_general(left, right, (((left_dim,), (right_dim,)), ((), ())), pre...  21.2 us
    reshape x1, local copies, waits for them, and re-layouts, on_device(): table_term.reshape(parts, tab_rows, own_blocks, width).transpose(0, 2, 1, 3)  14.6 us
    reshape x1, local copies, waits for them, and re-layouts, on_device(): stacked = jnp.concatenate(pieces, axis=1).reshape(parts * 8, -1)  12 us
    reshape x1, local copies, waits for them, and re-layouts, on_device(): pieces = [qkv_term.reshape(parts, qkv_rows * 3 * local_cols), wo_term.res...  11 us
  transfers between devices with their start and end apart: 1, of which 1 were waited for; matrix products, arithmetic and copies ran while one was open for 5% of the time, Pallas kernels for 11%

profile of v2, /device:TPU:1, one launch (start us, length us, event | category | flops | bytes accessed | tf_op | source)
XLA Modules:
  0.0 465.9 jit_solution(7103368942073691122)
XLA Ops:
  7.2 1.4 slice.64
  8.7 2.4 fusion.59
  11.1 1.2 convolution_convert_fusion.4
  13.0 4.5 convolution_convert_fusion
  17.5 4.2 reshape.192
  21.7 4.8 %slice_bitcast_fusion = (bf16[64,32,4,64]{3,2,1,0:T(4,128)(2,1)}, bf16[64,32,4,64]{3,2,1,0:T(4,128)(2,1)S(1)}) fusion(bf16[64,32,2,4,64]{4,3,2,1,0:T(4,128)(2,1)} %reshape.192), kind=kLoop, calls=%fused_computation.9 | loop fusion | bytes 4194304 | tf_op jit(solution)/shard_map/squeeze | solution.py:169
  26.5 1.3 copy-done.8
  27.8 1.2 fusion.6
  29.6 6.0 %fusion.13 = f32[64,4,32]{1,2,0:T(8,128)S(1)} fusion(f32[64,4,1,32]{1,3,0,2:T(8,128)S(1)} %copy.74, f32[64,32]{1,0:T(8,128)S(1)} %fusion.31), kind=kOutput, calls=%fused_computation.34 | output fusion | flops 41247 | bytes 73728 | tf_op jit(solution)/shard_map/div | solution.py:177
  35.6 1.0 copy-done.4
  36.8 0.8 copy.75
  37.7 2.3 fusion.2
  40.1 3.5 gather_fusion
  44.6 17.5 %shard_map.137 = f32[128,1024]{1,0:T(8,128)} custom-call(bf16[128,1024]{1,0:T(8,128)(2,1)} %pad_maximum_fusion.1.x_ref), custom_call_target="tpu_custom_call" | custom-call | tf_op jit(solution)/shard_map/pallas_call | solution.py:62
  62.2 1.1 fusion.58
  63.8 1.7 exponential_reduce_fusion
  65.6 3.8 multiply_reduce_fusion
  70.0 6.7 %shard_map.138 = f32[8,64]{1,0:T(8,128)} custom-call(f32[8,64]{1,0:T(8,128)} %pad.6.x_ref), custom_call_target="tpu_custom_call" | custom-call | tf_op jit(solution)/shard_map/pallas_call | solution.py:62
  77.5 3.7 convolution_convert_fusion.1.x_ref
  81.3 8.9 %shard_map.139 = f32[64,1024]{1,0:T(8,128)} custom-call(bf16[64,1024]{1,0:T(8,128)(2,1)} %convolution_convert_fusion.1.x_ref), custom_call_target="tpu_custom_call" | custom-call | tf_op jit(solution)/shard_map/pallas_call | solution.py:62
  90.2 1.4 multiply_reduce_fusion.1
  91.6 1.5 convert_bitcast_fusion.1
  94.4 0.9 fusion.37
  95.4 2.8 fusion
  98.1 1.5 copy.79
  99.6 2.4 fusion.9
  102.1 2.5 multiply_bitcast_fusion
  104.5 2.7 multiply_bitcast_fusion.1
  107.2 5.4 %maximum_convert_fusion = bf16[64,32,2,4,64]{4,3,2,1,0:T(4,128)(2,1)} fusion(bf16[64,32,1,4,64]{4,3,2,1,0:T(4,128)(2,1)S(1)} %multiply_bitcast_fusion, bf16[64,32,1,4,64]{4,3,2,1,0:T(4,128)(2,1)S(1)} %multiply_bitcast_fusion.1), kind=kLoop, calls=%fused_computation.2 | loop fusion | flops 1048576 | bytes 4194304 | tf_op jit(solution)/shard_map/convert_element_type | solution.py:247
  112.7 7.6 %convert_element_type.106 = bf16[64,32,512]{2,1,0:T(8,128)(2,1)} reshape(bf16[64,32,2,4,64]{4,3,2,1,0:T(4,128)(2,1)} %maximum_convert_fusion) | data formatting | bytes 4194304 | tf_op jit(solution)/shard_map/convert_element_type | solution.py:247
  121.1 2.3 fusion.4
  123.5 6.5 %fusion.61 = f32[512,1024,1]{1,0,2:T(8,128)} fusion(bf16[64,32,512]{2,1,0:T(8,128)(2,1)} %convert_element_type.106, bf16[64,32,1024]{2,1,0:T(8,128)(2,1)} %param.12), kind=kOutput, calls=%fused_computation.117 | convolution fusion | flops 2147483648 | bytes 8388608 | tf_op jit(solution)/shard_map/dot_general | solution.py:145
  130.0 2.9 copy.59
  132.9 1.3 convolution_bitcast_fusion.2
  134.2 3.6 copy.58
  137.8 5.0 %pad_maximum_fusion = f32[1024,3,256]{2,1,0:T(4,128)} fusion(f32[1024,2,256]{2,1,0:T(2,128)S(1)} %copy.59, f32[1024,1,256]{2,1,0:T(1,128)} %copy.58), kind=kLoop, calls=%fused_computation.4 | loop fusion | flops 786432 | bytes 6291456 | tf_op jit(solution)/shard_map/concatenate | solution.py:253
  142.9 5.5 %reshape.198 = f32[64,12288]{1,0:T(8,128)} reshape(f32[1024,3,256]{2,1,0:T(4,128)} %pad_maximum_fusion) | data formatting | bytes 6291456 | tf_op jit(solution)/shard_map/reshape | solution.py:279
  148.3 3.9 constant_dynamic-update-slice_fusion.2
  152.4 1.3 convolution_bitcast_fusion.1
  153.7 2.5 copy.62
  156.3 1.6 copy.68
  157.8 4.5 convolution_bitcast_fusion
  162.4 8.9 %copy.64 = f32[256,8,1024]{2,1,0:T(8,128)} copy(f32[256,8,1024]{0,2,1:T(8,128)} %convolution_bitcast_fusion) | data formatting | bytes 16777216 | tf_op jit(solution)/shard_map/mbr,md->rbd/transpose | solution.py:270
  171.3 10.7 %scatter_fusion = f32[256,8,1024]{2,1,0:T(8,128)} fusion(f32[256,8,1024]{2,1,0:T(8,128)} %copy.64, s32[64]{0:T(128)S(1)} %fusion.36, f32[64,1024]{1,0:T(8,128)S(1)} %fusion.37), kind=kCustom, calls=%fused_computation.1 | custom fusion | flops 65536 | bytes 786944 | tf_op jit(solution)/shard_map/scatter-add | solution.py:273
  182.0 14.6 %copy.107 = f32[64,4,8,1024]{3,1,2,0:T(4,128)} copy(f32[64,4,8,1024]{3,2,1,0:T(8,128)} %bitcast.150) | data formatting | bytes 16777216 | tf_op jit(solution)/shard_map/reshape | solution.py:281
  196.6 11.0 %reshape.202 = f32[64,32768]{1,0:T(8,128)} reshape(f32[64,8,4,1024]{3,2,1,0:T(4,128)} %bitcast.151) | data formatting | bytes 16777216 | tf_op jit(solution)/shard_map/reshape | solution.py:283
  208.1 1.0 constant_dynamic-update-slice_fusion.1
  209.1 7.2 %constant_dynamic-update-slice_fusion = f32[64,50176]{1,0:T(8,128)} fusion(f32[64,50176]{1,0:T(8,128)} %constant_dynamic-update-slice_fusion.1, f32[64,32768]{1,0:T(8,128)} %reshape.202), kind=kLoop, calls=%fused_computation.75 | loop fusion | bytes 16777216
  216.3 1.4 dynamic-update-slice.6
  217.7 1.9 dynamic-update-slice.7
  219.6 12.0 %reshape.204 = f32[512,6272]{1,0:T(8,128)} reshape(f32[64,50176]{1,0:T(8,128)} %dynamic-update-slice.7) | data formatting | bytes 25690112 | tf_op jit(solution)/shard_map/reshape | solution.py:289
  231.6 1.2 copy-done.3
  232.8 1.1 copy.57
  233.9 1.0 reshape.229
  234.9 1.3 fusion.15
  236.2 4.1 fusion.60
  240.3 3.2 copy-done.2
  243.9 6.1 %scatter-add.12 = f32[64,32,1024]{2,1,0:T(8,128)} dynamic-update-slice(f32[64,32,1024]{2,1,0:T(8,128)} %copy-done.2, f32[64,1,1024]{2,1,0:T(1,128)S(1)} %slice_add_fusion, s32[]{:T(128)} %constant.56.clone.1, s32[]{:T(128)} %constant.56.clone.1, s32[]{:T(128)} %constant.56.clone.1) | dynamic-update-slice | bytes 524292 | tf_op jit(solution)/shard_map/scatter-add | solution.py:263
  250.0 6.4 %convert_element_type.109.y_ref = bf16[64,32,1024]{2,1,0:T(8,128)(2,1)} convert(f32[64,32,1024]{2,1,0:T(8,128)} %scatter-add.12) | non-fusion elementwise | flops 2097152 | bytes 12582912 | tf_op jit(solution)/shard_map/convert_element_type | solution.py:263
  257.0 50.9 %shard_map.140 = bf16[16,32,1024]{2,1,0:T(8,128)(2,1)} custom-call(bf16[64,32,1024]{2,1,0:T(8,128)(2,1)} %convert_element_type.109.y_ref, f32[16,1024]{1,0:T(8,128)} %constant_dynamic-slice_fusion.1.resid_ref), custom_call_target="tpu_custom_call" | custom-call | tf_op jit(solution)/shard_map/pallas_call | solution.py:126
  309.1 142.1 %all-reduce.4.cloned.1.call-done = f32[512,6272]{1,0:T(8,128)} async-done(((f32[512,6272]{1,0:T(8,128)}), f32[512,6272]{1,0:T(8,128)}) %all-reduce.4.cloned.1.call-update) | async-done | bytes 12845072
  451.3 0.9 constant_dynamic-slice_fusion
  454.8 0.9 slice.89
  457.8 1.0 copy.116
  (111 shorter events, 13.7 us)
Async XLA Ops:
  7.2 36.5 %copy-start = (bf16[256,1024]{1,0:T(8,128)(2,1)S(1)}, bf16[256,1024]{1,0:T(8,128)(2,1)}, u32[]{:S(2)}) copy-start(bf16[256,1024]{1,0:T(8,128)(2,1)} %param.14) | copy-start | bytes 1572868
  7.2 444.1 %all-reduce.4.cloned.1.call-start = ((), (), s32[]{:S(2)}) async-start(), calls=%async_computation | async-start | bytes 25690112
  8.7 53.5 %copy-start.9 = (bf16[64,1,1024]{2,1,0:T(2,128)(2,1)}, bf16[64,1,1024]{2,1,0:T(2,128)(2,1)S(1)}, u32[]{:S(2)}) copy-start(bf16[64,1,1024]{2,1,0:T(2,128)(2,1)S(1)} %slice.64) | copy-start | bytes 393220
  12.4 0.6 copy-start.14
  21.7 7.8 %copy-start.25 = (s32[64]{0:T(128)S(1)}, s32[64]{0:T(128)}, u32[]{:S(2)}) copy-start(s32[64]{0:T(128)} %param.18) | copy-start | bytes 772
  26.5 1.3 copy-start.8
  29.5 7.3 %copy-start.23 = (s32[64]{0:T(128)S(1)}, s32[64]{0:T(128)}, u32[]{:S(2)}) copy-start(s32[64]{0:T(128)} %param.19) | copy-start | bytes 772
  29.5 7.3 %copy-start.21 = (s32[64]{0:T(128)S(1)}, s32[64]{0:T(128)}, u32[]{:S(2)}) copy-start(s32[64]{0:T(128)} %param.20) | copy-start | bytes 772
  35.5 1.0 copy-start.4
  36.7 26.8 %copy-start.26 = (s32[1,4]{1,0:T(1,128)S(1)}, s32[1,4]{1,0:T(1,128)}, u32[]{:S(2)}) copy-start(s32[1,4]{1,0:T(1,128)} %param.21) | copy-start | bytes 52
  36.7 27.0 %copy-start.17 = (f32[1024]{0:T(1024)S(1)}, f32[1024]{0:T(1024)}, u32[]{:S(2)}) copy-start(f32[1024]{0:T(1024)} %param.15) | copy-start | bytes 12292
  36.7 27.0 %copy-start.20 = (f32[1024]{0:T(1024)S(1)}, f32[1024]{0:T(1024)}, u32[]{:S(2)}) copy-start(f32[1024]{0:T(1024)} %param.16) | copy-start | bytes 12292
  40.0 4.7 %copy-start.11 = (bf16[64,4,64]{2,1,0:T(4,128)(2,1)}, bf16[64,4,64]{2,1,0:T(4,128)(2,1)S(1)}, u32[]{:S(2)}) copy-start(bf16[64,4,64]{2,1,0:T(4,128)(2,1)S(1)} %convert_element_type.92) | copy-start | bytes 98308
  63.5 17.8 %copy-start.18 = (f32[64]{0:T(128)}, f32[64]{0:T(128)S(1)}, u32[]{:S(2)}) copy-start(f32[64]{0:T(128)S(1)} %add_rsqrt_fusion) | copy-start | bytes 772
  65.6 24.6 %copy-start.7 = (f32[128,1024]{1,0:T(8,128)S(1)}, f32[128,1024]{1,0:T(8,128)}, u32[]{:S(2)}) copy-start(f32[128,1024]{1,0:T(8,128)} %shard_map.137) | copy-start | bytes 1572868
  77.3 12.8 %copy-start.19 = (f32[64]{0:T(128)}, f32[64]{0:T(128)S(1)}, u32[]{:S(2)}) copy-start(f32[64]{0:T(128)S(1)} %fusion.35) | copy-start | bytes 772
  77.5 16.0 %copy-start.15 = (bf16[64,256]{1,0:T(8,128)(2,1)S(1)}, bf16[64,256]{1,0:T(8,128)(2,1)}, u32[]{:S(2)}) copy-start(bf16[64,256]{1,0:T(8,128)(2,1)} %copy-done.14) | copy-start | bytes 98308
  77.5 16.1 %copy-start.12 = (bf16[64,4,64]{2,1,0:T(4,128)(2,1)S(1)}, bf16[64,4,64]{2,1,0:T(4,128)(2,1)}, u32[]{:S(2)}) copy-start(bf16[64,4,64]{2,1,0:T(4,128)(2,1)} %copy-done.11) | copy-start | bytes 98308
  77.5 16.9 %copy-start.22 = (s32[64]{0:T(128)S(1)}, s32[64]{0:T(128)}, u32[]{:S(2)}) copy-start(s32[64]{0:T(128)} %param.20) | copy-start | bytes 772
  77.5 16.9 %copy-start.24 = (s32[64]{0:T(128)S(1)}, s32[64]{0:T(128)}, u32[]{:S(2)}) copy-start(s32[64]{0:T(128)} %param.19) | copy-start | bytes 772
  130.0 2.9 copy-start.10
  148.3 3.9 copy-start.13
  148.3 4.1 copy-start.16
  196.6 11.4 %copy-start.5 = (f32[64,4096]{1,0:T(8,128)S(1)}, f32[64,4096]{1,0:T(8,128)}, u32[]{:S(2)}) copy-start(f32[64,4096]{1,0:T(8,128)} %copy.68) | copy-start | bytes 3145732
  231.6 1.2 copy-start.3
  240.3 3.2 copy-start.2
  256.4 51.5 %copy-start.27 = (u32[256]{0:T(256)S(1)}, u32[256]{0:T(256)}, u32[]{:S(2)}) copy-start(u32[256]{0:T(256)} %constant.86) | copy-start | bytes 3076
  257.0 201.7 %copy-start.1 = (bf16[256,1024]{1,0:T(8,128)(2,1)S(1)}, bf16[256,1024]{1,0:T(8,128)(2,1)}, u32[]{:S(2)}) copy-start(bf16[256,1024]{1,0:T(8,128)(2,1)} %param.14) | copy-start | bytes 1572868
  307.9 149.9 %copy-start.6 = (bf16[16,32,1024]{2,1,0:T(8,128)(2,1)S(1)}, bf16[16,32,1024]{2,1,0:T(8,128)(2,1)}, u32[]{:S(2)}) copy-start(bf16[16,32,1024]{2,1,0:T(8,128)(2,1)} %shard_map.140) | copy-start | bytes 3145732
Sparse Core Ops, SparseCore 0:
  231.7 219.4 all-reduce.3

commit v3 on v2

--- a/solution.py
+++ b/solution.py
@@ -272,27 +272,23 @@
     row_slot = jnp.where(inside, gold_row, count)
     table_term = neg_term.at[row_slot, safe_block].add(gold_terms, mode="drop")
     parts = lax.axis_size("ment")
+    place = lax.axis_index("ment")
     qkv_rows = width // parts
     wo_cols = width // parts
     tab_rows = block_rows // parts
-    pieces = [
-        qkv_term.reshape(parts, qkv_rows * 3 * local_cols),
-        wo_term.reshape(local_cols, parts, wo_cols).transpose(1, 0, 2).reshape(parts, -1),
-        table_term.reshape(parts, tab_rows, own_blocks, width)
-        .transpose(0, 2, 1, 3)
-        .reshape(parts, -1),
-        ln_terms.reshape(2, parts, wo_cols).transpose(1, 0, 2).reshape(parts, -1),
-    ]
-    sizes = [piece.shape[1] for piece in pieces]
-    padded = -sum(sizes) % 1024
-    pieces.append(jnp.zeros((parts, padded), jnp.float32))
-    stacked = jnp.concatenate(pieces, axis=1).reshape(parts * 8, -1)
-    merged = lax.psum_scatter(stacked, "ment", scatter_dimension=0, tiled=True).reshape(-1)
-    offsets = [sum(sizes[:k]) for k in range(len(sizes))]
-    grad_qkv = merged[offsets[0] : offsets[0] + sizes[0]].reshape(qkv_rows, 3, local_cols)
-    grad_wo = merged[offsets[1] : offsets[1] + sizes[1]].reshape(local_cols, wo_cols)
-    grad_table = merged[offsets[2] : offsets[2] + sizes[2]].reshape(own_blocks, tab_rows, width)
-    grad_ln = merged[offsets[3] : offsets[3] + sizes[3]].reshape(2, wo_cols)
+    terms = (qkv_term, wo_term, table_term, ln_terms)
+    summed_all = lax.psum(jnp.concatenate([term.reshape(-1) for term in terms]), "ment")
+    sums, at = [], 0
+    for term in terms:
+        sums.append(summed_all[at : at + term.size].reshape(term.shape))
+        at += term.size
+    qkv_sum, wo_sum, table_sum, ln_sum = sums
+    grad_qkv = lax.dynamic_slice_in_dim(qkv_sum, place * qkv_rows, qkv_rows, 0)
+    grad_wo = lax.dynamic_slice_in_dim(wo_sum, place * wo_cols, wo_cols, 1)
+    grad_ln = lax.dynamic_slice_in_dim(ln_sum, place * wo_cols, wo_cols, 1)
+    grad_table = jnp.transpose(
+        lax.dynamic_slice_in_dim(table_sum, place * tab_rows, tab_rows, 0), (1, 0, 2)
+    )
     return (grad_hidden, grad_qkv, grad_wo, grad_ln, grad_table)
 
 

time: 472 us -> 465 us (0.985)
  local copies, waits for them, and re-layouts: 132 us -> 108 us
  other arithmetic: 46.5 us -> 65.6 us
    psum x0 -> x1, waiting for transfers between devices: none -> 142 us  [on_device(): lax.psum(jnp.concatenate([term.reshape(-1) for term in terms]), 'ment')]
    unnamed x2 -> x1, waiting for transfers between devices: 142 us -> 0.02 us
    reshape x9 -> x3, local copies, waits for them, and re-layouts: 46.2 us -> 21.5 us  [the longest x2 15.4 us: on_device(): sums.append(summed_all[at:at + term.size].reshape(term.shape))]
    concatenate x0 -> x1, other arithmetic: none -> 17.4 us  [on_device(): jnp.concatenate([term.reshape(-1) for term in terms])]
    slice x5 -> x8, local copies, waits for them, and re-layouts: 2.8 us -> 9.6 us  [on_device(): sums.append(summed_all[at:at + term.size].reshape(term.shape))]
    unnamed x67 -> x55, local copies, waits for them, and re-layouts: 24.6 us -> 20.5 us
where the time goes in v3:
time: 465 us; the launch traced here: 459 us
  waiting for transfers between devices  142 us (31%)
  local copies, waits for them, and re-layouts  108 us (23%)
  Pallas kernels  85.1 us (18%)
  other arithmetic  65.6 us (14%)
  matrix products  43.5 us (9%)
  between operations  14.8 us (3%)
    psum x1, waiting for transfers between devices, on_device(): lax.psum(jnp.concatenate([term.reshape(-1) for term in terms]), 'ment')  142 us
    pallas_call x1, Pallas kernels, peer_scatter(): pl.pallas_call(functools.partial(_peer_scatter_kernel, n), out_shape=jax....  52 us
    pallas_call x3, Pallas kernels, peer_sum(): pl.pallas_call(functools.partial(_peer_sum_kernel, n), out_shape=jax.Shap...  33.1 us
    unnamed x55, local copies, waits for them, and re-layouts  20.5 us
    dot_general x9, matrix products, contract(): lax.dot_general(left, right, (((left_dim,), (right_dim,)), ((), ())), pre...  19.5 us
    concatenate x1, other arithmetic, on_device(): jnp.concatenate([term.reshape(-1) for term in terms])  17.4 us
    reshape x2, local copies, waits for them, and re-layouts, on_device(): sums.append(summed_all[at:at + term.size].reshape(term.shape))  15.4 us
    scatter-add x1, other arithmetic, on_device(): table_term = neg_term.at[row_slot, safe_block].add(gold_terms, mode='drop')  11.1 us
  transfers between devices with their start and end apart: 1, of which 1 were waited for; matrix products, arithmetic and copies ran while one was open for 5% of the time, Pallas kernels for 11%

profile of v3, /device:TPU:1, one launch (start us, length us, event | category | flops | bytes accessed | tf_op | source)
XLA Modules:
  0.0 459.1 jit_solution(1114803671565002059)
XLA Ops:
  7.2 1.4 slice.80
  8.7 2.3 fusion.59
  11.0 1.2 convolution_convert_fusion.4
  12.9 4.5 convolution_convert_fusion
  17.4 3.9 reshape.187
  21.4 4.8 %slice_bitcast_fusion = (bf16[64,32,4,64]{3,2,1,0:T(4,128)(2,1)}, bf16[64,32,4,64]{3,2,1,0:T(4,128)(2,1)S(1)}) fusion(bf16[64,32,2,4,64]{4,3,2,1,0:T(4,128)(2,1)} %reshape.187), kind=kLoop, calls=%fused_computation.9 | loop fusion | bytes 4194304 | tf_op jit(solution)/shard_map/squeeze | solution.py:169
  26.2 1.3 copy-done.10
  27.5 1.2 fusion.6
  29.2 6.0 %fusion.13 = f32[64,4,32]{1,2,0:T(8,128)S(1)} fusion(f32[64,4,1,32]{1,3,0,2:T(8,128)S(1)} %copy.43, f32[64,32]{1,0:T(8,128)S(1)} %fusion.31), kind=kOutput, calls=%fused_computation.34 | output fusion | flops 41247 | bytes 73728 | tf_op jit(solution)/shard_map/div | solution.py:177
  35.2 1.0 copy-done.4
  36.5 0.8 copy.44
  37.3 2.3 fusion.2
  39.8 3.5 gather_fusion
  44.4 17.5 %shard_map.137 = f32[128,1024]{1,0:T(8,128)} custom-call(bf16[128,1024]{1,0:T(8,128)(2,1)} %pad_maximum_fusion.2.x_ref), custom_call_target="tpu_custom_call" | custom-call | tf_op jit(solution)/shard_map/pallas_call | solution.py:62
  61.9 1.1 fusion.58
  63.6 1.1 exponential_reduce_fusion
  64.7 4.6 multiply_reduce_fusion
  69.9 6.7 %shard_map.138 = f32[8,64]{1,0:T(8,128)} custom-call(f32[8,64]{1,0:T(8,128)} %pad.6.x_ref), custom_call_target="tpu_custom_call" | custom-call | tf_op jit(solution)/shard_map/pallas_call | solution.py:62
  77.3 1.2 multiply_convert_fusion
  78.5 3.7 convolution_convert_fusion.1.x_ref
  82.2 8.9 %shard_map.139 = f32[64,1024]{1,0:T(8,128)} custom-call(bf16[64,1024]{1,0:T(8,128)(2,1)} %convolution_convert_fusion.1.x_ref), custom_call_target="tpu_custom_call" | custom-call | tf_op jit(solution)/shard_map/pallas_call | solution.py:62
  91.1 1.3 multiply_reduce_fusion.1
  92.5 0.8 subtract_multiply_fusion
  93.8 0.9 reshape.184
  95.3 0.9 fusion.37
  96.3 2.1 convolution_bitcast_fusion.1
  98.3 2.8 fusion
  101.1 1.5 copy.48
  102.6 2.4 fusion.9
  105.1 2.5 multiply_bitcast_fusion
  107.6 3.0 multiply_bitcast_fusion.1
  110.6 5.4 %maximum_convert_fusion = bf16[64,32,2,4,64]{4,3,2,1,0:T(4,128)(2,1)} fusion(bf16[64,32,1,4,64]{4,3,2,1,0:T(4,128)(2,1)S(1)} %multiply_bitcast_fusion, bf16[64,32,1,4,64]{4,3,2,1,0:T(4,128)(2,1)S(1)} %multiply_bitcast_fusion.1), kind=kLoop, calls=%fused_computation.3 | loop fusion | flops 1048576 | bytes 4194304 | tf_op jit(solution)/shard_map/convert_element_type | solution.py:247
  116.0 7.6 %convert_element_type.105 = bf16[64,32,512]{2,1,0:T(8,128)(2,1)} reshape(bf16[64,32,2,4,64]{4,3,2,1,0:T(4,128)(2,1)} %maximum_convert_fusion) | data formatting | bytes 4194304 | tf_op jit(solution)/shard_map/convert_element_type | solution.py:247
  123.7 0.8 copy.49
  124.5 2.3 fusion.4
  126.9 4.5 convolution_bitcast_fusion
  131.4 9.0 %copy.37 = f32[256,8,1024]{2,1,0:T(8,128)} copy(f32[256,8,1024]{0,2,1:T(8,128)} %convolution_bitcast_fusion) | data formatting | bytes 16777216 | tf_op jit(solution)/shard_map/mbr,md->rbd/transpose | solution.py:270
  140.4 11.1 %scatter_fusion = f32[256,8,1024]{2,1,0:T(8,128)} fusion(f32[256,8,1024]{2,1,0:T(8,128)} %copy.37, s32[64]{0:T(128)S(1)} %fusion.36, f32[64,1024]{1,0:T(8,128)S(1)} %fusion.37), kind=kCustom, calls=%fused_computation.1 | custom fusion | flops 65536 | bytes 786944 | tf_op jit(solution)/shard_map/scatter-add | solution.py:273
  151.5 8.9 %copy.56 = f32[256,8,8,128]{3,1,2,0:T(8,128)} copy(f32[256,8,8,128]{3,2,1,0:T(8,128)} %bitcast.150) | data formatting | bytes 16777216
  160.4 1.2 copy.55
  161.7 3.8 fusion.61
  165.4 2.8 copy.35
  168.3 1.4 convolution_bitcast_fusion.2
  169.7 3.6 copy.34
  173.3 5.1 %pad_maximum_fusion.1 = f32[1024,3,256]{2,1,0:T(4,128)} fusion(f32[1024,2,256]{2,1,0:T(2,128)S(1)} %copy.35, f32[1024,1,256]{2,1,0:T(1,128)} %copy.34), kind=kLoop, calls=%fused_computation.4 | loop fusion | flops 786432 | bytes 6291456 | tf_op jit(solution)/shard_map/concatenate | solution.py:253
  178.4 6.1 %reshape.193 = f32[786432]{0:T(1024)} reshape(f32[1024,3,256]{2,1,0:T(4,128)} %pad_maximum_fusion.1) | data formatting | bytes 6291456 | tf_op jit(solution)/shard_map/reshape | solution.py:280
  184.5 17.4 %pad_maximum_fusion = f32[3147776]{0:T(1024)} fusion(f32[2048]{0:T(1024)S(1)} %bitcast.164, f32[2097152]{0:T(1024)} %bitcast.151, f32[262144]{0:T(1024)S(1)} %bitcast.156, f32[786432]{0:T(1024)} %reshape.193), kind=kLoop, calls=%fused_computation.2 | loop fusion | flops 9443328 | bytes 25182208 | tf_op jit(solution)/shard_map/concatenate | solution.py:280
  201.9 1.2 copy-done.3
  203.1 1.1 copy.33
  204.2 0.9 reshape.221
  205.1 1.3 fusion.15
  206.4 4.1 fusion.60
  210.5 3.2 copy-done.2
  214.1 6.2 %scatter-add.12 = f32[64,32,1024]{2,1,0:T(8,128)} dynamic-update-slice(f32[64,32,1024]{2,1,0:T(8,128)} %copy-done.2, f32[64,1,1024]{2,1,0:T(1,128)S(1)} %slice_add_fusion, s32[]{:T(128)} %constant.60.clone.1, s32[]{:T(128)} %constant.60.clone.1, s32[]{:T(128)} %constant.60.clone.1) | dynamic-update-slice | bytes 524292 | tf_op jit(solution)/shard_map/scatter-add | solution.py:263
  220.3 6.3 %convert_element_type.108.y_ref = bf16[64,32,1024]{2,1,0:T(8,128)(2,1)} convert(f32[64,32,1024]{2,1,0:T(8,128)} %scatter-add.12) | non-fusion elementwise | flops 2097152 | bytes 12582912 | tf_op jit(solution)/shard_map/convert_element_type | solution.py:263
  227.2 52.0 %shard_map.140 = bf16[16,32,1024]{2,1,0:T(8,128)(2,1)} custom-call(bf16[64,32,1024]{2,1,0:T(8,128)(2,1)} %convert_element_type.108.y_ref, f32[16,1024]{1,0:T(8,128)} %constant_dynamic-slice_fusion.3.resid_ref), custom_call_target="tpu_custom_call" | custom-call | tf_op jit(solution)/shard_map/pallas_call | solution.py:126
  279.2 142.3 %all-reduce.3.cloned.1.call-done = f32[3147776]{0:T(1024)} async-done(((f32[3147776]{0:T(1024)}), f32[3147776]{0:T(1024)}) %all-reduce.3.cloned.1.call-update) | async-done | bytes 12591120 | tf_op jit(solution)/shard_map/psum | solution.py:280
  421.5 3.8 slice.103
  425.2 6.0 %reshape.198 = f32[1024,3,256]{2,1,0:T(4,128)} reshape(f32[786432]{0:T(1024)} %slice.103) | data formatting | bytes 6291456 | tf_op jit(solution)/shard_map/reshape | solution.py:283
  431.2 0.9 constant_dynamic-slice_fusion.2
  434.3 5.7 %slice.106 = f32[2097152]{0:T(1024)} slice(f32[3147776]{0:T(1024)} %all-reduce.3.cloned.1.call-done), slice={[1048576:3145728]} | slice | bytes 16777216 | tf_op jit(solution)/shard_map/slice | solution.py:283
  440.0 9.4 %reshape.199 = f32[256,8,1024]{2,1,0:T(8,128)} reshape(f32[2097152]{0:T(1024)} %slice.106) | data formatting | bytes 16777216 | tf_op jit(solution)/shard_map/reshape | solution.py:283
  449.4 0.9 dynamic-slice_bitcast_fusion
  451.1 1.0 copy.82
  (92 shorter events, 9.8 us)
Async XLA Ops:
  7.2 36.2 %copy-start = (bf16[256,1024]{1,0:T(8,128)(2,1)S(1)}, bf16[256,1024]{1,0:T(8,128)(2,1)}, u32[]{:S(2)}) copy-start(bf16[256,1024]{1,0:T(8,128)(2,1)} %param.14) | copy-start | bytes 1572868
  7.2 414.3 %all-reduce.3.cloned.1.call-start = ((), (), s32[]{:S(2)}) async-start(), calls=%async_computation | async-start | bytes 25182208 | tf_op jit(solution)/shard_map/psum | solution.py:280
  12.3 0.6 copy-start.13
  21.4 7.8 %copy-start.21 = (s32[64]{0:T(128)S(1)}, s32[64]{0:T(128)}, u32[]{:S(2)}) copy-start(s32[64]{0:T(128)} %param.18) | copy-start | bytes 772
  26.2 1.3 copy-start.10
  29.2 7.3 %copy-start.20 = (s32[64]{0:T(128)S(1)}, s32[64]{0:T(128)}, u32[]{:S(2)}) copy-start(s32[64]{0:T(128)} %param.19) | copy-start | bytes 772
  29.2 7.3 %copy-start.19 = (s32[64]{0:T(128)S(1)}, s32[64]{0:T(128)}, u32[]{:S(2)}) copy-start(s32[64]{0:T(128)} %param.20) | copy-start | bytes 772
  35.2 1.0 copy-start.4
  36.4 26.8 %copy-start.22 = (s32[1,4]{1,0:T(1,128)S(1)}, s32[1,4]{1,0:T(1,128)}, u32[]{:S(2)}) copy-start(s32[1,4]{1,0:T(1,128)} %param.21) | copy-start | bytes 52
  36.4 27.0 %copy-start.14 = (f32[1024]{0:T(1024)S(1)}, f32[1024]{0:T(1024)}, u32[]{:S(2)}) copy-start(f32[1024]{0:T(1024)} %param.15) | copy-start | bytes 12292
  36.4 27.0 %copy-start.18 = (f32[1024]{0:T(1024)S(1)}, f32[1024]{0:T(1024)}, u32[]{:S(2)}) copy-start(f32[1024]{0:T(1024)} %param.16) | copy-start | bytes 12292
  39.8 29.5 %copy-start.12 = (bf16[64,256]{1,0:T(8,128)(2,1)}, bf16[64,256]{1,0:T(8,128)(2,1)S(1)}, u32[]{:S(2)}) copy-start(bf16[64,256]{1,0:T(8,128)(2,1)S(1)} %convert_element_type.92) | copy-start | bytes 98308
  63.2 27.8 %copy-start.16 = (f32[64]{0:T(128)}, f32[64]{0:T(128)S(1)}, u32[]{:S(2)}) copy-start(f32[64]{0:T(128)S(1)} %add_rsqrt_fusion) | copy-start | bytes 772
  64.7 26.4 %copy-start.11 = (f32[64,64]{0,1:T(8,128)}, f32[64,64]{0,1:T(8,128)S(1)}, u32[]{:S(2)}) copy-start(f32[64,64]{0,1:T(8,128)S(1)} %get-tuple-element.40) | copy-start | bytes 49156
  64.7 26.4 %copy-start.8 = (f32[128,1024]{1,0:T(8,128)S(1)}, f32[128,1024]{1,0:T(8,128)}, u32[]{:S(2)}) copy-start(f32[128,1024]{1,0:T(8,128)} %shard_map.137) | copy-start | bytes 1572868
  77.3 15.2 %copy-start.17 = (f32[64]{0:T(128)}, f32[64]{0:T(128)S(1)}, u32[]{:S(2)}) copy-start(f32[64]{0:T(128)S(1)} %fusion.35) | copy-start | bytes 772
  151.5 8.9 %copy-start.5 = (f32[32,8,8,128]{3,2,1,0:T(8,128)S(1)}, f32[32,8,8,128]{3,2,1,0:T(8,128)}, u32[]{:S(2)}) copy-start(f32[32,8,8,128]{3,2,1,0:T(8,128)} %convolution_bitcast_fusion.1) | copy-start | bytes 3145732
  151.5 10.2 %copy-start.9 = (bf16[64,32,512]{2,1,0:T(8,128)(2,1)S(1)}, bf16[64,32,512]{2,1,0:T(8,128)(2,1)}, u32[]{:S(2)}) copy-start(bf16[64,32,512]{2,1,0:T(8,128)(2,1)} %convert_element_type.105) | copy-start | bytes 6291460
  151.5 10.2 %copy-start.15 = (bf16[64,32,1024]{2,1,0:T(8,128)(2,1)S(1)}, bf16[64,32,1024]{2,1,0:T(8,128)(2,1)}, u32[]{:S(2)}) copy-start(bf16[64,32,1024]{2,1,0:T(8,128)(2,1)} %param.12) | copy-start | bytes 12582916
  178.4 6.1 %copy-start.7 = (f32[32,8,8,128]{3,1,2,0:T(8,128)S(1)}, f32[32,8,8,128]{3,1,2,0:T(8,128)}, u32[]{:S(2)}) copy-start(f32[32,8,8,128]{3,1,2,0:T(8,128)} %copy.55) | copy-start | bytes 3145732
  201.9 1.2 copy-start.3
  210.5 3.2 copy-start.2
  425.2 7.5 %slice-start = ((f32[3147776]{0:T(1024)}), f32[262144]{0:T(1024)S(1)}, s32[]{:S(2)}) async-start(f32[3147776]{0:T(1024)} %all-reduce.3.cloned.1.call-done), calls=%async_computation.1 | async-start | bytes 2097152 | tf_op jit(solution)/shard_map/slice | solution.py:283
  431.2 2.5 slice-start.1
  440.0 11.1 %copy-start.6 = (bf16[16,32,1024]{2,1,0:T(8,128)(2,1)S(1)}, bf16[16,32,1024]{2,1,0:T(8,128)(2,1)}, u32[]{:S(2)}) copy-start(bf16[16,32,1024]{2,1,0:T(8,128)(2,1)} %shard_map.140) | copy-start | bytes 3145732
  440.0 12.0 %copy-start.1 = (bf16[256,1024]{1,0:T(8,128)(2,1)S(1)}, bf16[256,1024]{1,0:T(8,128)(2,1)}, u32[]{:S(2)}) copy-start(bf16[256,1024]{1,0:T(8,128)(2,1)} %param.14) | copy-start | bytes 1572868
Sparse Core Ops, SparseCore 0:
  202.0 219.4 all-reduce.2

commit v4 on v3

--- a/solution.py
+++ b/solution.py
@@ -272,23 +272,33 @@
     row_slot = jnp.where(inside, gold_row, count)
     table_term = neg_term.at[row_slot, safe_block].add(gold_terms, mode="drop")
     parts = lax.axis_size("ment")
-    place = lax.axis_index("ment")
     qkv_rows = width // parts
     wo_cols = width // parts
     tab_rows = block_rows // parts
-    terms = (qkv_term, wo_term, table_term, ln_terms)
-    summed_all = lax.psum(jnp.concatenate([term.reshape(-1) for term in terms]), "ment")
+    pieces = [
+        table_term.reshape(parts, -1),
+        qkv_term.reshape(parts, -1),
+        wo_term.T.reshape(parts, -1),
+        ln_terms.T.reshape(parts, -1),
+    ]
+    sizes = [piece.shape[1] for piece in pieces]
+    slab = own_blocks * width
+    pieces.append(jnp.zeros((parts, -sum(sizes) % slab), jnp.float32))
+    merged = lax.psum_scatter(
+        jnp.concatenate(pieces, axis=1).reshape(-1, own_blocks, width),
+        "ment",
+        scatter_dimension=0,
+        tiled=True,
+    )
+    merged = lax.optimization_barrier(merged).reshape(-1)
     sums, at = [], 0
-    for term in terms:
-        sums.append(summed_all[at : at + term.size].reshape(term.shape))
-        at += term.size
-    qkv_sum, wo_sum, table_sum, ln_sum = sums
-    grad_qkv = lax.dynamic_slice_in_dim(qkv_sum, place * qkv_rows, qkv_rows, 0)
-    grad_wo = lax.dynamic_slice_in_dim(wo_sum, place * wo_cols, wo_cols, 1)
-    grad_ln = lax.dynamic_slice_in_dim(ln_sum, place * wo_cols, wo_cols, 1)
-    grad_table = jnp.transpose(
-        lax.dynamic_slice_in_dim(table_sum, place * tab_rows, tab_rows, 0), (1, 0, 2)
-    )
+    for size in sizes:
+        sums.append(merged[at : at + size])
+        at += size
+    grad_table = sums[0].reshape(tab_rows, own_blocks, width).transpose(1, 0, 2)
+    grad_qkv = sums[1].reshape(qkv_rows, 3, local_cols)
+    grad_wo = sums[2].reshape(wo_cols, local_cols).T
+    grad_ln = sums[3].reshape(wo_cols, 2).T
     return (grad_hidden, grad_qkv, grad_wo, grad_ln, grad_table)
 
 

time: 465 us -> 425 us (0.914)
  waiting for transfers between devices: 142 us -> 90.1 us
  local copies, waits for them, and re-layouts: 108 us -> 137 us
  other arithmetic: 65.6 us -> 47.5 us
    psum x1 -> x0, waiting for transfers between devices: 142 us -> none  [on_device(): lax.psum(jnp.concatenate([term.reshape(-1) for term in terms]), 'ment')]
    unnamed x1 -> x2, waiting for transfers between devices: 0.02 us -> 90.1 us
    concatenate x1 -> x0, other arithmetic: 17.4 us -> none  [on_device(): jnp.concatenate([term.reshape(-1) for term in terms])]
    concatenate x0 -> x1, local copies, waits for them, and re-layouts: none -> 10.8 us  [on_device(): jnp.concatenate(pieces, axis=1).reshape(-1, own_blocks, width)]
    slice x8 -> x3, local copies, waits for them, and re-layouts: 9.6 us -> 17.9 us  [on_device(): sums.append(merged[at:at + size])]
    reshape x3 -> x6, local copies, waits for them, and re-layouts: 21.5 us -> 28.6 us  [the longest x1 13.2 us: on_device(): jnp.concatenate(pieces, axis=1).reshape(-1, own_blocks, width)]
    unnamed x55 -> x61, local copies, waits for them, and re-layouts: 20.5 us -> 24 us
  transfers between devices with their start and end apart: 1 -> 1, of which waited for: 1 -> 1; matrix products, arithmetic and copies ran while one was open for 5% -> 5% of each run, Pallas kernels for 11% -> 12%
where the time goes in v4:
time: 425 us; the launch traced here: 417 us
  local copies, waits for them, and re-layouts  137 us (32%)
  waiting for transfers between devices  90.1 us (21%)
  Pallas kernels  84.2 us (20%)
  other arithmetic  47.5 us (11%)
  matrix products  43.4 us (10%)
  between operations  14.9 us (4%)
    unnamed x2, waiting for transfers between devices  90.1 us
    pallas_call x1, Pallas kernels, peer_scatter(): pl.pallas_call(functools.partial(_peer_scatter_kernel, n), out_shape=jax....  51 us
    pallas_call x3, Pallas kernels, peer_sum(): pl.pallas_call(functools.partial(_peer_sum_kernel, n), out_shape=jax.Shap...  33.1 us
    unnamed x61, local copies, waits for them, and re-layouts  24 us
    dot_general x9, matrix products, contract(): lax.dot_general(left, right, (((left_dim,), (right_dim,)), ((), ())), pre...  19.4 us
    slice x3, local copies, waits for them, and re-layouts, on_device(): sums.append(merged[at:at + size])  17.9 us
    reshape x1, local copies, waits for them, and re-layouts, on_device(): jnp.concatenate(pieces, axis=1).reshape(-1, own_blocks, width)  13.2 us
    concatenate x1, local copies, waits for them, and re-layouts, on_device(): jnp.concatenate(pieces, axis=1).reshape(-1, own_blocks, width)  10.8 us
  transfers between devices with their start and end apart: 1, of which 1 were waited for; matrix products, arithmetic and copies ran while one was open for 5% of the time, Pallas kernels for 12%

profile of v4, /device:TPU:1, one launch (start us, length us, event | category | flops | bytes accessed | tf_op | source)
XLA Modules:
  0.0 416.6 jit_solution(4441351460060815954)
XLA Ops:
  7.2 1.4 slice.67
  8.7 2.3 fusion.60
  11.0 1.2 convolution_convert_fusion.4
  12.9 4.5 %convolution_convert_fusion = bf16[2048,512]{1,0:T(8,128)(2,1)S(1)} fusion(bf16[2048,1024]{1,0:T(8,128)(2,1)} %bitcast.164, bf16[1024,512]{1,0:T(8,128)(2,1)S(1)} %bitcast.156), kind=kOutput, calls=%fused_computation.7 | convolution fusion | flops 2148532224 | bytes 7340032 | tf_op jit(solution)/shard_map/dot_general | solution.py:164
  17.4 4.1 reshape.181
  21.5 4.8 %slice_bitcast_fusion = (bf16[64,32,4,64]{3,2,1,0:T(4,128)(2,1)}, bf16[64,32,4,64]{3,2,1,0:T(4,128)(2,1)S(1)}) fusion(bf16[64,32,2,4,64]{4,3,2,1,0:T(4,128)(2,1)} %reshape.181), kind=kLoop, calls=%fused_computation.8 | loop fusion | bytes 4194304 | tf_op jit(solution)/shard_map/squeeze | solution.py:169
  26.3 1.3 copy-done.10
  27.7 1.2 fusion.6
  29.4 6.0 %fusion.13 = f32[64,4,32]{1,2,0:T(8,128)S(1)} fusion(f32[64,4,1,32]{1,3,0,2:T(8,128)S(1)} %copy.55, f32[64,32]{1,0:T(8,128)S(1)} %fusion.32), kind=kOutput, calls=%fused_computation.32 | output fusion | flops 41247 | bytes 73728 | tf_op jit(solution)/shard_map/div | solution.py:177
  35.4 1.0 copy-done.4
  36.7 0.8 copy.56
  37.5 2.3 fusion.2
  39.9 3.5 gather_fusion
  44.5 17.5 %shard_map.137 = f32[128,1024]{1,0:T(8,128)} custom-call(bf16[128,1024]{1,0:T(8,128)(2,1)} %pad_maximum_fusion.1.x_ref), custom_call_target="tpu_custom_call" | custom-call | tf_op jit(solution)/shard_map/pallas_call | solution.py:62
  62.1 1.1 fusion.59
  63.7 1.1 exponential_reduce_fusion
  64.9 4.6 %multiply_reduce_fusion = (f32[64]{0:T(128)S(1)}, f32[64,2048]{1,0:T(8,128)}) fusion(f32[2048]{0:T(1024)S(1)} %bitcast.160, bf16[64,1024]{1,0:T(8,128)(2,1)S(1)} %add_convert_fusion, bf16[2048,1024]{1,0:T(8,128)(2,1)} %bitcast.150), kind=kOutput, calls=%fused_computation.38 | convolution fusion | flops 268697536 | bytes 4858112 | tf_op jit(solution)/shard_map/dot_general | solution.py:145
  70.1 6.7 %shard_map.138 = f32[8,64]{1,0:T(8,128)} custom-call(f32[8,64]{1,0:T(8,128)} %pad.6.x_ref), custom_call_target="tpu_custom_call" | custom-call | tf_op jit(solution)/shard_map/pallas_call | solution.py:62
  77.5 1.2 multiply_convert_fusion
  78.7 3.7 convolution_convert_fusion.1.x_ref
  82.4 8.9 %shard_map.139 = f32[64,1024]{1,0:T(8,128)} custom-call(bf16[64,1024]{1,0:T(8,128)(2,1)} %convolution_convert_fusion.1.x_ref), custom_call_target="tpu_custom_call" | custom-call | tf_op jit(solution)/shard_map/pallas_call | solution.py:62
  91.3 1.3 multiply_reduce_fusion.1
  92.6 0.8 subtract_multiply_fusion
  93.9 0.9 reshape.178
  95.5 0.9 fusion.38
  96.4 2.1 fusion.28
  98.5 2.8 fusion
  101.3 1.5 copy.60
  102.8 2.4 fusion.9
  105.3 2.5 multiply_bitcast_fusion
  107.8 2.7 multiply_bitcast_fusion.1
  110.4 5.4 %maximum_convert_fusion = bf16[64,32,2,4,64]{4,3,2,1,0:T(4,128)(2,1)} fusion(bf16[64,32,1,4,64]{4,3,2,1,0:T(4,128)(2,1)S(1)} %multiply_bitcast_fusion, bf16[64,32,1,4,64]{4,3,2,1,0:T(4,128)(2,1)S(1)} %multiply_bitcast_fusion.1), kind=kLoop, calls=%fused_computation.2 | loop fusion | flops 1048576 | bytes 4194304 | tf_op jit(solution)/shard_map/convert_element_type | solution.py:247
  115.9 7.6 %convert_element_type.105 = bf16[64,32,512]{2,1,0:T(8,128)(2,1)} reshape(bf16[64,32,2,4,64]{4,3,2,1,0:T(4,128)(2,1)} %maximum_convert_fusion) | data formatting | bytes 4194304 | tf_op jit(solution)/shard_map/convert_element_type | solution.py:247
  123.5 0.8 copy.61
  124.3 2.3 fusion.4
  126.7 4.5 %convolution_bitcast_fusion = f32[256,8,1024]{0,2,1:T(8,128)} fusion(bf16[8,8,8,256]{3,2,1,0:T(8,128)(2,1)S(1)} %bitcast.154, bf16[64,1024]{1,0:T(8,128)(2,1)S(1)} %add_convert_fusion), kind=kOutput, calls=%fused_computation.6 | convolution fusion | flops 268435456 | bytes 8781824 | tf_op jit(solution)/shard_map/mbr,md->rbd/dot_general | solution.py:270
  131.2 9.0 %copy.46 = f32[256,8,1024]{2,1,0:T(8,128)} copy(f32[256,8,1024]{0,2,1:T(8,128)} %convolution_bitcast_fusion) | data formatting | bytes 16777216 | tf_op jit(solution)/shard_map/mbr,md->rbd/transpose | solution.py:270
  140.2 10.5 %scatter_fusion = f32[256,8,1024]{2,1,0:T(8,128)} fusion(f32[256,8,1024]{2,1,0:T(8,128)} %copy.46, s32[64]{0:T(128)S(1)} %fusion.37, f32[64,1024]{1,0:T(8,128)S(1)} %fusion.38), kind=kCustom, calls=%fused_computation.1 | custom fusion | flops 65536 | bytes 786944 | tf_op jit(solution)/shard_map/scatter-add | solution.py:273
  150.7 9.4 %reshape.187 = f32[64,32768]{1,0:T(8,128)} reshape(f32[256,8,1024]{2,1,0:T(8,128)} %scatter_fusion) | data formatting | bytes 16777216 | tf_op jit(solution)/shard_map/reshape | solution.py:279
  160.1 7.4 %constant_dynamic-update-slice_fusion.2 = f32[64,57344]{1,0:T(8,128)} fusion(f32[64,32768]{1,0:T(8,128)} %reshape.187), kind=kLoop, calls=%fused_computation.78 | loop fusion | bytes 16777216
  167.5 3.7 fusion.62
  171.2 2.8 copy.48
  174.1 1.3 convolution_bitcast_fusion.1
  175.4 3.8 copy.47
  179.2 5.1 %pad_maximum_fusion = f32[1024,3,256]{2,1,0:T(4,128)} fusion(f32[1024,2,256]{2,1,0:T(2,128)S(1)} %copy.48, f32[1024,1,256]{2,1,0:T(1,128)} %copy.47), kind=kLoop, calls=%fused_computation.3 | loop fusion | flops 786432 | bytes 6291456 | tf_op jit(solution)/shard_map/concatenate | solution.py:253
  184.3 5.5 %reshape.189 = f32[64,12288]{1,0:T(8,128)} reshape(f32[1024,3,256]{2,1,0:T(4,128)} %pad_maximum_fusion) | data formatting | bytes 6291456 | tf_op jit(solution)/shard_map/reshape | solution.py:280
  190.5 3.8 constant_dynamic-update-slice_fusion.1
  194.3 1.1 constant_dynamic-update-slice_fusion
  195.4 1.4 dynamic-update-slice.6
  196.9 10.8 %dynamic-update-slice.7 = f32[64,57344]{1,0:T(8,128)} dynamic-update-slice(f32[64,57344]{1,0:T(8,128)} %dynamic-update-slice.6, f32[64,8160]{1,0:T(8,128)S(1)} %broadcast_in_dim.55, s32[]{} %constant.88, s32[]{} %constant.92) | dynamic-update-slice | bytes 4177924 | tf_op jit(solution)/shard_map/concatenate | solution.py:288
  207.7 13.2 %reshape.192 = f32[448,8,1024]{2,1,0:T(8,128)} reshape(f32[64,57344]{1,0:T(8,128)} %dynamic-update-slice.7) | data formatting | bytes 29360128 | tf_op jit(solution)/shard_map/reshape | solution.py:288
  220.9 1.2 copy-done.3
  222.1 1.1 copy.44
  223.9 1.3 fusion.15
  225.3 4.1 fusion.61
  229.4 3.2 copy-done.2
  232.9 6.1 %scatter-add.12 = f32[64,32,1024]{2,1,0:T(8,128)} dynamic-update-slice(f32[64,32,1024]{2,1,0:T(8,128)} %copy-done.2, f32[64,1,1024]{2,1,0:T(1,128)S(1)} %slice_add_fusion, s32[]{:T(128)} %constant.56.clone.1, s32[]{:T(128)} %constant.56.clone.1, s32[]{:T(128)} %constant.56.clone.1) | dynamic-update-slice | bytes 524292 | tf_op jit(solution)/shard_map/scatter-add | solution.py:263
  239.0 6.4 %convert_element_type.108.y_ref = bf16[64,32,1024]{2,1,0:T(8,128)(2,1)} convert(f32[64,32,1024]{2,1,0:T(8,128)} %scatter-add.12) | non-fusion elementwise | flops 2097152 | bytes 12582912 | tf_op jit(solution)/shard_map/convert_element_type | solution.py:263
  246.1 51.0 %shard_map.140 = bf16[16,32,1024]{2,1,0:T(8,128)(2,1)} custom-call(bf16[64,32,1024]{2,1,0:T(8,128)(2,1)} %convert_element_type.108.y_ref, f32[16,1024]{1,0:T(8,128)} %constant_dynamic-slice_fusion.resid_ref), custom_call_target="tpu_custom_call" | custom-call | tf_op jit(solution)/shard_map/pallas_call | solution.py:126
  297.1 90.0 %reduce-scatter.4.cloned.1.call-done = f32[7,8,1024]{2,1,0:T(8,128)} async-done(((f32[448,8,1024]{2,1,0:T(8,128)}), f32[7,8,1024]{2,1,0:T(8,128)}) %reduce-scatter.4.cloned.1.call-update) | async-done | bytes 229392
  387.2 1.0 slice.77
  388.2 16.9 %slice.79 = f32[28672,2]{1,0:T(8,128)} reshape(f32[7,8,1024]{2,1,0:T(8,128)} %reduce-scatter.4.cloned.1.call-done) | data formatting | bytes 458752 | tf_op jit(solution)/shard_map/slice | solution.py:296
  407.8 0.7 copy.52
  408.5 1.0 copy.93
  (97 shorter events, 11.0 us)
Async XLA Ops:
  7.2 36.4 %copy-start = (bf16[256,1024]{1,0:T(8,128)(2,1)S(1)}, bf16[256,1024]{1,0:T(8,128)(2,1)}, u32[]{:S(2)}) copy-start(bf16[256,1024]{1,0:T(8,128)(2,1)} %param.14) | copy-start | bytes 1572868
  7.2 380.0 %reduce-scatter.4.cloned.1.call-start = ((), (), s32[]{:S(2)}) async-start(), calls=%async_computation.1 | async-start | bytes 14909440
  12.3 0.6 copy-start.15
  21.5 7.8 %copy-start.23 = (s32[64]{0:T(128)S(1)}, s32[64]{0:T(128)}, u32[]{:S(2)}) copy-start(s32[64]{0:T(128)} %param.18) | copy-start | bytes 772
  26.3 1.3 copy-start.10
  29.3 7.3 %copy-start.22 = (s32[64]{0:T(128)S(1)}, s32[64]{0:T(128)}, u32[]{:S(2)}) copy-start(s32[64]{0:T(128)} %param.19) | copy-start | bytes 772
  29.3 7.3 %copy-start.21 = (s32[64]{0:T(128)S(1)}, s32[64]{0:T(128)}, u32[]{:S(2)}) copy-start(s32[64]{0:T(128)} %param.20) | copy-start | bytes 772
  35.4 1.0 copy-start.4
  36.6 26.8 %copy-start.24 = (s32[1,4]{1,0:T(1,128)S(1)}, s32[1,4]{1,0:T(1,128)}, u32[]{:S(2)}) copy-start(s32[1,4]{1,0:T(1,128)} %param.21) | copy-start | bytes 52
  36.6 27.0 %copy-start.16 = (f32[1024]{0:T(1024)S(1)}, f32[1024]{0:T(1024)}, u32[]{:S(2)}) copy-start(f32[1024]{0:T(1024)} %param.15) | copy-start | bytes 12292
  36.6 27.0 %copy-start.20 = (f32[1024]{0:T(1024)S(1)}, f32[1024]{0:T(1024)}, u32[]{:S(2)}) copy-start(f32[1024]{0:T(1024)} %param.16) | copy-start | bytes 12292
  39.9 29.5 %copy-start.14 = (bf16[64,256]{1,0:T(8,128)(2,1)}, bf16[64,256]{1,0:T(8,128)(2,1)S(1)}, u32[]{:S(2)}) copy-start(bf16[64,256]{1,0:T(8,128)(2,1)S(1)} %convert_element_type.92) | copy-start | bytes 98308
  63.4 27.8 %copy-start.18 = (f32[64]{0:T(128)}, f32[64]{0:T(128)S(1)}, u32[]{:S(2)}) copy-start(f32[64]{0:T(128)S(1)} %add_rsqrt_fusion) | copy-start | bytes 772
  64.9 26.4 %copy-start.13 = (f32[64,64]{0,1:T(8,128)}, f32[64,64]{0,1:T(8,128)S(1)}, u32[]{:S(2)}) copy-start(f32[64,64]{0,1:T(8,128)S(1)} %get-tuple-element.45) | copy-start | bytes 49156
  64.9 26.4 %copy-start.7 = (f32[128,1024]{1,0:T(8,128)S(1)}, f32[128,1024]{1,0:T(8,128)}, u32[]{:S(2)}) copy-start(f32[128,1024]{1,0:T(8,128)} %shard_map.137) | copy-start | bytes 1572868
  77.5 15.2 %copy-start.19 = (f32[64]{0:T(128)}, f32[64]{0:T(128)S(1)}, u32[]{:S(2)}) copy-start(f32[64]{0:T(128)S(1)} %fusion.36) | copy-start | bytes 772
  126.7 47.3 %copy-start.11 = (bf16[64,256]{1,0:T(8,128)(2,1)}, bf16[64,256]{1,0:T(8,128)(2,1)S(1)}, u32[]{:S(2)}) copy-start(bf16[64,256]{1,0:T(8,128)(2,1)S(1)} %convert_element_type.107) | copy-start | bytes 98308
  160.1 7.4 %copy-start.9 = (bf16[64,32,512]{2,1,0:T(8,128)(2,1)S(1)}, bf16[64,32,512]{2,1,0:T(8,128)(2,1)}, u32[]{:S(2)}) copy-start(bf16[64,32,512]{2,1,0:T(8,128)(2,1)} %convert_element_type.105) | copy-start | bytes 6291460
  160.1 7.4 %copy-start.17 = (bf16[64,32,1024]{2,1,0:T(8,128)(2,1)S(1)}, bf16[64,32,1024]{2,1,0:T(8,128)(2,1)}, u32[]{:S(2)}) copy-start(bf16[64,32,1024]{2,1,0:T(8,128)(2,1)} %param.12) | copy-start | bytes 12582916
  184.3 5.5 %copy-start.5 = (f32[1024,256]{1,0:T(8,128)S(1)}, f32[1024,256]{1,0:T(8,128)}, u32[]{:S(2)}) copy-start(f32[1024,256]{1,0:T(8,128)} %fusion.28) | copy-start | bytes 3145732
  220.9 1.2 copy-start.3
  220.9 3.0 copy-start.12
  229.4 3.2 copy-start.2
  388.2 17.0 %copy-start.8 = (f32[7,8,1024]{2,1,0:T(8,128)S(1)}, f32[7,8,1024]{2,1,0:T(8,128)}, u32[]{:S(2)}) copy-start(f32[7,8,1024]{2,1,0:T(8,128)} %reduce-scatter.4.cloned.1.call-done) | copy-start | bytes 688132
  388.2 20.4 %copy-start.6 = (bf16[16,32,1024]{2,1,0:T(8,128)(2,1)S(1)}, bf16[16,32,1024]{2,1,0:T(8,128)(2,1)}, u32[]{:S(2)}) copy-start(bf16[16,32,1024]{2,1,0:T(8,128)(2,1)} %shard_map.140) | copy-start | bytes 3145732
  388.2 21.3 %copy-start.1 = (bf16[256,1024]{1,0:T(8,128)(2,1)S(1)}, bf16[256,1024]{1,0:T(8,128)(2,1)}, u32[]{:S(2)}) copy-start(bf16[256,1024]{1,0:T(8,128)(2,1)} %param.14) | copy-start | bytes 1572868
Sparse Core Ops, SparseCore 0:
  221.1 166.0 reduce-scatter.3

commit v5 on v4

--- a/solution.py
+++ b/solution.py
@@ -274,31 +274,31 @@
     parts = lax.axis_size("ment")
     qkv_rows = width // parts
     wo_cols = width // parts
-    tab_rows = block_rows // parts
-    pieces = [
-        table_term.reshape(parts, -1),
-        qkv_term.reshape(parts, -1),
-        wo_term.T.reshape(parts, -1),
-        ln_terms.T.reshape(parts, -1),
-    ]
-    sizes = [piece.shape[1] for piece in pieces]
     slab = own_blocks * width
-    pieces.append(jnp.zeros((parts, -sum(sizes) % slab), jnp.float32))
+    table_piece = table_term.reshape(parts, -1, own_blocks, width)
+    rows_piece = jnp.concatenate(
+        [qkv_term.reshape(width, 3 * local_cols), wo_term.T], axis=1
+    ).reshape(parts, -1, own_blocks, width)
+    ln_flat = ln_terms.T.reshape(parts, -1)
+    ln_piece = jnp.pad(ln_flat, ((0, 0), (0, -ln_flat.shape[1] % slab))).reshape(
+        parts, -1, own_blocks, width
+    )
+    pieces = [table_piece, rows_piece, ln_piece]
+    counts = [piece.shape[1] for piece in pieces]
     merged = lax.psum_scatter(
         jnp.concatenate(pieces, axis=1).reshape(-1, own_blocks, width),
         "ment",
         scatter_dimension=0,
         tiled=True,
     )
-    merged = lax.optimization_barrier(merged).reshape(-1)
-    sums, at = [], 0
-    for size in sizes:
-        sums.append(merged[at : at + size])
-        at += size
-    grad_table = sums[0].reshape(tab_rows, own_blocks, width).transpose(1, 0, 2)
-    grad_qkv = sums[1].reshape(qkv_rows, 3, local_cols)
-    grad_wo = sums[2].reshape(wo_cols, local_cols).T
-    grad_ln = sums[3].reshape(wo_cols, 2).T
+    merged = lax.optimization_barrier(merged)
+    table_sum = merged[: counts[0]]
+    rows_sum = merged[counts[0] : counts[0] + counts[1]].reshape(qkv_rows, -1)
+    ln_sum = merged[counts[0] + counts[1] :].reshape(-1)[: ln_flat.shape[1]]
+    grad_table = table_sum.transpose(1, 0, 2)
+    grad_qkv = rows_sum[:, : 3 * local_cols].reshape(qkv_rows, 3, local_cols)
+    grad_wo = rows_sum[:, 3 * local_cols :].T
+    grad_ln = ln_sum.reshape(wo_cols, 2).T
     return (grad_hidden, grad_qkv, grad_wo, grad_ln, grad_table)
 
 

time: 425 us -> 384 us (0.904)
  local copies, waits for them, and re-layouts: 137 us -> 84.8 us
  other arithmetic: 47.5 us -> 61.9 us
    reshape x6 -> x3, local copies, waits for them, and re-layouts: 28.6 us -> 2.3 us  [the longest x1 0.84 us: on_device(): rows_sum = merged[counts[0]:counts[0] + counts[1]].reshape(qkv_rows, -1)]
    slice x3, local copies, waits for them, and re-layouts: 17.9 us -> 2.85 us  [the longest x2 2.84 us: on_device(): ln_sum = merged[counts[0] + counts[1]:].reshape(-1)[:ln_flat.shape[1]]]
    unnamed x61 -> x56, local copies, waits for them, and re-layouts: 24 us -> 13.3 us
    concatenate x0 -> x1, other arithmetic: none -> 10.5 us  [on_device(): jnp.concatenate(pieces, axis=1).reshape(-1, own_blocks, width)]
    concatenate x1, local copies, waits for them, and re-layouts: 10.8 us -> 6.29 us  [on_device(): jnp.concatenate([qkv_term.reshape(width, 3 * local_cols), wo_term.T], axi...]
  transfers between devices with their start and end apart: 1 -> 1, of which waited for: 1 -> 1; matrix products, arithmetic and copies ran while one was open for 5% -> 6% of each run, Pallas kernels for 12% -> 14%
where the time goes in v5:
time: 384 us; the launch traced here: 377 us
  waiting for transfers between devices  89.9 us (23%)
  local copies, waits for them, and re-layouts  84.8 us (22%)
  Pallas kernels  84 us (22%)
  other arithmetic  61.9 us (16%)
  matrix products  41.2 us (11%)
  between operations  14.7 us (4%)
    unnamed x2, waiting for transfers between devices  89.9 us
    pallas_call x1, Pallas kernels, peer_scatter(): pl.pallas_call(functools.partial(_peer_scatter_kernel, n), out_shape=jax....  51 us
    pallas_call x3, Pallas kernels, peer_sum(): pl.pallas_call(functools.partial(_peer_sum_kernel, n), out_shape=jax.Shap...  33.1 us
    dot_general x9, matrix products, contract(): lax.dot_general(left, right, (((left_dim,), (right_dim,)), ((), ())), pre...  19.1 us
    unnamed x56, local copies, waits for them, and re-layouts  13.3 us
    scatter-add x1, other arithmetic, on_device(): table_term = neg_term.at[row_slot, safe_block].add(gold_terms, mode='drop')  10.6 us
    concatenate x1, other arithmetic, on_device(): jnp.concatenate(pieces, axis=1).reshape(-1, own_blocks, width)  10.5 us
    transpose x1, local copies, waits for them, and re-layouts, on_device(): jnp.einsum('mbr,md->rbd', weight_blocks, embed, preferred_element_type=jn...  8.99 us
  transfers between devices with their start and end apart: 1, of which 1 were waited for; matrix products, arithmetic and copies ran while one was open for 6% of the time, Pallas kernels for 14%

profile of v5, /device:TPU:1, one launch (start us, length us, event | category | flops | bytes accessed | tf_op | source)
XLA Modules:
  0.0 376.6 jit_solution(9938346125124258121)
XLA Ops:
  9.3 1.4 slice.69
  10.7 1.3 convolution_convert_fusion.4
  12.9 2.5 fusion.60
  15.6 2.4 convolution_convert_fusion
  18.0 3.9 %reshape.180 = bf16[64,32,2,4,64]{4,3,2,1,0:T(4,128)(2,1)} reshape(bf16[2048,512]{1,0:T(8,128)(2,1)S(1)} %convolution_convert_fusion) | data formatting | bytes 4194304 | tf_op jit(solution)/shard_map/reshape | solution.py:167
  21.9 4.8 %slice_bitcast_fusion = (bf16[64,32,4,64]{3,2,1,0:T(4,128)(2,1)}, bf16[64,32,4,64]{3,2,1,0:T(4,128)(2,1)S(1)}) fusion(bf16[64,32,2,4,64]{4,3,2,1,0:T(4,128)(2,1)} %reshape.180), kind=kLoop, calls=%fused_computation.9 | loop fusion | bytes 4194304 | tf_op jit(solution)/shard_map/squeeze | solution.py:169
  26.7 1.3 copy-done.7
  28.1 1.2 fusion.6
  29.7 6.0 %fusion.13 = f32[64,4,32]{1,2,0:T(8,128)S(1)} fusion(f32[64,4,1,32]{1,3,0,2:T(8,128)S(1)} %copy.65, f32[64,32]{1,0:T(8,128)S(1)} %fusion.32), kind=kOutput, calls=%fused_computation.33 | output fusion | flops 41247 | bytes 73728 | tf_op jit(solution)/shard_map/div | solution.py:177
  35.7 1.0 copy-done.4
  36.9 0.8 copy.66
  37.7 2.3 fusion.2
  41.1 3.5 gather_fusion
  45.6 17.5 %shard_map.137 = f32[128,1024]{1,0:T(8,128)} custom-call(bf16[128,1024]{1,0:T(8,128)(2,1)} %pad_maximum_fusion.2.x_ref), custom_call_target="tpu_custom_call" | custom-call | tf_op jit(solution)/shard_map/pallas_call | solution.py:62
  63.1 1.1 fusion.59
  64.6 1.7 exponential_reduce_fusion
  66.4 3.8 multiply_reduce_fusion
  70.7 6.7 %shard_map.138 = f32[8,64]{1,0:T(8,128)} custom-call(f32[8,64]{1,0:T(8,128)} %pad.10.x_ref), custom_call_target="tpu_custom_call" | custom-call | tf_op jit(solution)/shard_map/pallas_call | solution.py:62
  78.3 3.7 convolution_convert_fusion.1.x_ref
  82.0 8.9 %shard_map.139 = f32[64,1024]{1,0:T(8,128)} custom-call(bf16[64,1024]{1,0:T(8,128)(2,1)} %convolution_convert_fusion.1.x_ref), custom_call_target="tpu_custom_call" | custom-call | tf_op jit(solution)/shard_map/pallas_call | solution.py:62
  90.9 1.4 multiply_reduce_fusion.1
  92.3 0.8 convert_bitcast_fusion.1
  93.6 0.9 fusion.38
  94.6 1.5 convert.12
  96.7 2.8 fusion
  99.5 0.9 copy.57
  100.6 0.8 reshape.188
  101.4 1.4 copy.70
  102.9 2.4 fusion.9
  105.3 1.5 copy.71
  106.8 2.3 fusion.4
  109.8 1.6 convert_element_type.110
  111.3 2.1 convolution_bitcast_fusion.1
  113.4 3.6 copy.55
  117.0 2.5 multiply_bitcast_fusion.1
  119.5 2.9 multiply_bitcast_fusion
  122.4 5.4 %maximum_convert_fusion = bf16[64,32,2,4,64]{4,3,2,1,0:T(4,128)(2,1)} fusion(bf16[64,32,1,4,64]{4,3,2,1,0:T(4,128)(2,1)S(1)} %multiply_bitcast_fusion, bf16[64,32,1,4,64]{4,3,2,1,0:T(4,128)(2,1)S(1)} %multiply_bitcast_fusion.1), kind=kLoop, calls=%fused_computation.3 | loop fusion | flops 1048576 | bytes 4194304 | tf_op jit(solution)/shard_map/convert_element_type | solution.py:247
  127.9 7.6 %convert_element_type.108 = bf16[64,32,512]{2,1,0:T(8,128)(2,1)} reshape(bf16[64,32,2,4,64]{4,3,2,1,0:T(4,128)(2,1)} %maximum_convert_fusion) | data formatting | bytes 4194304 | tf_op jit(solution)/shard_map/convert_element_type | solution.py:247
  135.7 1.2 copy.79
  137.1 1.2 copy-done.18
  138.3 3.7 fusion.62
  142.0 4.1 %copy.56 = f32[1024,2,256]{2,1,0:T(2,128)} copy(f32[1024,2,256]{0,2,1:T(8,128)} %bitcast.176) | data formatting | bytes 4194304 | tf_op jit(solution)/shard_map/reshape | solution.py:254
  146.2 5.7 %pad_maximum_fusion.1 = f32[1024,3,256]{2,1,0:T(4,128)} fusion(f32[1024,2,256]{2,1,0:T(2,128)} %copy.56, f32[1024,1,256]{2,1,0:T(1,128)} %copy.55), kind=kLoop, calls=%fused_computation.4 | loop fusion | flops 786432 | bytes 6291456 | tf_op jit(solution)/shard_map/concatenate | solution.py:253
  151.8 6.3 %concatenate.23 = f32[64,2,8,768]{3,2,1,0:T(8,128)} reshape(f32[1024,3,256]{2,1,0:T(4,128)} %pad_maximum_fusion.1) | data formatting | bytes 6291456 | tf_op jit(solution)/shard_map/concatenate | solution.py:279
  158.1 4.5 %convolution_bitcast_fusion = f32[256,8,1024]{0,2,1:T(8,128)} fusion(bf16[8,8,8,256]{3,2,1,0:T(8,128)(2,1)S(1)} %bitcast.175, bf16[64,1024]{1,0:T(8,128)(2,1)S(1)} %add_convert_fusion), kind=kOutput, calls=%fused_computation.7 | convolution fusion | flops 268435456 | bytes 8781824 | tf_op jit(solution)/shard_map/mbr,md->rbd/dot_general | solution.py:270
  162.6 9.0 %copy.54 = f32[256,8,1024]{2,1,0:T(8,128)} copy(f32[256,8,1024]{0,2,1:T(8,128)} %convolution_bitcast_fusion) | data formatting | bytes 16777216 | tf_op jit(solution)/shard_map/mbr,md->rbd/transpose | solution.py:270
  171.6 1.2 fusion.30
  172.9 10.6 %scatter_fusion = f32[256,8,1024]{2,1,0:T(8,128)} fusion(f32[256,8,1024]{2,1,0:T(8,128)} %copy.54, s32[64]{0:T(128)S(1)} %fusion.37, f32[64,1024]{1,0:T(8,128)S(1)} %fusion.38), kind=kCustom, calls=%fused_computation.1 | custom fusion | flops 65536 | bytes 786944 | tf_op jit(solution)/shard_map/scatter-add | solution.py:273
  183.4 10.5 %pad_maximum_fusion = f32[64,7,8,1024]{3,2,1,0:T(8,128)} fusion(f32[64,1,8,1024]{3,2,1,0:T(8,128)S(1)} %bitcast.173, f32[64,2,8,256]{3,2,1,0:T(8,128)} %fusion.30, f32[64,2,8,768]{3,2,1,0:T(8,128)} %concatenate.23, f32[64,4,8,1024]{3,2,1,0:T(8,128)} %bitcast.168), kind=kLoop, calls=%fused_computation.2 | loop fusion | flops 11010048 | bytes 29360128 | tf_op jit(solution)/shard_map/concatenate | solution.py:289
  193.9 1.2 copy-done.3
  195.1 1.1 copy.52
  196.9 1.3 fusion.15
  198.2 4.1 %fusion.61 = f32[64,32,1024]{2,1,0:T(8,128)S(1)} fusion(bf16[64,32,512]{2,1,0:T(8,128)(2,1)} %convert_element_type.108, bf16[1024,512,1]{1,0,2:T(8,128)(2,1)S(1)} %reshape.214), kind=kOutput, calls=%fused_computation.117 | convolution fusion | flops 2147483648 | bytes 11534336 | tf_op jit(solution)/shard_map/dot_general | solution.py:145
  202.3 3.3 copy-done.2
  206.0 6.1 %scatter-add.12 = f32[64,32,1024]{2,1,0:T(8,128)} dynamic-update-slice(f32[64,32,1024]{2,1,0:T(8,128)} %copy-done.2, f32[64,1,1024]{2,1,0:T(1,128)S(1)} %slice_add_fusion, s32[]{:T(128)} %constant.55.clone.1, s32[]{:T(128)} %constant.55.clone.1, s32[]{:T(128)} %constant.55.clone.1) | dynamic-update-slice | bytes 524292 | tf_op jit(solution)/shard_map/scatter-add | solution.py:263
  212.1 6.5 %convert_element_type.111.y_ref = bf16[64,32,1024]{2,1,0:T(8,128)(2,1)} convert(f32[64,32,1024]{2,1,0:T(8,128)} %scatter-add.12) | non-fusion elementwise | flops 2097152 | bytes 12582912 | tf_op jit(solution)/shard_map/convert_element_type | solution.py:263
  219.1 51.0 %shard_map.140 = bf16[16,32,1024]{2,1,0:T(8,128)(2,1)} custom-call(bf16[64,32,1024]{2,1,0:T(8,128)(2,1)} %convert_element_type.111.y_ref, f32[16,1024]{1,0:T(8,128)} %constant_dynamic-slice_fusion.resid_ref), custom_call_target="tpu_custom_call" | custom-call | tf_op jit(solution)/shard_map/pallas_call | solution.py:126
  270.1 89.9 %reduce-scatter.4.cloned.1.call-done = f32[7,8,1024]{2,1,0:T(8,128)} async-done(((f32[448,8,1024]{2,1,0:T(8,128)}), f32[7,8,1024]{2,1,0:T(8,128)}) %reduce-scatter.4.cloned.1.call-update) | async-done | bytes 229392
  360.0 0.8 slice.96
  360.8 0.8 slice_bitcast_fusion.3
  361.6 0.9 slice_bitcast_fusion.2
  363.2 0.7 copy.62
  364.5 2.1 slice.82
  367.3 2.3 copy.103
  (92 shorter events, 13.7 us)
Async XLA Ops:
  7.2 37.5 %copy-start = (bf16[256,1024]{1,0:T(8,128)(2,1)S(1)}, bf16[256,1024]{1,0:T(8,128)(2,1)}, u32[]{:S(2)}) copy-start(bf16[256,1024]{1,0:T(8,128)(2,1)} %param.14) | copy-start | bytes 1572868
  7.2 8.2 %copy-start.23 = (s32[64]{0:T(128)S(1)}, s32[64]{0:T(128)}, u32[]{:S(2)}) copy-start(s32[64]{0:T(128)} %param.18) | copy-start | bytes 772
  7.2 352.8 %reduce-scatter.4.cloned.1.call-start = ((), (), s32[]{:S(2)}) async-start(), calls=%async_computation.1 | async-start | bytes 14909440
  10.7 52.4 %copy-start.8 = (bf16[64,1,1024]{2,1,0:T(2,128)(2,1)}, bf16[64,1,1024]{2,1,0:T(2,128)(2,1)S(1)}, u32[]{:S(2)}) copy-start(bf16[64,1,1024]{2,1,0:T(2,128)(2,1)S(1)} %slice.69) | copy-start | bytes 393220
  12.9 2.7 copy-start.17
  26.7 1.4 copy-start.7
  35.7 1.0 copy-start.4
  36.7 4.2 %copy-start.24 = (s32[1,4]{1,0:T(1,128)S(1)}, s32[1,4]{1,0:T(1,128)}, u32[]{:S(2)}) copy-start(s32[1,4]{1,0:T(1,128)} %param.21) | copy-start | bytes 52
  36.9 27.6 %copy-start.16 = (f32[1024]{0:T(1024)S(1)}, f32[1024]{0:T(1024)}, u32[]{:S(2)}) copy-start(f32[1024]{0:T(1024)} %param.15) | copy-start | bytes 12292
  36.9 27.6 %copy-start.22 = (f32[1024]{0:T(1024)S(1)}, f32[1024]{0:T(1024)}, u32[]{:S(2)}) copy-start(f32[1024]{0:T(1024)} %param.16) | copy-start | bytes 12292
  64.3 17.7 %copy-start.19 = (f32[64]{0:T(128)}, f32[64]{0:T(128)S(1)}, u32[]{:S(2)}) copy-start(f32[64]{0:T(128)S(1)} %broadcast_multiply_fusion.2) | copy-start | bytes 772
  64.5 17.5 %copy-start.20 = (f32[64]{0:T(128)}, f32[64]{0:T(128)S(1)}, u32[]{:S(2)}) copy-start(f32[64]{0:T(128)S(1)} %add_rsqrt_fusion) | copy-start | bytes 772
  66.4 24.5 %copy-start.5 = (f32[128,1024]{1,0:T(8,128)S(1)}, f32[128,1024]{1,0:T(8,128)}, u32[]{:S(2)}) copy-start(f32[128,1024]{1,0:T(8,128)} %shard_map.137) | copy-start | bytes 1572868
  78.1 12.7 %copy-start.21 = (f32[64]{0:T(128)}, f32[64]{0:T(128)S(1)}, u32[]{:S(2)}) copy-start(f32[64]{0:T(128)S(1)} %fusion.36) | copy-start | bytes 772
  101.4 9.9 %copy-start.9 = (bf16[64,1,1024]{2,1,0:T(2,128)(2,1)S(1)}, bf16[64,1,1024]{2,1,0:T(2,128)(2,1)}, u32[]{:S(2)}) copy-start(bf16[64,1,1024]{2,1,0:T(2,128)(2,1)} %copy-done.8) | copy-start | bytes 393220
  105.3 11.7 %copy-start.12 = (f32[64,4,64]{2,1,0:T(4,128)S(1)}, f32[64,4,64]{2,1,0:T(4,128)}, u32[]{:S(2)}) copy-start(f32[64,4,64]{2,1,0:T(4,128)} %convert.12) | copy-start | bytes 196612
  106.7 12.7 %copy-start.11 = (f32[64,4,64]{2,1,0:T(4,128)S(1)}, f32[64,4,64]{2,1,0:T(4,128)}, u32[]{:S(2)}) copy-start(f32[64,4,64]{2,1,0:T(4,128)} %convert.14) | copy-start | bytes 196612
  127.9 7.6 %copy-start.14 = (f32[64,32]{1,0:T(8,128)S(1)}, f32[64,32]{1,0:T(8,128)}, u32[]{:S(2)}) copy-start(f32[64,32]{1,0:T(8,128)} %reshape.188) | copy-start | bytes 24580
  135.5 1.6 copy-start.6
  135.5 2.8 copy-start.18
  162.6 9.0 %copy-start.10 = (bf16[1024,64]{1,0:T(8,128)(2,1)S(1)}, bf16[1024,64]{1,0:T(8,128)(2,1)}, u32[]{:S(2)}) copy-start(bf16[1024,64]{1,0:T(8,128)(2,1)} %copy.57) | copy-start | bytes 393220
  162.6 9.0 %copy-start.15 = (bf16[64,256,1,1]{1,0,2,3:T(8,128)(2,1)S(1)}, bf16[64,256,1,1]{1,0,2,3:T(8,128)(2,1)}, u32[]{:S(2)}) copy-start(bf16[64,256,1,1]{1,0,2,3:T(8,128)(2,1)} %reshape.219) | copy-start | bytes 98308
  193.9 1.2 copy-start.3
  193.9 3.0 copy-start.13
  202.3 3.3 copy-start.2
  218.5 151.0 %copy-start.1 = (bf16[256,1024]{1,0:T(8,128)(2,1)S(1)}, bf16[256,1024]{1,0:T(8,128)(2,1)}, u32[]{:S(2)}) copy-start(bf16[256,1024]{1,0:T(8,128)(2,1)} %param.14) | copy-start | bytes 1572868
Sparse Core Ops, SparseCore 0:
  194.0 165.9 reduce-scatter.3

commit v6 on v5

--- a/solution.py
+++ b/solution.py
@@ -220,7 +220,6 @@
         - normed * jnp.mean(upper * normed, axis=-1, keepdims=True)
     )
     d_resid_bf = d_resid.astype(jnp.bfloat16)
-    wo_term = contract(context_rows, d_resid_bf, 0, 0)
     d_context = contract(d_resid_bf, w_out, 1, 1).astype(jnp.bfloat16)
     context_head_gradient = d_context.reshape(ment_rows, local_heads, HD)
     probability_gradient = jnp.einsum(
@@ -250,9 +249,6 @@
     count = lax.axis_size("ment") * (width // lax.axis_size("ment"))
     kv_term = contract(hidden_in.reshape(ment_rows * seq_len, count), flat_grad, 0, 0)
     query_term = contract(hidden_in[:, 0, :], query_gradient, 0, 0)
-    qkv_term = jnp.concatenate(
-        [query_term[:, None, :], kv_term.reshape(count, 2, local_cols)], axis=1
-    )
     share = ment_rows // lax.axis_size("ent")
     grad_part = d_keyval.reshape(share * lax.axis_size("ent") * seq_len, 2 * local_cols)
     token_term = contract(grad_part, w_keyval, 1, 1).reshape(
@@ -265,19 +261,26 @@
         3,
     )
     gold_terms = contract(w_inb, embed, 0, 0)
-    weight_blocks = w_neg.reshape(ment_rows, own_blocks, block_rows)
-    count = lax.axis_size("ment") * (block_rows // lax.axis_size("ment"))
-    neg_term = jnp.einsum("mbr,md->rbd", weight_blocks, embed, preferred_element_type=jnp.float32)
-    inside = owned & (gold_row >= 0) & (gold_row < count)
-    row_slot = jnp.where(inside, gold_row, count)
-    table_term = neg_term.at[row_slot, safe_block].add(gold_terms, mode="drop")
+    neg_weights = (
+        w_neg.reshape(ment_rows, own_blocks, block_rows).transpose(0, 2, 1).reshape(ment_rows, -1)
+    )
+    slot = gold_row * own_blocks + safe_block
+    hit = (slot[:, None] == jnp.arange(block_rows * own_blocks)[None, :]) & owned[:, None]
+    gold_add = lax.dot_general(
+        hit.astype(jnp.float32),
+        gold_terms,
+        (((0,), (0,)), ((), ())),
+        precision=lax.Precision.HIGHEST,
+        preferred_element_type=jnp.float32,
+    )
+    table_term = contract(neg_weights, embed, 0, 0) + gold_add
     parts = lax.axis_size("ment")
     qkv_rows = width // parts
     wo_cols = width // parts
     slab = own_blocks * width
     table_piece = table_term.reshape(parts, -1, own_blocks, width)
     rows_piece = jnp.concatenate(
-        [qkv_term.reshape(width, 3 * local_cols), wo_term.T], axis=1
+        [query_term, kv_term, contract(d_resid_bf, context_rows, 0, 0)], axis=1
     ).reshape(parts, -1, own_blocks, width)
     ln_flat = ln_terms.T.reshape(parts, -1)
     ln_piece = jnp.pad(ln_flat, ((0, 0), (0, -ln_flat.shape[1] % slab))).reshape(

time: 384 us -> 348 us (0.906)
  other arithmetic: 61.9 us -> 42.3 us
  local copies, waits for them, and re-layouts: 84.8 us -> 66.8 us
    scatter-add x1 -> x0, other arithmetic: 10.6 us -> none  [on_device(): table_term = neg_term.at[row_slot, safe_block].add(gold_terms, mode='drop')]
    transpose x1 -> x0, local copies, waits for them, and re-layouts: 8.99 us -> none  [on_device(): jnp.einsum('mbr,md->rbd', weight_blocks, embed, preferred_element_type=jn...]
    concatenate x1, other arithmetic: 10.5 us -> 5.85 us  [on_device(): jnp.concatenate(pieces, axis=1).reshape(-1, own_blocks, width)]
    concatenate x2 -> x1, other arithmetic: 6.4 us -> 2.29 us  [on_device(): jnp.concatenate([query_term, kv_term, contract(d_resid_bf, context_rows,...]
    dot_general x9 -> x10, matrix products: 19.1 us -> 19.9 us  [contract(): lax.dot_general(left, right, (((left_dim,), (right_dim,)), ((), ())), pre...]
    unnamed x56 -> x65, local copies, waits for them, and re-layouts: 13.3 us -> 13.9 us
  transfers between devices with their start and end apart: 1 -> 1, of which waited for: 1 -> 1; matrix products, arithmetic and copies ran while one was open for 6% -> 6% of each run, Pallas kernels for 14% -> 15%
where the time goes in v6:
time: 348 us; the launch traced here: 341 us
  waiting for transfers between devices  89.6 us (26%)
  Pallas kernels  84.2 us (24%)
  local copies, waits for them, and re-layouts  66.8 us (19%)
  matrix products  43.1 us (12%)
  other arithmetic  42.3 us (12%)
  between operations  14.9 us (4%)
    unnamed x2, waiting for transfers between devices  89.6 us
    pallas_call x1, Pallas kernels, peer_scatter(): pl.pallas_call(functools.partial(_peer_scatter_kernel, n), out_shape=jax....  51.2 us
    pallas_call x3, Pallas kernels, peer_sum(): pl.pallas_call(functools.partial(_peer_sum_kernel, n), out_shape=jax.Shap...  33.1 us
    dot_general x10, matrix products, contract(): lax.dot_general(left, right, (((left_dim,), (right_dim,)), ((), ())), pre...  19.9 us
    unnamed x65, local copies, waits for them, and re-layouts  13.9 us
    convert_element_type x1, local copies, waits for them, and re-layouts, on_device(): d_keyval = jnp.stack([key_gradient, value_gradient], axis=2).reshape(ment...  7.64 us
  transfers between devices with their start and end apart: 1, of which 1 were waited for; matrix products, arithmetic and copies ran while one was open for 6% of the time, Pallas kernels for 15%

profile of v6, /device:TPU:1, one launch (start us, length us, event | category | flops | bytes accessed | tf_op | source)
XLA Modules:
  0.0 341.0 jit_solution(8742311514416914551)
XLA Ops:
  7.3 1.4 slice.69
  8.7 1.2 convolution_convert_fusion.4
  10.0 0.7 reshape.174
  10.8 2.3 fusion.59
  14.0 4.5 %convolution_convert_fusion = bf16[2048,512]{1,0:T(8,128)(2,1)S(1)} fusion(bf16[2048,1024]{1,0:T(8,128)(2,1)} %bitcast.165, bf16[1024,512]{1,0:T(8,128)(2,1)S(1)} %bitcast.156), kind=kOutput, calls=%fused_computation.7 | convolution fusion | flops 2148532224 | bytes 7340032 | tf_op jit(solution)/shard_map/dot_general | solution.py:164
  18.6 4.1 %reshape.177 = bf16[64,32,2,4,64]{4,3,2,1,0:T(4,128)(2,1)} reshape(bf16[2048,512]{1,0:T(8,128)(2,1)S(1)} %convolution_convert_fusion) | data formatting | bytes 4194304 | tf_op jit(solution)/shard_map/reshape | solution.py:167
  22.7 4.8 %slice_bitcast_fusion = (bf16[64,32,4,64]{3,2,1,0:T(4,128)(2,1)}, bf16[64,32,4,64]{3,2,1,0:T(4,128)(2,1)S(1)}) fusion(bf16[64,32,2,4,64]{4,3,2,1,0:T(4,128)(2,1)} %reshape.177), kind=kLoop, calls=%fused_computation.8 | loop fusion | bytes 4194304 | tf_op jit(solution)/shard_map/squeeze | solution.py:169
  27.5 1.3 copy-done.10
  28.8 1.2 fusion.6
  30.5 6.0 %fusion.13 = f32[64,4,32]{1,2,0:T(8,128)S(1)} fusion(f32[64,4,1,32]{1,3,0,2:T(8,128)S(1)} %copy.53, f32[64,32]{1,0:T(8,128)S(1)} %fusion.35), kind=kOutput, calls=%fused_computation.33 | output fusion | flops 41247 | bytes 73728 | tf_op jit(solution)/shard_map/div | solution.py:177
  36.5 1.0 copy-done.5
  37.7 0.8 copy.54
  38.5 2.3 fusion.2
  40.9 3.5 %gather_fusion = bf16[64,1024]{1,0:T(8,128)(2,1)S(1)} fusion(bf16[2048,1024]{1,0:T(8,128)(2,1)} %bitcast.147, s32[1024]{0:T(1024)S(1)} %pad_clamp_fusion), kind=kCustom, calls=%fused_computation | custom fusion | bytes 262400 | tf_op jit(solution)/shard_map/gather | solution.py:188
  44.8 0.7 pad_maximum_fusion.2.x_ref
  45.5 17.5 %shard_map.137 = f32[128,1024]{1,0:T(8,128)} custom-call(bf16[128,1024]{1,0:T(8,128)(2,1)} %pad_maximum_fusion.2.x_ref), custom_call_target="tpu_custom_call" | custom-call | tf_op jit(solution)/shard_map/pallas_call | solution.py:62
  63.1 1.1 fusion.58
  64.5 1.7 exponential_reduce_fusion
  66.3 3.8 %multiply_reduce_fusion = (f32[64]{0:T(128)S(1)}, f32[64,2048]{1,0:T(8,128)S(1)}) fusion(f32[2048]{0:T(1024)S(1)} %bitcast.160, bf16[64,1024]{1,0:T(8,128)(2,1)S(1)} %add_convert_fusion, bf16[2048,1024]{1,0:T(8,128)(2,1)} %bitcast.148), kind=kOutput, calls=%fused_computation.42 | convolution fusion | flops 268697536 | bytes 4858112 | tf_op jit(solution)/shard_map/dot_general | solution.py:145
  70.7 6.7 %shard_map.138 = f32[8,64]{1,0:T(8,128)} custom-call(f32[8,64]{1,0:T(8,128)} %pad.10.x_ref), custom_call_target="tpu_custom_call" | custom-call | tf_op jit(solution)/shard_map/pallas_call | solution.py:62
  77.4 0.7 fusion.36
  78.8 3.7 %convolution_convert_fusion.1.x_ref = bf16[64,1024]{1,0:T(8,128)(2,1)} fusion(bf16[64,2048]{1,0:T(8,128)(2,1)S(1)} %multiply_convert_fusion, bf16[2048,1024]{1,0:T(8,128)(2,1)} %bitcast.149), kind=kOutput, calls=%fused_computation.21 | convolution fusion | flops 268500992 | bytes 4587520 | tf_op jit(solution)/shard_map/dot_general | solution.py:211
  82.5 8.9 %shard_map.139 = f32[64,1024]{1,0:T(8,128)} custom-call(bf16[64,1024]{1,0:T(8,128)(2,1)} %convolution_convert_fusion.1.x_ref), custom_call_target="tpu_custom_call" | custom-call | tf_op jit(solution)/shard_map/pallas_call | solution.py:62
  91.4 1.4 multiply_reduce_fusion.1
  92.7 0.7 subtract_multiply_fusion
  94.0 0.9 fusion.37
  94.9 2.1 fusion.31
  97.0 1.5 convert.12
  99.2 2.8 fusion
  102.7 0.8 reshape.186
  103.5 1.4 copy.58
  104.9 2.4 fusion.9
  107.3 1.5 copy.59
  108.8 2.3 fusion.4
  111.8 1.6 convert_element_type.110
  113.3 2.1 convolution_bitcast_fusion.1
  115.4 3.5 %multiply_bitcast_fusion.1 = bf16[64,32,1,4,64]{4,3,2,1,0:T(4,128)(2,1)S(1)} fusion(f32[64,4,32]{1,2,0:T(8,128)S(1)} %fusion.9, f32[64,4,64]{2,1,0:T(4,128)} %convert.12), kind=kLoop, calls=%fused_computation.6 | loop fusion | flops 1572864 | bytes 1146880 | tf_op jit(solution)/shard_map/stack | solution.py:244
  119.0 2.5 multiply_bitcast_fusion
  121.5 5.4 %maximum_convert_fusion = bf16[64,32,2,4,64]{4,3,2,1,0:T(4,128)(2,1)} fusion(bf16[64,32,1,4,64]{4,3,2,1,0:T(4,128)(2,1)S(1)} %multiply_bitcast_fusion, bf16[64,32,1,4,64]{4,3,2,1,0:T(4,128)(2,1)S(1)} %multiply_bitcast_fusion.1), kind=kLoop, calls=%fused_computation.2 | loop fusion | flops 1048576 | bytes 4194304 | tf_op jit(solution)/shard_map/convert_element_type | solution.py:246
  126.9 7.6 %convert_element_type.108 = bf16[64,32,512]{2,1,0:T(8,128)(2,1)} reshape(bf16[64,32,2,4,64]{4,3,2,1,0:T(4,128)(2,1)} %maximum_convert_fusion) | data formatting | bytes 4194304 | tf_op jit(solution)/shard_map/convert_element_type | solution.py:246
  134.7 1.2 copy.66
  136.2 1.2 copy-done.16
  137.4 2.3 convolution_bitcast_fusion
  139.8 2.3 pad_maximum_fusion.1
  142.0 5.5 %copy.45 = f32[1024,1024]{1,0:T(8,128)} copy(f32[1024,1024]{0,1:T(8,128)} %pad_maximum_fusion.1) | data formatting | bytes 8388608 | tf_op jit(solution)/shard_map/concatenate | solution.py:282
  147.6 1.2 fusion.15
  148.9 3.6 %convolution_add_fusion = f32[2048,1024]{1,0:T(8,128)S(1)} fusion(f32[2048,1024]{1,0:T(8,128)S(1)} %fusion.15, f32[64,1024]{1,0:T(8,128)S(1)} %fusion.37, s32[64]{0:T(128)S(1)} %copy-done.24, pred[64]{0:T(512)(128)(4,1)S(1)} %copy-done.23), kind=kOutput, calls=%fused_computation.3 | convolution fusion | flops 1612972032 | bytes 17039680 | tf_op jit(solution)/shard_map/dot_general | solution.py:269
  152.5 5.8 %pad_maximum_fusion = f32[64,7,8,1024]{3,2,1,0:T(8,128)} fusion(f32[64,1,8,1024]{3,2,1,0:T(8,128)S(1)} %bitcast.152, f32[64,2,8,1024]{3,2,1,0:T(8,128)S(1)} %bitcast.150, f32[64,4,8,1024]{3,2,1,0:T(8,128)S(1)} %bitcast.146), kind=kLoop, calls=%fused_computation.1 | loop fusion | flops 7340032 | bytes 29360128 | tf_op jit(solution)/shard_map/concatenate | solution.py:292
  158.4 1.2 copy-done.4
  159.6 1.1 copy.43
  160.7 0.7 reshape.206
  161.4 1.3 fusion.17
  162.7 4.1 %fusion.60 = f32[64,32,1024]{2,1,0:T(8,128)S(1)} fusion(bf16[64,32,512]{2,1,0:T(8,128)(2,1)} %convert_element_type.108, bf16[1024,512,1]{1,0,2:T(8,128)(2,1)S(1)} %reshape.206), kind=kOutput, calls=%fused_computation.110 | convolution fusion | flops 2147483648 | bytes 11534336 | tf_op jit(solution)/shard_map/dot_general | solution.py:145
  166.8 3.3 copy-done.3
  170.4 6.1 %scatter-add.4 = f32[64,32,1024]{2,1,0:T(8,128)} dynamic-update-slice(f32[64,32,1024]{2,1,0:T(8,128)} %copy-done.3, f32[64,1,1024]{2,1,0:T(1,128)S(1)} %slice_add_fusion, s32[]{:T(128)} %constant.54.clone.1, s32[]{:T(128)} %constant.54.clone.1, s32[]{:T(128)} %constant.54.clone.1) | dynamic-update-slice | bytes 524292 | tf_op jit(solution)/shard_map/scatter-add | solution.py:259
  176.5 6.4 %convert_element_type.111.y_ref = bf16[64,32,1024]{2,1,0:T(8,128)(2,1)} convert(f32[64,32,1024]{2,1,0:T(8,128)} %scatter-add.4) | non-fusion elementwise | flops 2097152 | bytes 12582912 | tf_op jit(solution)/shard_map/convert_element_type | solution.py:259
  183.6 51.2 %shard_map.140 = bf16[16,32,1024]{2,1,0:T(8,128)(2,1)} custom-call(bf16[64,32,1024]{2,1,0:T(8,128)(2,1)} %convert_element_type.111.y_ref, f32[16,1024]{1,0:T(8,128)} %constant_dynamic-slice_fusion.resid_ref), custom_call_target="tpu_custom_call" | custom-call | tf_op jit(solution)/shard_map/pallas_call | solution.py:126
  234.8 89.6 %reduce-scatter.4.cloned.1.call-done = f32[7,8,1024]{2,1,0:T(8,128)} async-done(((f32[448,8,1024]{2,1,0:T(8,128)}), f32[7,8,1024]{2,1,0:T(8,128)}) %reduce-scatter.4.cloned.1.call-update) | async-done | bytes 229392
  324.4 0.8 slice.94
  325.2 0.8 slice_bitcast_fusion.3
  326.0 0.9 slice_bitcast_fusion.2
  327.6 0.7 copy.50
  328.9 2.1 slice.82
  331.7 2.3 copy.85
  (96 shorter events, 9.6 us)
Async XLA Ops:
  7.2 37.4 %copy-start = (bf16[256,1024]{1,0:T(8,128)(2,1)S(1)}, bf16[256,1024]{1,0:T(8,128)(2,1)}, u32[]{:S(2)}) copy-start(bf16[256,1024]{1,0:T(8,128)(2,1)} %param.14) | copy-start | bytes 1572868
  7.2 6.0 %copy-start.27 = (s32[64]{0:T(128)S(1)}, s32[64]{0:T(128)}, u32[]{:S(2)}) copy-start(s32[64]{0:T(128)} %param.19) | copy-start | bytes 772
  7.2 6.0 %copy-start.28 = (s32[1,4]{1,0:T(1,128)S(1)}, s32[1,4]{1,0:T(1,128)}, u32[]{:S(2)}) copy-start(s32[1,4]{1,0:T(1,128)} %param.21) | copy-start | bytes 52
  7.2 6.1 %copy-start.26 = (s32[64]{0:T(128)S(1)}, s32[64]{0:T(128)}, u32[]{:S(2)}) copy-start(s32[64]{0:T(128)} %param.20) | copy-start | bytes 772
  7.2 6.7 %copy-start.25 = (s32[64]{0:T(128)S(1)}, s32[64]{0:T(128)}, u32[]{:S(2)}) copy-start(s32[64]{0:T(128)} %param.18) | copy-start | bytes 772
  7.2 317.2 %reduce-scatter.4.cloned.1.call-start = ((), (), s32[]{:S(2)}) async-start(), calls=%async_computation.1 | async-start | bytes 14909440
  13.2 31.3 %copy-start.22 = (pred[64]{0:T(512)(128)(4,1)}, pred[64]{0:T(512)(128)(4,1)S(1)}, u32[]{:S(2)}) copy-start(pred[64]{0:T(512)(128)(4,1)S(1)} %compare_and_fusion) | copy-start | bytes 196
  27.5 1.3 copy-start.10
  36.5 1.0 copy-start.5
  37.7 26.7 %copy-start.15 = (f32[1024]{0:T(1024)S(1)}, f32[1024]{0:T(1024)}, u32[]{:S(2)}) copy-start(f32[1024]{0:T(1024)} %param.15) | copy-start | bytes 12292
  37.7 26.7 %copy-start.21 = (f32[1024]{0:T(1024)S(1)}, f32[1024]{0:T(1024)}, u32[]{:S(2)}) copy-start(f32[1024]{0:T(1024)} %param.16) | copy-start | bytes 12292
  40.9 25.3 %copy-start.13 = (bf16[64,256]{1,0:T(8,128)(2,1)}, bf16[64,256]{1,0:T(8,128)(2,1)S(1)}, u32[]{:S(2)}) copy-start(bf16[64,256]{1,0:T(8,128)(2,1)S(1)} %convert_element_type.95) | copy-start | bytes 98308
  64.4 1.9 copy-start.17
  66.3 25.0 %copy-start.8 = (f32[128,1024]{1,0:T(8,128)S(1)}, f32[128,1024]{1,0:T(8,128)}, u32[]{:S(2)}) copy-start(f32[128,1024]{1,0:T(8,128)} %shard_map.137) | copy-start | bytes 1572868
  78.1 0.5 copy-start.19
  78.7 12.6 %copy-start.18 = (f32[64]{0:T(128)S(1)}, f32[64]{0:T(128)}, u32[]{:S(2)}) copy-start(f32[64]{0:T(128)} %copy-done.17) | copy-start | bytes 772
  78.7 12.6 %copy-start.20 = (f32[64]{0:T(128)S(1)}, f32[64]{0:T(128)}, u32[]{:S(2)}) copy-start(f32[64]{0:T(128)} %copy-done.19) | copy-start | bytes 772
  113.3 5.6 %copy-start.11 = (f32[64,4,64]{2,1,0:T(4,128)S(1)}, f32[64,4,64]{2,1,0:T(4,128)}, u32[]{:S(2)}) copy-start(f32[64,4,64]{2,1,0:T(4,128)} %convert.14) | copy-start | bytes 196612
  126.9 7.6 %copy-start.14 = (f32[64,32]{1,0:T(8,128)S(1)}, f32[64,32]{1,0:T(8,128)}, u32[]{:S(2)}) copy-start(f32[64,32]{1,0:T(8,128)} %reshape.186) | copy-start | bytes 24580
  134.6 1.6 copy-start.9
  134.6 2.8 copy-start.16
  137.4 2.4 copy-start.6
  137.4 2.4 copy-start.7
  147.6 1.3 copy-start.23
  147.6 1.3 copy-start.24
  148.9 3.7 %copy-start.2 = (f32[1024,1024]{1,0:T(8,128)S(1)}, f32[1024,1024]{1,0:T(8,128)}, u32[]{:S(2)}) copy-start(f32[1024,1024]{1,0:T(8,128)} %copy.45) | copy-start | bytes 12582916
  158.4 1.2 copy-start.4
  158.4 3.0 copy-start.12
  166.8 3.3 copy-start.3
  183.0 151.0 %copy-start.1 = (bf16[256,1024]{1,0:T(8,128)(2,1)S(1)}, bf16[256,1024]{1,0:T(8,128)(2,1)}, u32[]{:S(2)}) copy-start(bf16[256,1024]{1,0:T(8,128)(2,1)} %param.14) | copy-start | bytes 1572868
Sparse Core Ops, SparseCore 0:
  158.5 165.8 reduce-scatter.3

commit v7 on v6

--- a/solution.py
+++ b/solution.py
@@ -240,19 +240,17 @@
     value_gradient = jnp.einsum(
         "ryk,ryo->rkyo", probability_half, context_head_gradient, preferred_element_type=jnp.float32
     )
-    d_keyval = (
-        jnp.stack([key_gradient, value_gradient], axis=2)
-        .reshape(ment_rows, seq_len, 2 * local_cols)
-        .astype(jnp.bfloat16)
-    )
-    flat_grad = d_keyval.reshape(ment_rows * seq_len, 2 * local_cols)
-    count = lax.axis_size("ment") * (width // lax.axis_size("ment"))
-    kv_term = contract(hidden_in.reshape(ment_rows * seq_len, count), flat_grad, 0, 0)
+    d_keyval = jnp.stack([key_gradient, value_gradient], axis=2).astype(jnp.bfloat16)
+    kv_term = lax.dot_general(
+        hidden_in, d_keyval, (((0, 1), (0, 1)), ((), ())), preferred_element_type=jnp.float32
+    ).reshape(width, 2 * local_cols)
     query_term = contract(hidden_in[:, 0, :], query_gradient, 0, 0)
     share = ment_rows // lax.axis_size("ent")
-    grad_part = d_keyval.reshape(share * lax.axis_size("ent") * seq_len, 2 * local_cols)
-    token_term = contract(grad_part, w_keyval, 1, 1).reshape(
-        share * lax.axis_size("ent"), seq_len, width
+    token_term = lax.dot_general(
+        d_keyval,
+        w_keyval.reshape(width, 2, local_heads, HD),
+        (((2, 3, 4), (1, 2, 3)), ((), ())),
+        preferred_element_type=jnp.float32,
     )
     resid_mine = lax.dynamic_slice_in_dim(d_resid, owner * share, share, 0)
     grad_hidden = peer_scatter(

time: 348 us -> 306 us (0.88)
  other arithmetic: 42.3 us -> 21.1 us
  local copies, waits for them, and re-layouts: 66.8 us -> 53.2 us
  matrix products: 43.1 us -> 37.8 us
    dot_general x10 -> x8, matrix products: 19.9 us -> 8.2 us  [contract(): lax.dot_general(left, right, (((left_dim,), (right_dim,)), ((), ())), pre...]
    convert_element_type x2 -> x0, local copies, waits for them, and re-layouts: 8.46 us -> none  [the longest x1 7.64 us: on_device(): d_keyval = jnp.stack([key_gradient, value_gradient], axis=2).reshape(ment...]
    dot_general x0 -> x2, matrix products: none -> 7.77 us  [the longest x1 5.4 us: on_device(): lax.dot_general(d_keyval, w_keyval.reshape(width, 2, local_heads, HD), ((...]
    div x1 -> x0, other arithmetic: 6 us -> none  [on_device(): probs = expo / jnp.sum(expo, axis=-1, keepdims=True)]
    convert_element_type x1 -> x0, other arithmetic: 5.44 us -> none  [on_device(): d_keyval = jnp.stack([key_gradient, value_gradient], axis=2).reshape(ment...]
    another operation x4, other arithmetic: 8.19 us -> 3.08 us  [the longest x2 3.05 us: on_device(): jnp.stack([key_gradient, value_gradient], axis=2).astype(jnp.bfloat16)]
    unnamed x65 -> x56, local copies, waits for them, and re-layouts: 13.9 us -> 15 us
  transfers between devices with their start and end apart: 1 -> 1, of which waited for: 1 -> 1; matrix products, arithmetic and copies ran while one was open for 6% -> 6% of each run, Pallas kernels for 15% -> 17%
where the time goes in v7:
time: 306 us; the launch traced here: 302 us
  waiting for transfers between devices  91.1 us (30%)
  Pallas kernels  84.2 us (28%)
  local copies, waits for them, and re-layouts  53.2 us (17%)
  matrix products  37.8 us (12%)
  other arithmetic  21.1 us (7%)
  between operations  14.7 us (5%)
    unnamed x2, waiting for transfers between devices  91.1 us
    pallas_call x1, Pallas kernels, peer_scatter(): pl.pallas_call(functools.partial(_peer_scatter_kernel, n), out_shape=jax....  51.1 us
    pallas_call x3, Pallas kernels, peer_sum(): pl.pallas_call(functools.partial(_peer_sum_kernel, n), out_shape=jax.Shap...  33.1 us
    unnamed x56, local copies, waits for them, and re-layouts  15 us
    dot_general x8, matrix products, contract(): lax.dot_general(left, right, (((left_dim,), (right_dim,)), ((), ())), pre...  8.2 us
    convert_element_type x1, other arithmetic, on_device(): token_term.at[:, 0, :].add(contract(query_gradient, w_query, 1, 1))  6.47 us
  transfers between devices with their start and end apart: 1, of which 1 were waited for; matrix products, arithmetic and copies ran while one was open for 6% of the time, Pallas kernels for 17%

profile of v7, /device:TPU:1, one launch (start us, length us, event | category | flops | bytes accessed | tf_op | source)
XLA Modules:
  0.0 302.2 jit_solution(6244617036490087814)
XLA Ops:
  7.2 1.5 slice.69
  8.8 1.2 convolution_convert_fusion.4
  10.0 0.7 reshape.163
  10.8 0.7 fusion.36
  11.6 1.3 copy.76
  12.9 4.9 %convolution_convert_fusion = bf16[2048,512]{1,0:T(8,128)(2,1)S(1)} fusion(bf16[2048,1024]{1,0:T(8,128)(2,1)} %bitcast.155, bf16[1024,512]{0,1:T(8,128)(2,1)} %bitcast.139), kind=kOutput, calls=%fused_computation.10 | convolution fusion | flops 2148532224 | bytes 7340032 | tf_op jit(solution)/shard_map/dot_general | solution.py:164
  17.8 3.6 %reshape.166 = bf16[64,32,2,4,64]{4,3,2,1,0:T(4,128)(2,1)} reshape(bf16[2048,512]{1,0:T(8,128)(2,1)S(1)} %convolution_convert_fusion) | data formatting | bytes 4194304 | tf_op jit(solution)/shard_map/reshape | solution.py:167
  21.4 3.4 %slice_bitcast_fusion = (bf16[64,32,4,64]{3,2,1,0:T(4,128)(2,1)S(1)}, bf16[64,32,4,64]{3,2,1,0:T(4,128)(2,1)S(1)}) fusion(bf16[64,32,2,4,64]{4,3,2,1,0:T(4,128)(2,1)} %reshape.166), kind=kLoop, calls=%fused_computation.13 | loop fusion | bytes 4194304 | tf_op jit(solution)/shard_map/squeeze | solution.py:169
  24.9 1.3 copy-done.9
  26.1 1.2 fusion.11
  27.7 0.6 fusion.7
  28.3 0.7 reshape.200
  29.3 0.5 multiply_add_fusion
  29.9 3.5 %gather_fusion = bf16[64,1024]{1,0:T(8,128)(2,1)S(1)} fusion(bf16[2048,1024]{1,0:T(8,128)(2,1)} %bitcast.131, s32[1024]{0:T(1024)S(1)} %pad_clamp_fusion), kind=kCustom, calls=%fused_computation | custom fusion | bytes 262400 | tf_op jit(solution)/shard_map/gather | solution.py:188
  33.8 0.7 pad_maximum_fusion.2.x_ref
  34.5 17.5 %shard_map.137 = f32[128,1024]{1,0:T(8,128)} custom-call(bf16[128,1024]{1,0:T(8,128)(2,1)} %pad_maximum_fusion.2.x_ref), custom_call_target="tpu_custom_call" | custom-call | tf_op jit(solution)/shard_map/pallas_call | solution.py:62
  52.0 1.1 fusion.39
  53.5 1.1 exponential_reduce_fusion
  54.6 3.8 %multiply_reduce_fusion = (f32[64]{0:T(128)S(1)}, f32[64,2048]{1,0:T(8,128)S(1)}) fusion(f32[2048]{0:T(1024)S(1)} %bitcast.150, bf16[64,1024]{1,0:T(8,128)(2,1)S(1)} %add_convert_fusion, bf16[2048,1024]{1,0:T(8,128)(2,1)} %bitcast.132), kind=kOutput, calls=%fused_computation.37 | convolution fusion | flops 268697536 | bytes 4858112 | tf_op jit(solution)/shard_map/dot_general | solution.py:145
  58.4 0.6 pad.10.x_ref
  59.0 6.7 %shard_map.138 = f32[8,64]{1,0:T(8,128)} custom-call(f32[8,64]{1,0:T(8,128)} %pad.10.x_ref), custom_call_target="tpu_custom_call" | custom-call | tf_op jit(solution)/shard_map/pallas_call | solution.py:62
  65.7 0.7 fusion.37
  66.6 3.7 %convolution_convert_fusion.1.x_ref = bf16[64,1024]{1,0:T(8,128)(2,1)} fusion(bf16[64,2048]{1,0:T(8,128)(2,1)S(1)} %multiply_convert_fusion.2, bf16[2048,1024]{1,0:T(8,128)(2,1)} %bitcast.133), kind=kOutput, calls=%fused_computation.26 | convolution fusion | flops 268500992 | bytes 4587520 | tf_op jit(solution)/shard_map/dot_general | solution.py:211
  70.3 8.9 %shard_map.139 = f32[64,1024]{1,0:T(8,128)} custom-call(bf16[64,1024]{1,0:T(8,128)(2,1)} %convolution_convert_fusion.1.x_ref), custom_call_target="tpu_custom_call" | custom-call | tf_op jit(solution)/shard_map/pallas_call | solution.py:62
  79.2 1.3 multiply_reduce_fusion.1
  80.7 0.3 convolution_convert_fusion.3
  81.2 0.9 fusion.38
  82.2 2.8 fusion.5
  85.3 2.2 fusion.9
  87.7 0.8 copy.55
  88.6 0.4 copy.51
  89.2 0.3 reshape.174
  89.5 0.3 convolution_bitcast_fusion.1
  89.8 1.3 copy.52
  91.2 1.6 fusion.3
  93.0 2.5 copy.80
  95.5 1.4 fusion.4
  96.9 1.3 copy-done.8
  98.2 2.4 fusion.13
  100.6 3.2 %copy.54 = f32[1024,2,4,64]{3,2,1,0:T(4,128)} copy(f32[1024,2,4,64]{0,3,1,2:T(8,128)S(1)} %fusion.13) | data formatting | bytes 4194304 | tf_op jit(solution)/shard_map/dot_general | solution.py:244
  103.8 4.7 %concatenate.18 = f32[64,2,8,512]{3,2,1,0:T(8,128)S(1)} reshape(f32[1024,2,4,64]{3,2,1,0:T(4,128)} %copy.54) | data formatting | bytes 4194304 | tf_op jit(solution)/shard_map/concatenate | solution.py:280
  108.5 1.2 fusion.18
  109.8 0.3 fusion.34
  110.1 3.6 %convolution_add_fusion = f32[2048,1024]{1,0:T(8,128)S(1)} fusion(f32[2048,1024]{1,0:T(8,128)S(1)} %fusion.18, f32[64,1024]{1,0:T(8,128)S(1)} %fusion.38, s32[64]{0:T(128)S(1)} %copy-done.20, pred[64]{0:T(512)(128)(4,1)S(1)} %compare_and_fusion), kind=kOutput, calls=%fused_computation.2 | convolution fusion | flops 1612972032 | bytes 17039680 | tf_op jit(solution)/shard_map/dot_general | solution.py:267
  113.8 6.0 %pad_maximum_fusion = f32[64,7,8,1024]{3,2,1,0:T(8,128)} fusion(f32[64,1,8,1024]{3,2,1,0:T(8,128)S(1)} %bitcast.134, f32[64,2,8,256]{3,2,1,0:T(8,128)S(1)} %fusion.34, f32[64,2,8,512]{3,2,1,0:T(8,128)S(1)} %concatenate.18, f32[64,2,8,256]{3,2,1,0:T(8,128)S(1)} %bitcast.136, f32[64,4,8,1024]{3,2,1,0:T(8,128)S(1)} %bitcast.130), kind=kLoop, calls=%fused_computation.1 | loop fusion | flops 14680064 | bytes 29360128 | tf_op jit(solution)/shard_map/concatenate | solution.py:290
  119.8 1.4 copy-done.5
  121.2 0.3 fusion.20
  121.4 5.4 %convolution_bitcast_fusion = f32[64,32,1024]{2,1,0:T(8,128)S(1)} fusion(bf16[1024,2,4,64,1]{0,3,2,4,1:T(8,128)(2,1)} %bitcast.140, bf16[64,32,1,4,64]{4,1,3,0,2:T(8,128)(2,1)} %copy-done.8, bf16[64,32,1,4,64]{4,1,3,0,2:T(8,128)(2,1)} %copy-done.7), kind=kOutput, calls=%fused_computation.9 | convolution fusion | flops 2148532224 | bytes 11534336 | tf_op jit(solution)/shard_map/dot_general | solution.py:249
  126.8 3.3 %copy-done.2 = f32[64,32,1024]{2,1,0:T(8,128)} copy-done((f32[64,32,1024]{2,1,0:T(8,128)}, f32[64,32,1024]{2,1,0:T(8,128)S(1)}, u32[]{:S(2)}) %copy-start.2) | copy-done | bytes 8388632
  130.1 0.3 slice_add_fusion
  130.4 6.1 %scatter-add.4 = f32[64,32,1024]{2,1,0:T(8,128)} dynamic-update-slice(f32[64,32,1024]{2,1,0:T(8,128)} %copy-done.2, f32[64,1,1024]{2,1,0:T(1,128)S(1)} %slice_add_fusion, s32[]{:T(128)} %constant.54.clone.1, s32[]{:T(128)} %constant.54.clone.1, s32[]{:T(128)} %constant.54.clone.1) | dynamic-update-slice | bytes 524292 | tf_op jit(solution)/shard_map/scatter-add | solution.py:257
  136.5 6.5 %convert_element_type.96.y_ref = bf16[64,32,1024]{2,1,0:T(8,128)(2,1)} convert(f32[64,32,1024]{2,1,0:T(8,128)} %scatter-add.4) | non-fusion elementwise | flops 2097152 | bytes 12582912 | tf_op jit(solution)/shard_map/convert_element_type | solution.py:257
  143.0 0.6 constant_dynamic-slice_fusion.resid_ref
  143.6 51.1 %shard_map.140 = bf16[16,32,1024]{2,1,0:T(8,128)(2,1)} custom-call(bf16[64,32,1024]{2,1,0:T(8,128)(2,1)} %convert_element_type.96.y_ref, f32[16,1024]{1,0:T(8,128)} %constant_dynamic-slice_fusion.resid_ref), custom_call_target="tpu_custom_call" | custom-call | tf_op jit(solution)/shard_map/pallas_call | solution.py:126
  194.7 91.1 %reduce-scatter.4.cloned.1.call-done = f32[7,8,1024]{2,1,0:T(8,128)} async-done(((f32[448,8,1024]{2,1,0:T(8,128)}), f32[7,8,1024]{2,1,0:T(8,128)}) %reduce-scatter.4.cloned.1.call-update) | async-done | bytes 229392
  285.9 0.8 slice.94
  286.6 0.8 slice_bitcast_fusion.3
  287.5 0.9 slice_bitcast_fusion.2
  288.4 0.6 slice_bitcast_fusion.4
  289.0 0.7 copy.60
  289.7 0.6 copy.102
  290.4 2.1 slice.82
  292.5 0.6 copy.59
  293.1 2.3 copy.105
  (83 shorter events, 3.0 us)
Async XLA Ops:
  7.2 26.4 %copy-start = (bf16[256,1024]{1,0:T(8,128)(2,1)S(1)}, bf16[256,1024]{1,0:T(8,128)(2,1)}, u32[]{:S(2)}) copy-start(bf16[256,1024]{1,0:T(8,128)(2,1)} %param.14) | copy-start | bytes 1572868
  7.2 4.4 %slice-start = ((bf16[1024,3,256]{2,0,1:T(8,128)(2,1)}), bf16[1024,2,256]{2,0,1:T(8,128)(2,1)S(1)}, s32[]{:S(2)}) async-start(bf16[1024,3,256]{2,0,1:T(8,128)(2,1)} %param.13), calls=%async_computation.2 | async-start | bytes 2097152 | tf_op jit(solution)/shard_map/slice | solution.py:162
  7.2 278.7 %reduce-scatter.4.cloned.1.call-start = ((), (), s32[]{:S(2)}) async-start(), calls=%async_computation.1 | async-start | bytes 14909440
  24.8 1.3 copy-start.9
  24.8 2.8 copy-start.10
  24.8 4.4 %copy-start.22 = (s32[64]{0:T(128)S(1)}, s32[64]{0:T(128)}, u32[]{:S(2)}) copy-start(s32[64]{0:T(128)} %param.19) | copy-start | bytes 772
  24.8 4.4 %copy-start.23 = (s32[1,4]{1,0:T(1,128)S(1)}, s32[1,4]{1,0:T(1,128)}, u32[]{:S(2)}) copy-start(s32[1,4]{1,0:T(1,128)} %param.21) | copy-start | bytes 52
  24.8 4.5 %copy-start.21 = (s32[64]{0:T(128)S(1)}, s32[64]{0:T(128)}, u32[]{:S(2)}) copy-start(s32[64]{0:T(128)} %param.20) | copy-start | bytes 772
  27.3 26.0 %copy-start.17 = (f32[1024]{0:T(1024)S(1)}, f32[1024]{0:T(1024)}, u32[]{:S(2)}) copy-start(f32[1024]{0:T(1024)} %param.15) | copy-start | bytes 12292
  27.3 26.0 %copy-start.19 = (f32[1024]{0:T(1024)S(1)}, f32[1024]{0:T(1024)}, u32[]{:S(2)}) copy-start(f32[1024]{0:T(1024)} %param.16) | copy-start | bytes 12292
  54.6 24.6 %copy-start.14 = (f32[64,64]{0,1:T(8,128)}, f32[64,64]{0,1:T(8,128)S(1)}, u32[]{:S(2)}) copy-start(f32[64,64]{0,1:T(8,128)S(1)} %get-tuple-element.49) | copy-start | bytes 49156
  54.6 24.6 %copy-start.6 = (f32[128,1024]{1,0:T(8,128)S(1)}, f32[128,1024]{1,0:T(8,128)}, u32[]{:S(2)}) copy-start(f32[128,1024]{1,0:T(8,128)} %shard_map.137) | copy-start | bytes 1572868
  66.6 15.6 %copy-start.15 = (bf16[64,4,64]{2,1,0:T(4,128)(2,1)S(1)}, bf16[64,4,64]{2,1,0:T(4,128)(2,1)}, u32[]{:S(2)}) copy-start(bf16[64,4,64]{2,1,0:T(4,128)(2,1)} %reshape.163) | copy-start | bytes 98308
  87.7 5.1 %copy-start.12 = (bf16[64,256]{1,0:T(8,128)(2,1)}, bf16[64,256]{1,0:T(8,128)(2,1)S(1)}, u32[]{:S(2)}) copy-start(bf16[64,256]{1,0:T(8,128)(2,1)S(1)} %convert_element_type.95) | copy-start | bytes 98308
  92.8 4.1 %copy-start.7 = (bf16[64,32,1,4,64]{4,1,3,0,2:T(8,128)(2,1)}, bf16[64,32,1,4,64]{4,1,3,0,2:T(8,128)(2,1)S(1)}, u32[]{:S(2)}) copy-start(bf16[64,32,1,4,64]{4,1,3,0,2:T(8,128)(2,1)S(1)} %fusion.3) | copy-start | bytes 3145732
  92.8 5.4 %copy-start.18 = (bf16[64,32,1024]{2,1,0:T(8,128)(2,1)S(1)}, bf16[64,32,1024]{2,1,0:T(8,128)(2,1)}, u32[]{:S(2)}) copy-start(bf16[64,32,1024]{2,1,0:T(8,128)(2,1)} %param.12) | copy-start | bytes 12582916
  96.9 1.3 copy-start.8
  108.5 1.3 copy-start.11
  108.5 1.3 copy-start.16
  108.5 1.5 copy-start.20
  110.1 3.7 %copy-start.3 = (f32[8,8,8,1024]{3,2,1,0:T(8,128)S(1)}, f32[8,8,8,1024]{3,2,1,0:T(8,128)}, u32[]{:S(2)}) copy-start(f32[8,8,8,1024]{3,2,1,0:T(8,128)} %copy.80) | copy-start | bytes 6291460
  110.1 3.7 %copy-start.4 = (f32[1024,256]{1,0:T(8,128)S(1)}, f32[1024,256]{1,0:T(8,128)}, u32[]{:S(2)}) copy-start(f32[1024,256]{1,0:T(8,128)} %copy.52) | copy-start | bytes 3145732
  119.7 1.4 copy-start.5
  119.7 1.4 copy-start.13
  126.8 3.3 %copy-start.2 = (f32[64,32,1024]{2,1,0:T(8,128)}, f32[64,32,1024]{2,1,0:T(8,128)S(1)}, u32[]{:S(2)}) copy-start(f32[64,32,1024]{2,1,0:T(8,128)S(1)} %convolution_bitcast_fusion) | copy-start | bytes 25165828
  143.0 152.4 %copy-start.1 = (bf16[256,1024]{1,0:T(8,128)(2,1)S(1)}, bf16[256,1024]{1,0:T(8,128)(2,1)}, u32[]{:S(2)}) copy-start(bf16[256,1024]{1,0:T(8,128)(2,1)} %param.14) | copy-start | bytes 1572868
Sparse Core Ops, SparseCore 0:
  119.9 165.9 reduce-scatter.3

commit v8 on v7

--- a/solution.py
+++ b/solution.py
@@ -161,10 +161,12 @@
     w_query = w_qkv[:, 0, :]
     w_keyval = w_qkv[:, 1:, :].reshape(width, 2 * local_cols)
     query = jnp.dot(cls_rows, w_query, preferred_element_type=jnp.float32).astype(jnp.bfloat16)
-    keyval = jnp.dot(
-        hidden_in.reshape(ment_rows * seq_len, width), w_keyval, preferred_element_type=jnp.float32
-    )
-    keyval = keyval.astype(jnp.bfloat16).reshape(ment_rows, seq_len, 2, local_heads, HD)
+    keyval = lax.dot_general(
+        hidden_in,
+        w_keyval.reshape(width, 2, local_heads, HD),
+        (((2,), (0,)), ((), ())),
+        preferred_element_type=jnp.float32,
+    ).astype(jnp.bfloat16)
     key_heads = keyval[:, :, 0]
     value_heads = keyval[:, :, 1]
     query_heads = query.reshape(ment_rows, local_heads, HD)

time: 306 us -> 297 us (0.971)
  local copies, waits for them, and re-layouts: 53.2 us -> 43.3 us
    reshape x1 -> x0, local copies, waits for them, and re-layouts: 3.64 us -> none  [on_device(): keyval.astype(jnp.bfloat16).reshape(ment_rows, seq_len, 2, local_heads, HD)]
    squeeze x1 -> x0, local copies, waits for them, and re-layouts: 3.38 us -> none  [on_device(): value_heads = keyval[:, :, 1]]
    unnamed x56 -> x45, local copies, waits for them, and re-layouts: 15 us -> 12.4 us
  transfers between devices with their start and end apart: 1 -> 1, of which waited for: 1 -> 1; matrix products, arithmetic and copies ran while one was open for 6% -> 7% of each run, Pallas kernels for 17% -> 17%
where the time goes in v8:
time: 297 us; the launch traced here: 294 us
  waiting for transfers between devices  91.1 us (31%)
  Pallas kernels  84.2 us (28%)
  local copies, waits for them, and re-layouts  43.3 us (15%)
  matrix products  39.6 us (13%)
  other arithmetic  20.8 us (7%)
  between operations  14.6 us (5%)
    unnamed x2, waiting for transfers between devices  91.1 us
    pallas_call x1, Pallas kernels, peer_scatter(): pl.pallas_call(functools.partial(_peer_scatter_kernel, n), out_shape=jax....  51.1 us
    pallas_call x3, Pallas kernels, peer_sum(): pl.pallas_call(functools.partial(_peer_sum_kernel, n), out_shape=jax.Shap...  33.1 us
    unnamed x45, local copies, waits for them, and re-layouts  12.4 us
    dot_general x8, matrix products, contract(): lax.dot_general(left, right, (((left_dim,), (right_dim,)), ((), ())), pre...  8.19 us
    dot_general x1, matrix products, on_device(): lax.dot_general(hidden_in, w_keyval.reshape(width, 2, local_heads, HD), (...  6.72 us
    convert_element_type x1, other arithmetic, on_device(): token_term.at[:, 0, :].add(contract(query_gradient, w_query, 1, 1))  6.5 us
    scatter-add x1, local copies, waits for them, and re-layouts, on_device(): token_term.at[:, 0, :].add(contract(query_gradient, w_query, 1, 1))  6.07 us
  transfers between devices with their start and end apart: 1, of which 1 were waited for; matrix products, arithmetic and copies ran while one was open for 7% of the time, Pallas kernels for 17%

profile of v8, /device:TPU:1, one launch (start us, length us, event | category | flops | bytes accessed | tf_op | source)
XLA Modules:
  0.0 293.8 jit_solution(1066919835756112307)
XLA Ops:
  7.2 1.5 slice.69
  8.8 1.2 convolution_convert_fusion.3
  10.2 0.7 fusion.37
  11.0 0.5 copy.50
  11.5 6.7 %fusion.5 = bf16[64,32,2,4,64]{4,1,3,2,0:T(8,128)(2,1)S(1)} fusion(bf16[1024,2,4,64,1]{0,3,2,1,4:T(8,128)(2,1)S(1)} %bitcast.146, bf16[64,32,1024]{2,1,0:T(8,128)(2,1)} %param.12), kind=kOutput, calls=%fused_computation.12 | convolution fusion | flops 2148532224 | bytes 7340032 | tf_op jit(solution)/shard_map/dot_general | solution.py:164
  18.3 1.2 fusion.11
  19.5 0.2 fusion.32
  19.8 0.7 fusion.13
  20.5 0.7 reshape.188
  21.6 3.5 %gather_fusion = bf16[64,1024]{1,0:T(8,128)(2,1)S(1)} fusion(bf16[2048,1024]{1,0:T(8,128)(2,1)} %bitcast.138, s32[1024]{0:T(1024)S(1)} %pad_clamp_fusion), kind=kCustom, calls=%fused_computation | custom fusion | bytes 262400 | tf_op jit(solution)/shard_map/gather | solution.py:190
  25.2 0.2 convolution_convert_fusion.1
  25.4 0.7 pad_maximum_fusion.2.x_ref
  26.2 17.5 %shard_map.137 = f32[128,1024]{1,0:T(8,128)} custom-call(bf16[128,1024]{1,0:T(8,128)(2,1)} %pad_maximum_fusion.2.x_ref), custom_call_target="tpu_custom_call" | custom-call | tf_op jit(solution)/shard_map/pallas_call | solution.py:62
  43.7 1.1 fusion.40
  44.8 0.2 multiply_reduce_fusion.3
  45.1 1.1 exponential_reduce_fusion
  46.3 3.8 %multiply_reduce_fusion = (f32[64]{0:T(128)S(1)}, f32[64,2048]{1,0:T(8,128)S(1)}) fusion(f32[2048]{0:T(1024)S(1)} %bitcast.157, bf16[64,1024]{1,0:T(8,128)(2,1)S(1)} %add_convert_fusion, bf16[2048,1024]{1,0:T(8,128)(2,1)} %bitcast.139), kind=kOutput, calls=%fused_computation.35 | convolution fusion | flops 268697536 | bytes 4858112 | tf_op jit(solution)/shard_map/dot_general | solution.py:145
  50.1 0.6 pad.10.x_ref
  50.7 6.7 %shard_map.138 = f32[8,64]{1,0:T(8,128)} custom-call(f32[8,64]{1,0:T(8,128)} %pad.10.x_ref), custom_call_target="tpu_custom_call" | custom-call | tf_op jit(solution)/shard_map/pallas_call | solution.py:62
  57.4 0.7 fusion.38
  58.2 3.7 %convolution_convert_fusion.x_ref = bf16[64,1024]{1,0:T(8,128)(2,1)} fusion(bf16[64,2048]{1,0:T(8,128)(2,1)S(1)} %multiply_convert_fusion.2, bf16[2048,1024]{1,0:T(8,128)(2,1)} %bitcast.140), kind=kOutput, calls=%fused_computation.24 | convolution fusion | flops 268500992 | bytes 4587520 | tf_op jit(solution)/shard_map/dot_general | solution.py:213
  61.9 8.9 %shard_map.139 = f32[64,1024]{1,0:T(8,128)} custom-call(bf16[64,1024]{1,0:T(8,128)(2,1)} %convolution_convert_fusion.x_ref), custom_call_target="tpu_custom_call" | custom-call | tf_op jit(solution)/shard_map/pallas_call | solution.py:62
  70.8 1.3 multiply_reduce_fusion.1
  72.3 0.3 convolution_convert_fusion.2
  72.8 0.2 fusion.39
  73.0 2.8 fusion.12
  76.1 2.2 fusion.10
  78.4 0.7 convert_element_type.95
  79.2 0.2 copy.55
  79.4 0.4 copy.51
  79.8 0.2 copy.56
  80.1 0.3 reshape.162
  80.3 1.1 convolution_bitcast_fusion.1
  81.4 1.3 copy.52
  82.7 1.8 fusion.8
  84.7 2.5 copy.78
  87.2 1.4 fusion.9
  88.7 1.3 copy-done.8
  90.0 2.4 fusion.14
  92.4 3.2 %copy.54 = f32[1024,2,4,64]{3,2,1,0:T(4,128)} copy(f32[1024,2,4,64]{0,3,1,2:T(8,128)S(1)} %fusion.14) | data formatting | bytes 4194304 | tf_op jit(solution)/shard_map/dot_general | solution.py:246
  95.6 4.5 %concatenate.18 = f32[64,2,8,512]{3,2,1,0:T(8,128)S(1)} reshape(f32[1024,2,4,64]{3,2,1,0:T(4,128)} %copy.54) | data formatting | bytes 4194304 | tf_op jit(solution)/shard_map/concatenate | solution.py:282
  100.1 1.2 fusion.19
  101.3 0.3 fusion.35
  101.6 3.6 %convolution_add_fusion = f32[2048,1024]{1,0:T(8,128)S(1)} fusion(f32[2048,1024]{1,0:T(8,128)S(1)} %fusion.19, f32[64,1024]{1,0:T(8,128)S(1)} %fusion.39, s32[64]{0:T(128)S(1)} %get-tuple-element.44, pred[64]{0:T(512)(128)(4,1)S(1)} %compare_and_fusion), kind=kOutput, calls=%fused_computation.2 | convolution fusion | flops 1612972032 | bytes 17039680 | tf_op jit(solution)/shard_map/dot_general | solution.py:269
  105.3 6.0 %pad_maximum_fusion = f32[64,7,8,1024]{3,2,1,0:T(8,128)} fusion(f32[64,1,8,1024]{3,2,1,0:T(8,128)S(1)} %bitcast.141, f32[64,2,8,256]{3,2,1,0:T(8,128)S(1)} %fusion.35, f32[64,2,8,512]{3,2,1,0:T(8,128)S(1)} %concatenate.18, f32[64,2,8,256]{3,2,1,0:T(8,128)S(1)} %bitcast.143, f32[64,4,8,1024]{3,2,1,0:T(8,128)S(1)} %bitcast.137), kind=kLoop, calls=%fused_computation.1 | loop fusion | flops 14680064 | bytes 29360128 | tf_op jit(solution)/shard_map/concatenate | solution.py:292
  111.3 1.4 copy-done.5
  112.7 0.3 fusion.21
  113.0 5.4 %convolution_bitcast_fusion = f32[64,32,1024]{2,1,0:T(8,128)S(1)} fusion(bf16[1024,2,4,64,1]{0,3,2,4,1:T(8,128)(2,1)} %bitcast.147, bf16[64,32,1,4,64]{4,1,3,0,2:T(8,128)(2,1)} %copy-done.8, bf16[64,32,1,4,64]{4,1,3,0,2:T(8,128)(2,1)} %copy-done.7), kind=kOutput, calls=%fused_computation.11 | convolution fusion | flops 2148532224 | bytes 11534336 | tf_op jit(solution)/shard_map/dot_general | solution.py:251
  118.4 3.3 %copy-done.2 = f32[64,32,1024]{2,1,0:T(8,128)} copy-done((f32[64,32,1024]{2,1,0:T(8,128)}, f32[64,32,1024]{2,1,0:T(8,128)S(1)}, u32[]{:S(2)}) %copy-start.2) | copy-done | bytes 8388632
  121.7 0.3 slice_add_fusion
  122.0 6.1 %scatter-add.4 = f32[64,32,1024]{2,1,0:T(8,128)} dynamic-update-slice(f32[64,32,1024]{2,1,0:T(8,128)} %copy-done.2, f32[64,1,1024]{2,1,0:T(1,128)S(1)} %slice_add_fusion, s32[]{:T(128)} %constant.54.clone.1, s32[]{:T(128)} %constant.54.clone.1, s32[]{:T(128)} %constant.54.clone.1) | dynamic-update-slice | bytes 524292 | tf_op jit(solution)/shard_map/scatter-add | solution.py:259
  128.0 6.5 %convert_element_type.96.y_ref = bf16[64,32,1024]{2,1,0:T(8,128)(2,1)} convert(f32[64,32,1024]{2,1,0:T(8,128)} %scatter-add.4) | non-fusion elementwise | flops 2097152 | bytes 12582912 | tf_op jit(solution)/shard_map/convert_element_type | solution.py:259
  134.5 0.6 constant_dynamic-slice_fusion.resid_ref
  135.2 51.1 %shard_map.140 = bf16[16,32,1024]{2,1,0:T(8,128)(2,1)} custom-call(bf16[64,32,1024]{2,1,0:T(8,128)(2,1)} %convert_element_type.96.y_ref, f32[16,1024]{1,0:T(8,128)} %constant_dynamic-slice_fusion.resid_ref), custom_call_target="tpu_custom_call" | custom-call | tf_op jit(solution)/shard_map/pallas_call | solution.py:126
  186.3 91.1 %reduce-scatter.4.cloned.1.call-done = f32[7,8,1024]{2,1,0:T(8,128)} async-done(((f32[448,8,1024]{2,1,0:T(8,128)}), f32[7,8,1024]{2,1,0:T(8,128)}) %reduce-scatter.4.cloned.1.call-update) | async-done | bytes 229392
  277.4 0.8 slice.94
  278.2 0.8 slice_bitcast_fusion.7
  279.0 0.9 slice_bitcast_fusion.6
  279.9 0.6 slice_bitcast_fusion.8
  280.5 0.7 copy.60
  281.3 0.6 copy.92
  281.9 2.1 slice.82
  284.0 0.6 copy.59
  284.6 2.3 copy.95
  (71 shorter events, 2.2 us)
Async XLA Ops:
  7.2 18.1 %copy-start = (bf16[256,1024]{1,0:T(8,128)(2,1)S(1)}, bf16[256,1024]{1,0:T(8,128)(2,1)}, u32[]{:S(2)}) copy-start(bf16[256,1024]{1,0:T(8,128)(2,1)} %param.14) | copy-start | bytes 1572868
  7.2 3.8 %slice-start = ((bf16[1024,3,256]{2,0,1:T(8,128)(2,1)}), bf16[1024,2,256]{2,0,1:T(8,128)(2,1)S(1)}, s32[]{:S(2)}) async-start(bf16[1024,3,256]{2,0,1:T(8,128)(2,1)} %param.13), calls=%async_computation.2 | async-start | bytes 2097152 | tf_op jit(solution)/shard_map/slice | solution.py:162
  7.2 270.2 %reduce-scatter.4.cloned.1.call-start = ((), (), s32[]{:S(2)}) async-start(), calls=%async_computation.1 | async-start | bytes 14909440
  11.5 6.7 %copy-start.9 = (bf16[1024,2,256]{0,2,1:T(8,128)(2,1)}, bf16[1024,2,256]{0,2,1:T(8,128)(2,1)S(1)}, u32[]{:S(2)}) copy-start(bf16[1024,2,256]{0,2,1:T(8,128)(2,1)S(1)} %copy.50) | copy-start | bytes 3145732
  18.3 2.2 copy-start.18
  18.3 3.1 %copy-start.16 = (s32[64]{0:T(128)S(1)}, s32[64]{0:T(128)}, u32[]{:S(2)}) copy-start(s32[64]{0:T(128)} %param.19) | copy-start | bytes 772
  18.3 3.1 %copy-start.17 = (s32[1,4]{1,0:T(1,128)S(1)}, s32[1,4]{1,0:T(1,128)}, u32[]{:S(2)}) copy-start(s32[1,4]{1,0:T(1,128)} %param.21) | copy-start | bytes 52
  18.3 3.2 %copy-start.15 = (s32[64]{0:T(128)S(1)}, s32[64]{0:T(128)}, u32[]{:S(2)}) copy-start(s32[64]{0:T(128)} %param.20) | copy-start | bytes 772
  19.5 25.5 %copy-start.12 = (f32[1024]{0:T(1024)S(1)}, f32[1024]{0:T(1024)}, u32[]{:S(2)}) copy-start(f32[1024]{0:T(1024)} %param.15) | copy-start | bytes 12292
  19.5 25.5 %copy-start.14 = (f32[1024]{0:T(1024)S(1)}, f32[1024]{0:T(1024)}, u32[]{:S(2)}) copy-start(f32[1024]{0:T(1024)} %param.16) | copy-start | bytes 12292
  46.3 24.5 %copy-start.6 = (f32[128,1024]{1,0:T(8,128)S(1)}, f32[128,1024]{1,0:T(8,128)}, u32[]{:S(2)}) copy-start(f32[128,1024]{1,0:T(8,128)} %shard_map.137) | copy-start | bytes 1572868
  84.6 4.1 %copy-start.7 = (bf16[64,32,1,4,64]{4,1,3,0,2:T(8,128)(2,1)}, bf16[64,32,1,4,64]{4,1,3,0,2:T(8,128)(2,1)S(1)}, u32[]{:S(2)}) copy-start(bf16[64,32,1,4,64]{4,1,3,0,2:T(8,128)(2,1)S(1)} %fusion.8) | copy-start | bytes 3145732
  84.6 5.5 %copy-start.13 = (bf16[64,32,1024]{2,1,0:T(8,128)(2,1)S(1)}, bf16[64,32,1024]{2,1,0:T(8,128)(2,1)}, u32[]{:S(2)}) copy-start(bf16[64,32,1024]{2,1,0:T(8,128)(2,1)} %param.12) | copy-start | bytes 12582916
  88.7 1.4 copy-start.8
  100.1 1.2 copy-start.11
  101.6 3.7 %copy-start.3 = (f32[8,8,8,1024]{3,2,1,0:T(8,128)S(1)}, f32[8,8,8,1024]{3,2,1,0:T(8,128)}, u32[]{:S(2)}) copy-start(f32[8,8,8,1024]{3,2,1,0:T(8,128)} %copy.78) | copy-start | bytes 6291460
  101.6 3.7 %copy-start.4 = (f32[1024,256]{1,0:T(8,128)S(1)}, f32[1024,256]{1,0:T(8,128)}, u32[]{:S(2)}) copy-start(f32[1024,256]{1,0:T(8,128)} %copy.52) | copy-start | bytes 3145732
  111.3 1.4 copy-start.5
  111.3 1.4 copy-start.10
  118.4 3.3 %copy-start.2 = (f32[64,32,1024]{2,1,0:T(8,128)}, f32[64,32,1024]{2,1,0:T(8,128)S(1)}, u32[]{:S(2)}) copy-start(f32[64,32,1024]{2,1,0:T(8,128)S(1)} %convolution_bitcast_fusion) | copy-start | bytes 25165828
  134.5 152.4 %copy-start.1 = (bf16[256,1024]{1,0:T(8,128)(2,1)S(1)}, bf16[256,1024]{1,0:T(8,128)(2,1)}, u32[]{:S(2)}) copy-start(bf16[256,1024]{1,0:T(8,128)(2,1)} %param.14) | copy-start | bytes 1572868
Sparse Core Ops, SparseCore 0:
  111.4 165.9 reduce-scatter.3

commit v9 on v8

--- a/solution.py
+++ b/solution.py
@@ -74,7 +74,7 @@
     )(x)
 
 
-def _peer_scatter_kernel(n, y_ref, resid_ref, out_ref, recv, send_sem, recv_sem, own_sem):
+def _peer_scatter_kernel(n, y_ref, out_ref, recv, send_sem, recv_sem, own_sem):
     row = lax.axis_index("ment")
     me = lax.axis_index("ent")
     share = out_ref.shape[0]
@@ -107,26 +107,23 @@
     own.wait()
     for copy in sends:
         copy.wait_send()
-    first = lax.broadcasted_iota(jnp.int32, out_ref.shape[1:], 0) == 0
-
     def one_mention(i, carry):
         total = recv[0, i].astype(jnp.float32)
         for s in range(1, n):
             total = total + recv[s, i].astype(jnp.float32)
-        total = total + jnp.where(first, resid_ref[pl.ds(i, 1), :], 0.0)
-        out_ref[i] = total.astype(out_ref.dtype)
+        out_ref[i] = total
         return carry
 
     lax.fori_loop(0, share, one_mention, 0)
 
 
-def peer_scatter(y, resid, collective):
+def peer_scatter(y, collective):
     n = lax.axis_size("ent")
     share = y.shape[0] // n
     return pl.pallas_call(
         functools.partial(_peer_scatter_kernel, n),
-        out_shape=jax.ShapeDtypeStruct((share,) + y.shape[1:], jnp.bfloat16),
-        in_specs=[pl.BlockSpec(memory_space=pltpu.VMEM)] * 2,
+        out_shape=jax.ShapeDtypeStruct((share,) + y.shape[1:], jnp.float32),
+        in_specs=[pl.BlockSpec(memory_space=pltpu.VMEM)],
         out_specs=pl.BlockSpec(memory_space=pltpu.VMEM),
         scratch_shapes=[
             pltpu.VMEM((n, share) + y.shape[1:], y.dtype),
@@ -135,7 +132,7 @@
             pltpu.SemaphoreType.DMA(()),
         ],
         compiler_params=pltpu.CompilerParams(collective_id=collective, has_side_effects=True),
-    )(y, resid)
+    )(y)
 
 
 ln_eps = 1e-06
@@ -255,11 +252,11 @@
         preferred_element_type=jnp.float32,
     )
     resid_mine = lax.dynamic_slice_in_dim(d_resid, owner * share, share, 0)
-    grad_hidden = peer_scatter(
+    summed = peer_scatter(
         token_term.at[:, 0, :].add(contract(query_gradient, w_query, 1, 1)).astype(jnp.bfloat16),
-        resid_mine,
         3,
     )
+    grad_hidden = summed.at[:, 0, :].add(resid_mine).astype(jnp.bfloat16)
     gold_terms = contract(w_inb, embed, 0, 0)
     neg_weights = (
         w_neg.reshape(ment_rows, own_blocks, block_rows).transpose(0, 2, 1).reshape(ment_rows, -1)
@@ -297,7 +294,7 @@
     merged = lax.optimization_barrier(merged)
     table_sum = merged[: counts[0]]
     rows_sum = merged[counts[0] : counts[0] + counts[1]].reshape(qkv_rows, -1)
-    ln_sum = merged[counts[0] + counts[1] :].reshape(-1)[: ln_flat.shape[1]]
+    ln_sum = merged[counts[0] + counts[1], 0, : ln_flat.shape[1]]
     grad_table = table_sum.transpose(1, 0, 2)
     grad_qkv = rows_sum[:, : 3 * local_cols].reshape(qkv_rows, 3, local_cols)
     grad_wo = rows_sum[:, 3 * local_cols :].T

time: 297 us -> 293 us (0.987)
  waiting for transfers between devices: 91.1 us -> 85.6 us
  other arithmetic: 20.8 us -> 24.7 us
  local copies, waits for them, and re-layouts: 43.3 us -> 40.3 us
    unnamed x2, waiting for transfers between devices: 91.1 us -> 85.6 us
    unnamed x45 -> x44, local copies, waits for them, and re-layouts: 12.4 us -> 10.1 us
  transfers between devices with their start and end apart: 1 -> 1, of which waited for: 1 -> 1; matrix products, arithmetic and copies ran while one was open for 7% -> 8% of each run, Pallas kernels for 17% -> 18%
where the time goes in v9:
time: 293 us; the launch traced here: 289 us
  waiting for transfers between devices  85.6 us (29%)
  Pallas kernels  84.5 us (29%)
  local copies, waits for them, and re-layouts  40.3 us (14%)
  matrix products  39.6 us (14%)
  other arithmetic  24.7 us (8%)
  between operations  14.6 us (5%)
    unnamed x2, waiting for transfers between devices  85.6 us
    pallas_call x1, Pallas kernels, peer_scatter(): pl.pallas_call(functools.partial(_peer_scatter_kernel, n), out_shape=jax....  51.4 us
    pallas_call x3, Pallas kernels, peer_sum(): pl.pallas_call(functools.partial(_peer_sum_kernel, n), out_shape=jax.Shap...  33.1 us
    unnamed x44, local copies, waits for them, and re-layouts  10.1 us
    dot_general x8, matrix products, contract(): lax.dot_general(left, right, (((left_dim,), (right_dim,)), ((), ())), pre...  8.19 us
    dot_general x1, matrix products, on_device(): lax.dot_general(hidden_in, w_keyval.reshape(width, 2, local_heads, HD), (...  6.72 us
    convert_element_type x1, other arithmetic, on_device(): token_term.at[:, 0, :].add(contract(query_gradient, w_query, 1, 1))  6.54 us
    scatter-add x1, local copies, waits for them, and re-layouts, on_device(): token_term.at[:, 0, :].add(contract(query_gradient, w_query, 1, 1))  6.07 us
  transfers between devices with their start and end apart: 1, of which 1 were waited for; matrix products, arithmetic and copies ran while one was open for 8% of the time, Pallas kernels for 18%

profile of v9, /device:TPU:1, one launch (start us, length us, event | category | flops | bytes accessed | tf_op | source)
XLA Modules:
  0.0 289.4 jit_solution(7348907479860581115)
XLA Ops:
  7.2 1.5 slice.85
  8.8 1.2 convolution_convert_fusion.3
  10.2 0.7 fusion.37
  11.0 0.5 copy.50
  11.5 6.7 %fusion.5 = bf16[64,32,2,4,64]{4,1,3,2,0:T(8,128)(2,1)S(1)} fusion(bf16[1024,2,4,64,1]{0,3,2,1,4:T(8,128)(2,1)S(1)} %bitcast.145, bf16[64,32,1024]{2,1,0:T(8,128)(2,1)} %param.14), kind=kOutput, calls=%fused_computation.12 | convolution fusion | flops 2148532224 | bytes 7340032 | tf_op jit(solution)/shard_map/dot_general | solution.py:161
  18.3 1.2 fusion.11
  19.5 0.2 fusion.32
  19.8 0.7 fusion.13
  20.5 0.7 reshape.214
  21.6 3.5 %gather_fusion = bf16[64,1024]{1,0:T(8,128)(2,1)S(1)} fusion(bf16[2048,1024]{1,0:T(8,128)(2,1)} %bitcast.137, s32[1024]{0:T(1024)S(1)} %pad_clamp_fusion), kind=kCustom, calls=%fused_computation | custom fusion | bytes 262400 | tf_op jit(solution)/shard_map/gather | solution.py:187
  25.2 0.2 convolution_convert_fusion.1
  25.4 0.7 pad_maximum_fusion.2.x_ref
  26.2 17.5 %shard_map.137 = f32[128,1024]{1,0:T(8,128)} custom-call(bf16[128,1024]{1,0:T(8,128)(2,1)} %pad_maximum_fusion.2.x_ref), custom_call_target="tpu_custom_call" | custom-call | tf_op jit(solution)/shard_map/pallas_call | solution.py:62
  43.7 1.1 fusion.40
  44.8 0.2 multiply_reduce_fusion.3
  45.1 1.1 exponential_reduce_fusion
  46.3 3.8 %multiply_reduce_fusion = (f32[64]{0:T(128)S(1)}, f32[64,2048]{1,0:T(8,128)S(1)}) fusion(f32[2048]{0:T(1024)S(1)} %bitcast.156, bf16[64,1024]{1,0:T(8,128)(2,1)S(1)} %add_convert_fusion, bf16[2048,1024]{1,0:T(8,128)(2,1)} %bitcast.138), kind=kOutput, calls=%fused_computation.35 | convolution fusion | flops 268697536 | bytes 4858112 | tf_op jit(solution)/shard_map/dot_general | solution.py:142
  50.1 0.6 pad.12.x_ref
  50.7 6.7 %shard_map.138 = f32[8,64]{1,0:T(8,128)} custom-call(f32[8,64]{1,0:T(8,128)} %pad.12.x_ref), custom_call_target="tpu_custom_call" | custom-call | tf_op jit(solution)/shard_map/pallas_call | solution.py:62
  57.4 0.7 fusion.38
  58.2 3.7 %convolution_convert_fusion.x_ref = bf16[64,1024]{1,0:T(8,128)(2,1)} fusion(bf16[64,2048]{1,0:T(8,128)(2,1)S(1)} %multiply_convert_fusion.2, bf16[2048,1024]{1,0:T(8,128)(2,1)} %bitcast.139), kind=kOutput, calls=%fused_computation.24 | convolution fusion | flops 268500992 | bytes 4587520 | tf_op jit(solution)/shard_map/dot_general | solution.py:210
  61.9 8.9 %shard_map.139 = f32[64,1024]{1,0:T(8,128)} custom-call(bf16[64,1024]{1,0:T(8,128)(2,1)} %convolution_convert_fusion.x_ref), custom_call_target="tpu_custom_call" | custom-call | tf_op jit(solution)/shard_map/pallas_call | solution.py:62
  70.8 1.3 multiply_reduce_fusion.1
  72.3 0.3 convolution_convert_fusion.2
  72.8 0.2 fusion.39
  73.0 2.8 fusion.12
  76.1 2.2 fusion.10
  78.4 0.7 convert_element_type.98
  79.2 0.2 copy.55
  79.4 0.4 copy.51
  79.8 0.2 copy.56
  80.1 0.3 reshape.188
  80.3 1.1 convolution_bitcast_fusion.1
  81.4 1.3 copy.52
  82.7 1.8 fusion.8
  84.7 2.5 copy.78
  87.2 1.4 fusion.9
  88.7 1.3 copy-done.8
  90.0 2.4 fusion.14
  92.4 3.2 %copy.54 = f32[1024,2,4,64]{3,2,1,0:T(4,128)} copy(f32[1024,2,4,64]{0,3,1,2:T(8,128)S(1)} %fusion.14) | data formatting | bytes 4194304 | tf_op jit(solution)/shard_map/dot_general | solution.py:243
  95.6 4.5 %concatenate.20 = f32[64,2,8,512]{3,2,1,0:T(8,128)S(1)} reshape(f32[1024,2,4,64]{3,2,1,0:T(4,128)} %copy.54) | data formatting | bytes 4194304 | tf_op jit(solution)/shard_map/concatenate | solution.py:279
  100.1 1.2 fusion.19
  101.3 0.3 fusion.35
  101.6 3.6 %convolution_add_fusion = f32[2048,1024]{1,0:T(8,128)S(1)} fusion(f32[2048,1024]{1,0:T(8,128)S(1)} %fusion.19, f32[64,1024]{1,0:T(8,128)S(1)} %fusion.39, s32[64]{0:T(128)S(1)} %get-tuple-element.61, pred[64]{0:T(512)(128)(4,1)S(1)} %compare_and_fusion), kind=kOutput, calls=%fused_computation.2 | convolution fusion | flops 1612972032 | bytes 17039680 | tf_op jit(solution)/shard_map/dot_general | solution.py:266
  105.3 6.0 %pad_maximum_fusion = f32[64,7,8,1024]{3,2,1,0:T(8,128)} fusion(f32[64,1,8,1024]{3,2,1,0:T(8,128)S(1)} %bitcast.140, f32[64,2,8,256]{3,2,1,0:T(8,128)S(1)} %fusion.35, f32[64,2,8,512]{3,2,1,0:T(8,128)S(1)} %concatenate.20, f32[64,2,8,256]{3,2,1,0:T(8,128)S(1)} %bitcast.142, f32[64,4,8,1024]{3,2,1,0:T(8,128)S(1)} %bitcast.136), kind=kLoop, calls=%fused_computation.1 | loop fusion | flops 14680064 | bytes 29360128 | tf_op jit(solution)/shard_map/concatenate | solution.py:289
  111.3 1.4 copy-done.5
  112.7 0.3 fusion.21
  113.0 5.4 %convolution_bitcast_fusion = f32[64,32,1024]{2,1,0:T(8,128)S(1)} fusion(bf16[1024,2,4,64,1]{0,3,2,4,1:T(8,128)(2,1)} %bitcast.146, bf16[64,32,1,4,64]{4,1,3,0,2:T(8,128)(2,1)} %copy-done.8, bf16[64,32,1,4,64]{4,1,3,0,2:T(8,128)(2,1)} %copy-done.7), kind=kOutput, calls=%fused_computation.11 | convolution fusion | flops 2148532224 | bytes 11534336 | tf_op jit(solution)/shard_map/dot_general | solution.py:248
  118.4 3.3 %copy-done.2 = f32[64,32,1024]{2,1,0:T(8,128)} copy-done((f32[64,32,1024]{2,1,0:T(8,128)}, f32[64,32,1024]{2,1,0:T(8,128)S(1)}, u32[]{:S(2)}) %copy-start.2) | copy-done | bytes 8388632
  121.7 0.3 slice_add_fusion
  122.0 6.1 %scatter-add.6 = f32[64,32,1024]{2,1,0:T(8,128)} dynamic-update-slice(f32[64,32,1024]{2,1,0:T(8,128)} %copy-done.2, f32[64,1,1024]{2,1,0:T(1,128)S(1)} %slice_add_fusion, s32[]{:T(128)} %constant.74.clone.1, s32[]{:T(128)} %constant.74.clone.1, s32[]{:T(128)} %constant.74.clone.1) | dynamic-update-slice | bytes 524292 | tf_op jit(solution)/shard_map/scatter-add | solution.py:256
  128.0 6.5 %convert_element_type.99.y_ref = bf16[64,32,1024]{2,1,0:T(8,128)(2,1)} convert(f32[64,32,1024]{2,1,0:T(8,128)} %scatter-add.6) | non-fusion elementwise | flops 2097152 | bytes 12582912 | tf_op jit(solution)/shard_map/convert_element_type | solution.py:256
  134.6 51.4 %shard_map.140 = f32[16,32,1024]{2,1,0:T(8,128)} custom-call(bf16[64,32,1024]{2,1,0:T(8,128)(2,1)} %convert_element_type.99.y_ref), custom_call_target="tpu_custom_call" | custom-call | tf_op jit(solution)/shard_map/pallas_call | solution.py:123
  186.0 1.1 reshape_add_fusion
  187.1 2.0 scatter-add.9
  189.1 2.7 convert_element_type.100
  191.8 85.6 %reduce-scatter.4.cloned.1.call-done = f32[7,8,1024]{2,1,0:T(8,128)} async-done(((f32[448,8,1024]{2,1,0:T(8,128)}), f32[7,8,1024]{2,1,0:T(8,128)}) %reduce-scatter.4.cloned.1.call-update) | async-done | bytes 229392
  277.4 0.7 slice_reduce_fusion
  278.1 0.8 slice_bitcast_fusion.7
  278.9 0.9 slice_bitcast_fusion.6
  279.9 0.6 slice_bitcast_fusion.8
  280.5 0.6 copy.59
  281.2 0.7 copy.60
  281.9 0.6 copy.92
  (72 shorter events, 2.3 us)
Async XLA Ops:
  7.2 18.1 %copy-start = (bf16[256,1024]{1,0:T(8,128)(2,1)S(1)}, bf16[256,1024]{1,0:T(8,128)(2,1)}, u32[]{:S(2)}) copy-start(bf16[256,1024]{1,0:T(8,128)(2,1)} %param.16) | copy-start | bytes 1572868
  7.2 3.8 %slice-start = ((bf16[1024,3,256]{2,0,1:T(8,128)(2,1)}), bf16[1024,2,256]{2,0,1:T(8,128)(2,1)S(1)}, s32[]{:S(2)}) async-start(bf16[1024,3,256]{2,0,1:T(8,128)(2,1)} %param.15), calls=%async_computation.2 | async-start | bytes 2097152 | tf_op jit(solution)/shard_map/slice | solution.py:159
  7.2 270.2 %reduce-scatter.4.cloned.1.call-start = ((), (), s32[]{:S(2)}) async-start(), calls=%async_computation.1 | async-start | bytes 14909440
  11.5 6.7 %copy-start.9 = (bf16[1024,2,256]{0,2,1:T(8,128)(2,1)}, bf16[1024,2,256]{0,2,1:T(8,128)(2,1)S(1)}, u32[]{:S(2)}) copy-start(bf16[1024,2,256]{0,2,1:T(8,128)(2,1)S(1)} %copy.50) | copy-start | bytes 3145732
  18.3 2.2 copy-start.18
  18.3 3.1 %copy-start.16 = (s32[64]{0:T(128)S(1)}, s32[64]{0:T(128)}, u32[]{:S(2)}) copy-start(s32[64]{0:T(128)} %param.21) | copy-start | bytes 772
  18.3 3.1 %copy-start.17 = (s32[1,4]{1,0:T(1,128)S(1)}, s32[1,4]{1,0:T(1,128)}, u32[]{:S(2)}) copy-start(s32[1,4]{1,0:T(1,128)} %param.23) | copy-start | bytes 52
  18.3 3.2 %copy-start.15 = (s32[64]{0:T(128)S(1)}, s32[64]{0:T(128)}, u32[]{:S(2)}) copy-start(s32[64]{0:T(128)} %param.22) | copy-start | bytes 772
  19.5 25.5 %copy-start.12 = (f32[1024]{0:T(1024)S(1)}, f32[1024]{0:T(1024)}, u32[]{:S(2)}) copy-start(f32[1024]{0:T(1024)} %param.17) | copy-start | bytes 12292
  19.5 25.5 %copy-start.14 = (f32[1024]{0:T(1024)S(1)}, f32[1024]{0:T(1024)}, u32[]{:S(2)}) copy-start(f32[1024]{0:T(1024)} %param.18) | copy-start | bytes 12292
  46.3 24.5 %copy-start.6 = (f32[128,1024]{1,0:T(8,128)S(1)}, f32[128,1024]{1,0:T(8,128)}, u32[]{:S(2)}) copy-start(f32[128,1024]{1,0:T(8,128)} %shard_map.137) | copy-start | bytes 1572868
  84.6 4.1 %copy-start.7 = (bf16[64,32,1,4,64]{4,1,3,0,2:T(8,128)(2,1)}, bf16[64,32,1,4,64]{4,1,3,0,2:T(8,128)(2,1)S(1)}, u32[]{:S(2)}) copy-start(bf16[64,32,1,4,64]{4,1,3,0,2:T(8,128)(2,1)S(1)} %fusion.8) | copy-start | bytes 3145732
  84.6 5.5 %copy-start.13 = (bf16[64,32,1024]{2,1,0:T(8,128)(2,1)S(1)}, bf16[64,32,1024]{2,1,0:T(8,128)(2,1)}, u32[]{:S(2)}) copy-start(bf16[64,32,1024]{2,1,0:T(8,128)(2,1)} %param.14) | copy-start | bytes 12582916
  88.7 1.4 copy-start.8
  100.1 1.2 copy-start.11
  101.6 3.7 %copy-start.3 = (f32[8,8,8,1024]{3,2,1,0:T(8,128)S(1)}, f32[8,8,8,1024]{3,2,1,0:T(8,128)}, u32[]{:S(2)}) copy-start(f32[8,8,8,1024]{3,2,1,0:T(8,128)} %copy.78) | copy-start | bytes 6291460
  101.6 3.7 %copy-start.4 = (f32[1024,256]{1,0:T(8,128)S(1)}, f32[1024,256]{1,0:T(8,128)}, u32[]{:S(2)}) copy-start(f32[1024,256]{1,0:T(8,128)} %copy.52) | copy-start | bytes 3145732
  111.3 1.4 copy-start.5
  111.3 1.4 copy-start.10
  118.4 3.3 %copy-start.2 = (f32[64,32,1024]{2,1,0:T(8,128)}, f32[64,32,1024]{2,1,0:T(8,128)S(1)}, u32[]{:S(2)}) copy-start(f32[64,32,1024]{2,1,0:T(8,128)S(1)} %convolution_bitcast_fusion) | copy-start | bytes 25165828
  128.0 154.5 %copy-start.1 = (bf16[256,1024]{1,0:T(8,128)(2,1)S(1)}, bf16[256,1024]{1,0:T(8,128)(2,1)}, u32[]{:S(2)}) copy-start(bf16[256,1024]{1,0:T(8,128)(2,1)} %param.16) | copy-start | bytes 1572868
Sparse Core Ops, SparseCore 0:
  111.4 165.9 reduce-scatter.3

commit v10 on v9

--- a/solution.py
+++ b/solution.py
@@ -241,8 +241,8 @@
     )
     d_keyval = jnp.stack([key_gradient, value_gradient], axis=2).astype(jnp.bfloat16)
     kv_term = lax.dot_general(
-        hidden_in, d_keyval, (((0, 1), (0, 1)), ((), ())), preferred_element_type=jnp.float32
-    ).reshape(width, 2 * local_cols)
+        d_keyval, hidden_in, (((0, 1), (0, 1)), ((), ())), preferred_element_type=jnp.float32
+    ).reshape(2 * local_cols, width).T
     query_term = contract(hidden_in[:, 0, :], query_gradient, 0, 0)
     share = ment_rows // lax.axis_size("ent")
     token_term = lax.dot_general(

time: 293 us -> 288 us (0.983)
  local copies, waits for them, and re-layouts: 40.3 us -> 32.6 us
  other arithmetic: 24.7 us -> 28.9 us
    dot_general x3 -> x0, local copies, waits for them, and re-layouts: 4.71 us -> none  [the longest x1 3.2 us: on_device(): lax.dot_general(hidden_in, d_keyval, (((0, 1), (0, 1)), ((), ())), prefer...]
    unnamed x44 -> x40, local copies, waits for them, and re-layouts: 10.1 us -> 7.56 us
  transfers between devices with their start and end apart: 1 -> 1, of which waited for: 1 -> 1; matrix products, arithmetic and copies ran while one was open for 8% -> 9% of each run, Pallas kernels for 18% -> 18%
where the time goes in v10:
time: 288 us; the launch traced here: 284 us
  waiting for transfers between devices  85.5 us (30%)
  Pallas kernels  84.5 us (29%)
  matrix products  38.4 us (13%)
  local copies, waits for them, and re-layouts  32.6 us (11%)
  other arithmetic  28.9 us (10%)
  between operations  14.6 us (5%)
    unnamed x2, waiting for transfers between devices  85.5 us
    pallas_call x1, Pallas kernels, peer_scatter(): pl.pallas_call(functools.partial(_peer_scatter_kernel, n), out_shape=jax....  51.4 us
    pallas_call x3, Pallas kernels, peer_sum(): pl.pallas_call(functools.partial(_peer_sum_kernel, n), out_shape=jax.Shap...  33.1 us
    dot_general x8, matrix products, contract(): lax.dot_general(left, right, (((left_dim,), (right_dim,)), ((), ())), pre...  8.48 us
    unnamed x40, local copies, waits for them, and re-layouts  7.56 us
    dot_general x1, matrix products, on_device(): lax.dot_general(hidden_in, w_keyval.reshape(width, 2, local_heads, HD), (...  6.73 us
    convert_element_type x1, other arithmetic, on_device(): token_term.at[:, 0, :].add(contract(query_gradient, w_query, 1, 1))  6.53 us
    scatter-add x1, local copies, waits for them, and re-layouts, on_device(): token_term.at[:, 0, :].add(contract(query_gradient, w_query, 1, 1))  6.07 us
  transfers between devices with their start and end apart: 1, of which 1 were waited for; matrix products, arithmetic and copies ran while one was open for 9% of the time, Pallas kernels for 18%

profile of v10, /device:TPU:1, one launch (start us, length us, event | category | flops | bytes accessed | tf_op | source)
XLA Modules:
  0.0 284.5 jit_solution(3924687902467888924)
XLA Ops:
  7.2 1.5 slice.85
  8.8 1.2 convolution_convert_fusion.3
  10.2 0.7 compare_and_fusion
  10.9 0.7 compare_reduce_fusion
  11.7 0.7 multiply_add_fusion
  12.4 0.7 fusion.31
  13.2 0.5 copy.67
  13.7 6.7 %fusion.4 = bf16[64,32,2,4,64]{4,1,3,2,0:T(8,128)(2,1)S(1)} fusion(bf16[1024,2,4,64,1]{0,3,2,1,4:T(8,128)(2,1)S(1)} %bitcast.144, bf16[64,32,1024]{2,1,0:T(8,128)(2,1)} %param.14), kind=kOutput, calls=%fused_computation.12 | convolution fusion | flops 2148532224 | bytes 7340032 | tf_op jit(solution)/shard_map/dot_general | solution.py:161
  20.5 1.2 fusion.10
  21.6 0.2 fusion.26
  22.0 0.7 fusion.12
  22.8 3.5 %gather_fusion = bf16[64,1024]{1,0:T(8,128)(2,1)S(1)} fusion(bf16[2048,1024]{1,0:T(8,128)(2,1)} %bitcast.135, s32[1024]{0:T(1024)S(1)} %pad_clamp_fusion), kind=kCustom, calls=%fused_computation | custom fusion | bytes 262400 | tf_op jit(solution)/shard_map/gather | solution.py:187
  26.4 0.2 convolution_convert_fusion.1
  26.6 0.7 pad_maximum_fusion.5.x_ref
  27.4 17.5 %shard_map.137 = f32[128,1024]{1,0:T(8,128)} custom-call(bf16[128,1024]{1,0:T(8,128)(2,1)} %pad_maximum_fusion.5.x_ref), custom_call_target="tpu_custom_call" | custom-call | tf_op jit(solution)/shard_map/pallas_call | solution.py:62
  44.9 1.1 fusion.36
  46.0 0.2 multiply_reduce_fusion.3
  46.3 1.1 exponential_reduce_fusion
  47.5 3.8 %multiply_reduce_fusion = (f32[64]{0:T(128)S(1)}, f32[64,2048]{1,0:T(8,128)S(1)}) fusion(f32[2048]{0:T(1024)S(1)} %bitcast.154, bf16[64,1024]{1,0:T(8,128)(2,1)S(1)} %add_convert_fusion, bf16[2048,1024]{1,0:T(8,128)(2,1)} %bitcast.136), kind=kOutput, calls=%fused_computation.34 | convolution fusion | flops 268697536 | bytes 4858112 | tf_op jit(solution)/shard_map/dot_general | solution.py:142
  51.3 0.6 pad.12.x_ref
  51.9 6.7 %shard_map.138 = f32[8,64]{1,0:T(8,128)} custom-call(f32[8,64]{1,0:T(8,128)} %pad.12.x_ref), custom_call_target="tpu_custom_call" | custom-call | tf_op jit(solution)/shard_map/pallas_call | solution.py:62
  58.6 0.7 fusion.32
  59.3 0.2 multiply_convert_fusion.2
  59.4 3.7 %convolution_convert_fusion.x_ref = bf16[64,1024]{1,0:T(8,128)(2,1)} fusion(bf16[64,2048]{1,0:T(8,128)(2,1)S(1)} %multiply_convert_fusion.2, bf16[2048,1024]{1,0:T(8,128)(2,1)} %bitcast.137), kind=kOutput, calls=%fused_computation.23 | convolution fusion | flops 268500992 | bytes 4587520 | tf_op jit(solution)/shard_map/dot_general | solution.py:210
  63.1 8.9 %shard_map.139 = f32[64,1024]{1,0:T(8,128)} custom-call(bf16[64,1024]{1,0:T(8,128)(2,1)} %convolution_convert_fusion.x_ref), custom_call_target="tpu_custom_call" | custom-call | tf_op jit(solution)/shard_map/pallas_call | solution.py:62
  72.0 1.3 multiply_reduce_fusion.1
  73.5 0.3 convolution_convert_fusion.2
  74.0 0.2 fusion.33
  74.2 1.3 fusion.27
  75.6 2.9 %fusion.11 = f32[64,4,1,32]{3,2,1,0:T(1,128)S(1)} fusion(bf16[64,4,64,1]{2,3,1,0:T(2,128)(2,1)S(1)} %reshape.217, bf16[64,32,2,4,64]{4,1,3,2,0:T(8,128)(2,1)} %copy-done.15), kind=kOutput, calls=%fused_computation.19 | convolution fusion | flops 1048576 | bytes 2162688 | tf_op jit(solution)/shard_map/ybn,yqbn->ybq/dot_general | solution.py:224
  78.4 0.2 multiply_reduce_fusion.5
  78.7 0.7 fusion.9
  79.6 0.4 copy.68
  80.1 0.2 copy.72
  80.3 0.3 reshape.188
  80.5 0.3 convolution_bitcast_fusion.1
  80.9 1.8 fusion.7
  82.9 1.2 copy.97
  84.1 1.4 fusion.8
  85.7 2.4 fusion
  88.1 2.2 pad_maximum_fusion.2
  90.3 5.3 %copy.71 = f32[1024,1024]{1,0:T(8,128)} copy(f32[1024,1024]{0,1:T(8,128)} %pad_maximum_fusion.2) | data formatting | bytes 8388608 | tf_op jit(solution)/shard_map/concatenate | solution.py:279
  95.7 1.2 fusion.13
  96.9 3.6 %convolution_add_fusion = f32[2048,1024]{1,0:T(8,128)S(1)} fusion(f32[2048,1024]{1,0:T(8,128)S(1)} %fusion.13, f32[64,1024]{1,0:T(8,128)S(1)} %fusion.33, s32[64]{0:T(128)S(1)} %get-tuple-element.69, pred[64]{0:T(512)(128)(4,1)S(1)} %compare_and_fusion), kind=kOutput, calls=%fused_computation.2 | convolution fusion | flops 1612972032 | bytes 17039680 | tf_op jit(solution)/shard_map/dot_general | solution.py:266
  100.6 5.9 %pad_maximum_fusion = f32[64,7,8,1024]{3,2,1,0:T(8,128)} fusion(f32[64,1,8,1024]{3,2,1,0:T(8,128)S(1)} %bitcast.139, f32[64,2,8,1024]{3,2,1,0:T(8,128)S(1)} %bitcast.138, f32[64,4,8,1024]{3,2,1,0:T(8,128)S(1)} %bitcast.134), kind=kLoop, calls=%fused_computation.1 | loop fusion | flops 7340032 | bytes 29360128 | tf_op jit(solution)/shard_map/concatenate | solution.py:289
  106.5 1.4 copy-done.4
  107.9 0.3 fusion.15
  108.1 5.4 %convolution_bitcast_fusion = f32[64,32,1024]{2,1,0:T(8,128)S(1)} fusion(bf16[1024,2,4,64,1]{0,3,2,4,1:T(8,128)(2,1)} %bitcast.145, bf16[64,32,1,4,64]{4,1,3,0,2:T(8,128)(2,1)} %copy-done.8, bf16[64,32,1,4,64]{4,1,3,0,2:T(8,128)(2,1)} %copy-done.7), kind=kOutput, calls=%fused_computation.11 | convolution fusion | flops 2148532224 | bytes 11534336 | tf_op jit(solution)/shard_map/dot_general | solution.py:248
  113.5 3.3 %copy-done.3 = f32[64,32,1024]{2,1,0:T(8,128)} copy-done((f32[64,32,1024]{2,1,0:T(8,128)}, f32[64,32,1024]{2,1,0:T(8,128)S(1)}, u32[]{:S(2)}) %copy-start.3) | copy-done | bytes 8388632
  116.8 0.3 slice_add_fusion
  117.1 6.1 %scatter-add.6 = f32[64,32,1024]{2,1,0:T(8,128)} dynamic-update-slice(f32[64,32,1024]{2,1,0:T(8,128)} %copy-done.3, f32[64,1,1024]{2,1,0:T(1,128)S(1)} %slice_add_fusion, s32[]{:T(128)} %constant.74.clone.1, s32[]{:T(128)} %constant.74.clone.1, s32[]{:T(128)} %constant.74.clone.1) | dynamic-update-slice | bytes 524292 | tf_op jit(solution)/shard_map/scatter-add | solution.py:256
  123.2 6.5 %convert_element_type.98.y_ref = bf16[64,32,1024]{2,1,0:T(8,128)(2,1)} convert(f32[64,32,1024]{2,1,0:T(8,128)} %scatter-add.6) | non-fusion elementwise | flops 2097152 | bytes 12582912 | tf_op jit(solution)/shard_map/convert_element_type | solution.py:256
  129.7 51.4 %shard_map.140 = f32[16,32,1024]{2,1,0:T(8,128)} custom-call(bf16[64,32,1024]{2,1,0:T(8,128)(2,1)} %convert_element_type.98.y_ref), custom_call_target="tpu_custom_call" | custom-call | tf_op jit(solution)/shard_map/pallas_call | solution.py:123
  181.1 1.1 reshape_add_fusion
  182.2 2.0 scatter-add.9
  184.2 2.7 convert_element_type.99
  186.9 85.5 %reduce-scatter.4.cloned.1.call-done = f32[7,8,1024]{2,1,0:T(8,128)} async-done(((f32[448,8,1024]{2,1,0:T(8,128)}), f32[7,8,1024]{2,1,0:T(8,128)}) %reduce-scatter.4.cloned.1.call-update) | async-done | bytes 229392
  272.5 0.7 slice_reduce_fusion
  273.2 0.8 slice_bitcast_fusion.7
  274.0 0.9 slice_bitcast_fusion.6
  274.9 0.6 slice_bitcast_fusion.8
  275.6 0.6 copy.75
  276.3 0.7 copy.76
  277.0 0.6 copy.107
  (65 shorter events, 2.0 us)
Async XLA Ops:
  7.2 19.2 %copy-start = (bf16[256,1024]{1,0:T(8,128)(2,1)S(1)}, bf16[256,1024]{1,0:T(8,128)(2,1)}, u32[]{:S(2)}) copy-start(bf16[256,1024]{1,0:T(8,128)(2,1)} %param.16) | copy-start | bytes 1572868
  7.2 6.0 %slice-start = ((bf16[1024,3,256]{2,0,1:T(8,128)(2,1)}), bf16[1024,2,256]{2,0,1:T(8,128)(2,1)S(1)}, s32[]{:S(2)}) async-start(bf16[1024,3,256]{2,0,1:T(8,128)(2,1)} %param.15), calls=%async_computation.2 | async-start | bytes 2097152 | tf_op jit(solution)/shard_map/slice | solution.py:159
  7.2 265.3 %reduce-scatter.4.cloned.1.call-start = ((), (), s32[]{:S(2)}) async-start(), calls=%async_computation.1 | async-start | bytes 14909440
  13.7 6.7 %copy-start.9 = (bf16[1024,2,256]{0,2,1:T(8,128)(2,1)}, bf16[1024,2,256]{0,2,1:T(8,128)(2,1)S(1)}, u32[]{:S(2)}) copy-start(bf16[1024,2,256]{0,2,1:T(8,128)(2,1)S(1)} %copy.67) | copy-start | bytes 3145732
  20.5 2.2 copy-start.15
  21.6 24.6 %copy-start.12 = (f32[1024]{0:T(1024)S(1)}, f32[1024]{0:T(1024)}, u32[]{:S(2)}) copy-start(f32[1024]{0:T(1024)} %param.17) | copy-start | bytes 12292
  21.6 24.6 %copy-start.14 = (f32[1024]{0:T(1024)S(1)}, f32[1024]{0:T(1024)}, u32[]{:S(2)}) copy-start(f32[1024]{0:T(1024)} %param.18) | copy-start | bytes 12292
  47.5 24.5 %copy-start.6 = (f32[128,1024]{1,0:T(8,128)S(1)}, f32[128,1024]{1,0:T(8,128)}, u32[]{:S(2)}) copy-start(f32[128,1024]{1,0:T(8,128)} %shard_map.137) | copy-start | bytes 1572868
  74.0 4.7 %copy-start.16 = (bf16[64,32,2,4,64]{4,1,3,2,0:T(8,128)(2,1)S(1)}, bf16[64,32,2,4,64]{4,1,3,2,0:T(8,128)(2,1)}, u32[]{:S(2)}) copy-start(bf16[64,32,2,4,64]{4,1,3,2,0:T(8,128)(2,1)} %copy-done.15) | copy-start | bytes 6291460
  79.6 3.3 %copy-start.10 = (bf16[64,256]{1,0:T(8,128)(2,1)}, bf16[64,256]{1,0:T(8,128)(2,1)S(1)}, u32[]{:S(2)}) copy-start(bf16[64,256]{1,0:T(8,128)(2,1)S(1)} %convert_element_type.97) | copy-start | bytes 98308
  82.7 2.8 copy-start.7
  82.7 2.9 %copy-start.13 = (bf16[64,32,1024]{2,1,0:T(8,128)(2,1)S(1)}, bf16[64,32,1024]{2,1,0:T(8,128)(2,1)}, u32[]{:S(2)}) copy-start(bf16[64,32,1024]{2,1,0:T(8,128)(2,1)} %param.14) | copy-start | bytes 12582916
  85.7 2.4 copy-start.8
  85.7 2.4 copy-start.5
  96.9 3.7 %copy-start.2 = (f32[1024,1024]{1,0:T(8,128)S(1)}, f32[1024,1024]{1,0:T(8,128)}, u32[]{:S(2)}) copy-start(f32[1024,1024]{1,0:T(8,128)} %copy.71) | copy-start | bytes 12582916
  106.4 1.4 copy-start.4
  106.4 1.4 copy-start.11
  113.5 3.3 %copy-start.3 = (f32[64,32,1024]{2,1,0:T(8,128)}, f32[64,32,1024]{2,1,0:T(8,128)S(1)}, u32[]{:S(2)}) copy-start(f32[64,32,1024]{2,1,0:T(8,128)S(1)} %convolution_bitcast_fusion) | copy-start | bytes 25165828
  123.2 154.4 %copy-start.1 = (bf16[256,1024]{1,0:T(8,128)(2,1)S(1)}, bf16[256,1024]{1,0:T(8,128)(2,1)}, u32[]{:S(2)}) copy-start(bf16[256,1024]{1,0:T(8,128)(2,1)} %param.16) | copy-start | bytes 1572868
Sparse Core Ops, SparseCore 0:
  106.6 165.8 reduce-scatter.3

commit v11 on v10

--- a/solution.py
+++ b/solution.py
@@ -184,7 +184,9 @@
     owned = (local_block >= 0) & (local_block < own_blocks)
     safe_block = jnp.clip(local_block, 0, own_blocks - 1)
     flat_table = table.reshape(own_blocks * block_rows, width)
-    picked = flat_table[safe_block * block_rows + gold_row]
+    picked_row = safe_block * block_rows + gold_row
+    pick = (picked_row[:, None] == jnp.arange(own_blocks * block_rows)[None, :]).astype(table.dtype)
+    picked = jnp.dot(pick, flat_table, preferred_element_type=jnp.float32)
     picked = jnp.where(owned[:, None], picked.astype(jnp.float32), 0.0)
     both = peer_sum(
         jnp.concatenate([attn_part.astype(jnp.bfloat16), picked.astype(jnp.bfloat16)], axis=0), 0

time: 288 us -> 288 us (level)
  local copies, waits for them, and re-layouts: 32.6 us -> 29.1 us
  matrix products: 38.4 us -> 41.5 us
    gather x1 -> x0, local copies, waits for them, and re-layouts: 3.52 us -> none  [on_device(): picked = flat_table[safe_block * block_rows + gold_row]]
    dot_general x0 -> x1, matrix products: none -> 3.08 us  [on_device(): picked = jnp.dot(pick, flat_table, preferred_element_type=jnp.float32)]
where the time goes in v11:
time: 288 us; the launch traced here: 284 us
  waiting for transfers between devices  85.6 us (30%)
  Pallas kernels  84.5 us (29%)
  matrix products  41.5 us (14%)
  local copies, waits for them, and re-layouts  29.1 us (10%)
  other arithmetic  28.8 us (10%)
  between operations  14.6 us (5%)
    unnamed x2, waiting for transfers between devices  85.6 us
    pallas_call x1, Pallas kernels, peer_scatter(): pl.pallas_call(functools.partial(_peer_scatter_kernel, n), out_shape=jax....  51.4 us
    pallas_call x3, Pallas kernels, peer_sum(): pl.pallas_call(functools.partial(_peer_sum_kernel, n), out_shape=jax.Shap...  33.1 us
    dot_general x8, matrix products, contract(): lax.dot_general(left, right, (((left_dim,), (right_dim,)), ((), ())), pre...  8.47 us
    unnamed x40, local copies, waits for them, and re-layouts  7.56 us
    dot_general x1, matrix products, on_device(): lax.dot_general(hidden_in, w_keyval.reshape(width, 2, local_heads, HD), (...  6.72 us
    convert_element_type x1, other arithmetic, on_device(): token_term.at[:, 0, :].add(contract(query_gradient, w_query, 1, 1))  6.53 us
    scatter-add x1, local copies, waits for them, and re-layouts, on_device(): token_term.at[:, 0, :].add(contract(query_gradient, w_query, 1, 1))  6.07 us
  transfers between devices with their start and end apart: 1, of which 1 were waited for; matrix products, arithmetic and copies ran while one was open for 9% of the time, Pallas kernels for 18%

profile of v11, /device:TPU:1, one launch (start us, length us, event | category | flops | bytes accessed | tf_op | source)
XLA Modules:
  0.0 284.0 jit_solution(3039454418737614019)
XLA Ops:
  7.2 1.5 slice.85
  8.8 1.2 convolution_convert_fusion.3
  10.2 0.7 compare_and_fusion
  10.9 0.7 compare_reduce_fusion
  11.7 0.7 multiply_add_fusion
  12.4 0.7 fusion.33
  13.2 0.5 copy.67
  13.7 6.7 %fusion.4 = bf16[64,32,2,4,64]{4,1,3,2,0:T(8,128)(2,1)S(1)} fusion(bf16[1024,2,4,64,1]{0,3,2,1,4:T(8,128)(2,1)S(1)} %bitcast.145, bf16[64,32,1024]{2,1,0:T(8,128)(2,1)} %param.14), kind=kOutput, calls=%fused_computation.11 | convolution fusion | flops 2148532224 | bytes 7340032 | tf_op jit(solution)/shard_map/dot_general | solution.py:161
  20.5 1.2 fusion.10
  21.6 0.2 fusion.28
  22.0 0.7 fusion.12
  22.8 0.2 convolution_convert_fusion.1
  23.0 3.1 %fusion.13 = bf16[64,1024]{1,0:T(8,128)(2,1)S(1)} fusion(bf16[2048,1024]{1,0:T(8,128)(2,1)} %bitcast.135, s32[64]{0:T(128)S(1)} %get-tuple-element.70, pred[64]{0:T(512)(128)(4,1)S(1)} %compare_and_fusion), kind=kOutput, calls=%fused_computation.23 | convolution fusion | flops 268697600 | bytes 4325696 | tf_op jit(solution)/shard_map/dot_general | solution.py:189
  26.1 0.7 pad_maximum_fusion.5.x_ref
  26.8 17.5 %shard_map.137 = f32[128,1024]{1,0:T(8,128)} custom-call(bf16[128,1024]{1,0:T(8,128)(2,1)} %pad_maximum_fusion.5.x_ref), custom_call_target="tpu_custom_call" | custom-call | tf_op jit(solution)/shard_map/pallas_call | solution.py:62
  44.3 1.1 fusion.38
  45.5 0.2 multiply_reduce_fusion.3
  45.8 1.1 exponential_reduce_fusion
  47.0 3.8 %multiply_reduce_fusion = (f32[64]{0:T(128)S(1)}, f32[64,2048]{1,0:T(8,128)S(1)}) fusion(f32[2048]{0:T(1024)S(1)} %bitcast.155, bf16[64,1024]{1,0:T(8,128)(2,1)S(1)} %add_convert_fusion, bf16[2048,1024]{1,0:T(8,128)(2,1)} %bitcast.136), kind=kOutput, calls=%fused_computation.35 | convolution fusion | flops 268697536 | bytes 4858112 | tf_op jit(solution)/shard_map/dot_general | solution.py:142
  50.7 0.6 pad.12.x_ref
  51.3 6.7 %shard_map.138 = f32[8,64]{1,0:T(8,128)} custom-call(f32[8,64]{1,0:T(8,128)} %pad.12.x_ref), custom_call_target="tpu_custom_call" | custom-call | tf_op jit(solution)/shard_map/pallas_call | solution.py:62
  58.0 0.7 fusion.34
  58.7 0.2 multiply_convert_fusion.2
  58.9 3.7 %convolution_convert_fusion.x_ref = bf16[64,1024]{1,0:T(8,128)(2,1)} fusion(bf16[64,2048]{1,0:T(8,128)(2,1)S(1)} %multiply_convert_fusion.2, bf16[2048,1024]{1,0:T(8,128)(2,1)} %bitcast.137), kind=kOutput, calls=%fused_computation.24 | convolution fusion | flops 268500992 | bytes 4587520 | tf_op jit(solution)/shard_map/dot_general | solution.py:212
  62.6 8.9 %shard_map.139 = f32[64,1024]{1,0:T(8,128)} custom-call(bf16[64,1024]{1,0:T(8,128)(2,1)} %convolution_convert_fusion.x_ref), custom_call_target="tpu_custom_call" | custom-call | tf_op jit(solution)/shard_map/pallas_call | solution.py:62
  71.5 1.3 multiply_reduce_fusion.1
  73.0 0.3 convolution_convert_fusion.2
  73.5 0.2 fusion.35
  73.7 1.3 fusion.29
  75.0 2.9 %fusion.11 = f32[64,4,1,32]{3,2,1,0:T(1,128)S(1)} fusion(bf16[64,4,64,1]{2,3,1,0:T(2,128)(2,1)S(1)} %reshape.209, bf16[64,32,2,4,64]{4,1,3,2,0:T(8,128)(2,1)} %copy-done.15), kind=kOutput, calls=%fused_computation.18 | convolution fusion | flops 1048576 | bytes 2162688 | tf_op jit(solution)/shard_map/ybn,yqbn->ybq/dot_general | solution.py:226
  77.9 0.2 multiply_reduce_fusion.5
  78.2 0.7 fusion.9
  79.1 0.4 copy.68
  79.5 0.2 copy.72
  79.8 0.3 reshape.189
  80.0 0.3 convolution_bitcast_fusion.1
  80.3 1.8 fusion.7
  82.4 1.2 copy.97
  83.6 1.4 fusion.8
  85.1 2.4 fusion
  87.5 2.2 pad_maximum_fusion.2
  89.8 5.3 %copy.71 = f32[1024,1024]{1,0:T(8,128)} copy(f32[1024,1024]{0,1:T(8,128)} %pad_maximum_fusion.2) | data formatting | bytes 8388608 | tf_op jit(solution)/shard_map/concatenate | solution.py:281
  95.1 1.2 fusion.14
  96.4 3.6 %convolution_add_fusion = f32[2048,1024]{1,0:T(8,128)S(1)} fusion(f32[2048,1024]{1,0:T(8,128)S(1)} %fusion.14, f32[64,1024]{1,0:T(8,128)S(1)} %fusion.35, s32[64]{0:T(128)S(1)} %get-tuple-element.69, pred[64]{0:T(512)(128)(4,1)S(1)} %compare_and_fusion), kind=kOutput, calls=%fused_computation.1 | convolution fusion | flops 1612972032 | bytes 17039680 | tf_op jit(solution)/shard_map/dot_general | solution.py:268
  100.0 5.9 %pad_maximum_fusion = f32[64,7,8,1024]{3,2,1,0:T(8,128)} fusion(f32[64,1,8,1024]{3,2,1,0:T(8,128)S(1)} %bitcast.140, f32[64,2,8,1024]{3,2,1,0:T(8,128)S(1)} %bitcast.139, f32[64,4,8,1024]{3,2,1,0:T(8,128)S(1)} %bitcast.138), kind=kLoop, calls=%fused_computation | loop fusion | flops 7340032 | bytes 29360128 | tf_op jit(solution)/shard_map/concatenate | solution.py:291
  105.9 1.4 copy-done.4
  107.3 0.3 fusion.16
  107.6 5.4 %convolution_bitcast_fusion = f32[64,32,1024]{2,1,0:T(8,128)S(1)} fusion(bf16[1024,2,4,64,1]{0,3,2,4,1:T(8,128)(2,1)} %bitcast.146, bf16[64,32,1,4,64]{4,1,3,0,2:T(8,128)(2,1)} %copy-done.8, bf16[64,32,1,4,64]{4,1,3,0,2:T(8,128)(2,1)} %copy-done.7), kind=kOutput, calls=%fused_computation.10 | convolution fusion | flops 2148532224 | bytes 11534336 | tf_op jit(solution)/shard_map/dot_general | solution.py:250
  113.0 3.3 %copy-done.3 = f32[64,32,1024]{2,1,0:T(8,128)} copy-done((f32[64,32,1024]{2,1,0:T(8,128)}, f32[64,32,1024]{2,1,0:T(8,128)S(1)}, u32[]{:S(2)}) %copy-start.3) | copy-done | bytes 8388632
  116.3 0.3 slice_add_fusion
  116.6 6.1 %scatter-add.6 = f32[64,32,1024]{2,1,0:T(8,128)} dynamic-update-slice(f32[64,32,1024]{2,1,0:T(8,128)} %copy-done.3, f32[64,1,1024]{2,1,0:T(1,128)S(1)} %slice_add_fusion, s32[]{:T(128)} %constant.73.clone.1, s32[]{:T(128)} %constant.73.clone.1, s32[]{:T(128)} %constant.73.clone.1) | dynamic-update-slice | bytes 524292 | tf_op jit(solution)/shard_map/scatter-add | solution.py:258
  122.7 6.5 %convert_element_type.95.y_ref = bf16[64,32,1024]{2,1,0:T(8,128)(2,1)} convert(f32[64,32,1024]{2,1,0:T(8,128)} %scatter-add.6) | non-fusion elementwise | flops 2097152 | bytes 12582912 | tf_op jit(solution)/shard_map/convert_element_type | solution.py:258
  129.2 51.4 %shard_map.140 = f32[16,32,1024]{2,1,0:T(8,128)} custom-call(bf16[64,32,1024]{2,1,0:T(8,128)(2,1)} %convert_element_type.95.y_ref), custom_call_target="tpu_custom_call" | custom-call | tf_op jit(solution)/shard_map/pallas_call | solution.py:123
  180.6 1.1 reshape_add_fusion
  181.7 2.0 scatter-add.9
  183.7 2.7 convert_element_type.96
  186.4 85.6 %reduce-scatter.4.cloned.1.call-done = f32[7,8,1024]{2,1,0:T(8,128)} async-done(((f32[448,8,1024]{2,1,0:T(8,128)}), f32[7,8,1024]{2,1,0:T(8,128)}) %reduce-scatter.4.cloned.1.call-update) | async-done | bytes 229392
  272.0 0.7 slice_reduce_fusion
  272.7 0.8 slice_bitcast_fusion.7
  273.6 0.9 slice_bitcast_fusion.6
  274.5 0.6 slice_bitcast_fusion.8
  275.2 0.6 copy.75
  275.8 0.7 copy.76
  276.6 0.6 copy.107
  (63 shorter events, 1.9 us)
Async XLA Ops:
  7.2 15.6 %copy-start = (bf16[256,1024]{1,0:T(8,128)(2,1)S(1)}, bf16[256,1024]{1,0:T(8,128)(2,1)}, u32[]{:S(2)}) copy-start(bf16[256,1024]{1,0:T(8,128)(2,1)} %param.16) | copy-start | bytes 1572868
  7.2 6.0 %slice-start = ((bf16[1024,3,256]{2,0,1:T(8,128)(2,1)}), bf16[1024,2,256]{2,0,1:T(8,128)(2,1)S(1)}, s32[]{:S(2)}) async-start(bf16[1024,3,256]{2,0,1:T(8,128)(2,1)} %param.15), calls=%async_computation.2 | async-start | bytes 2097152 | tf_op jit(solution)/shard_map/slice | solution.py:159
  7.2 264.8 %reduce-scatter.4.cloned.1.call-start = ((), (), s32[]{:S(2)}) async-start(), calls=%async_computation.1 | async-start | bytes 14909440
  13.7 6.7 %copy-start.9 = (bf16[1024,2,256]{0,2,1:T(8,128)(2,1)}, bf16[1024,2,256]{0,2,1:T(8,128)(2,1)S(1)}, u32[]{:S(2)}) copy-start(bf16[1024,2,256]{0,2,1:T(8,128)(2,1)S(1)} %copy.67) | copy-start | bytes 3145732
  20.4 2.2 copy-start.15
  22.6 23.1 %copy-start.12 = (f32[1024]{0:T(1024)S(1)}, f32[1024]{0:T(1024)}, u32[]{:S(2)}) copy-start(f32[1024]{0:T(1024)} %param.17) | copy-start | bytes 12292
  22.6 23.1 %copy-start.14 = (f32[1024]{0:T(1024)S(1)}, f32[1024]{0:T(1024)}, u32[]{:S(2)}) copy-start(f32[1024]{0:T(1024)} %param.18) | copy-start | bytes 12292
  47.0 24.5 %copy-start.6 = (f32[128,1024]{1,0:T(8,128)S(1)}, f32[128,1024]{1,0:T(8,128)}, u32[]{:S(2)}) copy-start(f32[128,1024]{1,0:T(8,128)} %shard_map.137) | copy-start | bytes 1572868
  73.5 4.7 %copy-start.16 = (bf16[64,32,2,4,64]{4,1,3,2,0:T(8,128)(2,1)S(1)}, bf16[64,32,2,4,64]{4,1,3,2,0:T(8,128)(2,1)}, u32[]{:S(2)}) copy-start(bf16[64,32,2,4,64]{4,1,3,2,0:T(8,128)(2,1)} %copy-done.15) | copy-start | bytes 6291460
  79.0 3.3 %copy-start.10 = (bf16[64,256]{1,0:T(8,128)(2,1)}, bf16[64,256]{1,0:T(8,128)(2,1)S(1)}, u32[]{:S(2)}) copy-start(bf16[64,256]{1,0:T(8,128)(2,1)S(1)} %convert_element_type.94) | copy-start | bytes 98308
  82.2 2.8 copy-start.7
  82.2 2.9 %copy-start.13 = (bf16[64,32,1024]{2,1,0:T(8,128)(2,1)S(1)}, bf16[64,32,1024]{2,1,0:T(8,128)(2,1)}, u32[]{:S(2)}) copy-start(bf16[64,32,1024]{2,1,0:T(8,128)(2,1)} %param.14) | copy-start | bytes 12582916
  85.1 2.4 copy-start.8
  85.1 2.4 copy-start.5
  96.3 3.7 %copy-start.2 = (f32[1024,1024]{1,0:T(8,128)S(1)}, f32[1024,1024]{1,0:T(8,128)}, u32[]{:S(2)}) copy-start(f32[1024,1024]{1,0:T(8,128)} %copy.71) | copy-start | bytes 12582916
  105.9 1.4 copy-start.4
  105.9 1.4 copy-start.11
  113.0 3.3 %copy-start.3 = (f32[64,32,1024]{2,1,0:T(8,128)}, f32[64,32,1024]{2,1,0:T(8,128)S(1)}, u32[]{:S(2)}) copy-start(f32[64,32,1024]{2,1,0:T(8,128)S(1)} %convolution_bitcast_fusion) | copy-start | bytes 25165828
  122.6 154.5 %copy-start.1 = (bf16[256,1024]{1,0:T(8,128)(2,1)S(1)}, bf16[256,1024]{1,0:T(8,128)(2,1)}, u32[]{:S(2)}) copy-start(bf16[256,1024]{1,0:T(8,128)(2,1)} %param.16) | copy-start | bytes 1572868
Sparse Core Ops, SparseCore 0:
  106.0 165.9 reduce-scatter.3
